TPU v7x, 32 devices: a whole 2x2x4 slice. The times are simulated.
32 devices in a mesh: group: 4 (over y, x), expert: 8 (over z, core).
Axes of the slice: x: 2, y: 2, z: 4, core: 2. Of those that a mesh axis runs over, the one named last changes fastest.
Arguments:
- tokens: bfloat16 [12288, 2048], P(('group', 'expert')), may hold values from -6 to 6
- query_weight: bfloat16 [2048, 2048], P(('group', 'expert')), may hold values from -0.125 to 0.125
- key_weight: bfloat16 [2048, 2048], P(('group', 'expert')), may hold values from -0.125 to 0.125
- value_weight: bfloat16 [2048, 2048], P(('group', 'expert')), may hold values from -0.125 to 0.125
- output_weight: bfloat16 [2048, 2048], P(('group', 'expert')), may hold values from -2 to 2
- router_weight: bfloat16 [2048, 8], P(('group', 'expert')), may hold values from -0.0625 to 0.0625
- attnorm: bfloat16 [2048], P(('group', 'expert')), may hold values from 0.5 to 1.5
- querynorm: bfloat16 [2048], P(('group', 'expert')), may hold values from 0.5 to 1.5
- keynorm: bfloat16 [2048], P(('group', 'expert')), may hold values from 0.5 to 1.5
- mixnorm: bfloat16 [2048], P(('group', 'expert')), may hold values from 0.5 to 1.5
- gate_weight: bfloat16 [8, 2048, 1024], P('expert'), may hold values from -0.125 to 0.125
- up_weight: bfloat16 [8, 2048, 1024], P('expert'), may hold values from -0.125 to 0.125
- down_weight: bfloat16 [8, 1024, 2048], P('expert'), may hold values from -1 to 1
- routes: int32 [12288, 2], P(('group', 'expert')), may hold values from 0 to 7, all different within a row; in each aligned block of 384 rows (0 to 383, 384 to 767, ...) at most 192 rows name the same one
- lengths: int32 [4, 4], P('group'), may hold values from 1 to 2048, 3072 in all within a row
- seq_order: int32 [4, 4], P('group'), may hold values from 0 to 3, each once within a row
- cotangent: bfloat16 [12288, 2048], P(('group', 'expert')), may hold values from -6 to 6
Outputs:
- layer_result: bfloat16 [12288, 2048], P(('group', 'expert'))
- tokens_grad: bfloat16 [12288, 2048], P(('group', 'expert'))
- query_grad: float32 [2048, 2048], P(('group', 'expert'))
- key_grad: float32 [2048, 2048], P(('group', 'expert'))
- value_grad: float32 [2048, 2048], P(('group', 'expert'))
- output_grad: float32 [2048, 2048], P(('group', 'expert'))
- router_grad: float32 [2048, 8], P(('group', 'expert'))
- attnorm_grad: float32 [2048], P(('group', 'expert'))
- querynorm_grad: float32 [2048], P(('group', 'expert'))
- keynorm_grad: float32 [2048], P(('group', 'expert'))
- mixnorm_grad: float32 [2048], P(('group', 'expert'))
- gate_grad: float32 [8, 2048, 1024], P('expert')
- up_grad: float32 [8, 2048, 1024], P('expert')
- down_grad: float32 [8, 1024, 2048], P('expert')
Inputs may be any that keep to these rules, and one draw needn't show every extreme that they name: `routes`: the 2 entries of a row name different experts, every expert is named somewhere; at most 192 of the rows of one device name one expert, and in every draw some device's rows name some expert exactly 192 times. Each group's 4 lengths sum to 3072, and the largest of each group is exactly 2048. `seq_order`: each group's row holds every number 0 to 3 once.
All inputs are finite; a program needn't handle non-finite values.
Results may differ from a plain program's by a relative error of at most 0.025.
Values may be sent and summed in bfloat16 or wider, within the bound.
A program may use at most 384 MiB of HBM per device.

v0:
```python
import jax
import jax.numpy as jnp
from jax import lax
from jax.sharding import PartitionSpec as P

HEADS = 16
HEAD_DIM = 128
TOP = 2


masked_score = -1e30


def rms_scale(values, gain):
    return values * lax.rsqrt(jnp.mean(values * values, axis=-1, keepdims=True) + 1e-05) * gain


def angle_tables(position, head_size):
    half_size = head_size // 2
    frequency = 10000.0 ** (-(jnp.arange(half_size, dtype=jnp.float32) * 2.0 / head_size))
    angles = position.astype(jnp.float32)[:, None] * frequency[None, :]
    angles = jnp.concatenate([angles, angles], axis=1)
    return (jnp.cos(angles)[:, None, :], jnp.sin(angles)[:, None, :])


def rotate(values, cosine, sine_part):
    half_size = values.shape[-1] // 2
    turned = jnp.concatenate([-values[..., half_size:], values[..., :half_size]], axis=-1)
    return values * cosine + turned * sine_part


def placement_of(token_index, length_row, order_row):
    seq_count = order_row.shape[0]
    chosen = (order_row[:, None] == jnp.arange(seq_count, dtype=jnp.int32)[None, :]).astype(
        jnp.int32
    )
    placed = jnp.sum(chosen * length_row[None, :], axis=1)
    seq_ends = jnp.cumsum(placed)
    passed = (token_index[:, None] >= seq_ends[None, :]).astype(jnp.int32)
    segment = jnp.sum(passed, axis=1)
    seq_begin = jnp.sum(passed * placed[None, :], axis=1)
    return (segment, token_index - seq_begin)


def allowed_pairs(query_index, key_index, length_row, order_row):
    query_seg = placement_of(query_index, length_row, order_row)[0]
    key_seg = placement_of(key_index, length_row, order_row)[0]
    return (query_index[:, None] >= key_index[None, :]) & (query_seg[:, None] == key_seg[None, :])


def block_size():
    return 512


def score_grads(
    query_block, dout_block, lse_block, delta_block, key_block, value_block, allowed, scale_factor
):
    scores = (
        jnp.einsum("qhd,khd->hqk", query_block, key_block, preferred_element_type=jnp.float32)
        * scale_factor
    )
    weights = jnp.where(allowed[None], jnp.exp(scores - lse_block[:, :, None]), 0.0)
    dprob = jnp.einsum("qhd,khd->hqk", dout_block, value_block, preferred_element_type=jnp.float32)
    dscore = (weights * (dprob - delta_block[:, :, None])).astype(jnp.bfloat16)
    return (weights.astype(jnp.bfloat16), dscore)


def body(
    tokens,
    query_weight,
    key_weight,
    value_weight,
    output_weight,
    router_weight,
    attnorm,
    querynorm,
    keynorm,
    mixnorm,
    gate_weight,
    up_weight,
    down_weight,
    routes,
    lengths,
    seq_order,
    cotangent,
):
    row_count = tokens.shape[0]
    width = tokens.shape[1]
    ranks = lax.axis_size("expert")
    my_rank = lax.axis_index("expert")
    capacity = 2 * row_count * TOP // ranks
    group_rows = row_count * ranks
    scale_factor = HEAD_DIM ** (-0.5)
    length_row = lengths[0]
    order_row = seq_order[0]
    my_index = my_rank * row_count + jnp.arange(row_count, dtype=jnp.int32)
    position = placement_of(my_index, length_row, order_row)[1]
    cosine, sine_part = angle_tables(position, HEAD_DIM)
    gathered = (
        lax.all_gather(query_weight, ("group", "expert"), axis=0, tiled=True),
        lax.all_gather(key_weight, ("group", "expert"), axis=0, tiled=True),
        lax.all_gather(value_weight, ("group", "expert"), axis=0, tiled=True),
        lax.all_gather(output_weight, ("group", "expert"), axis=0, tiled=True),
        lax.all_gather(router_weight, ("group", "expert"), axis=0, tiled=True),
        lax.all_gather(attnorm, ("group", "expert"), axis=0, tiled=True),
        lax.all_gather(querynorm, ("group", "expert"), axis=0, tiled=True),
        lax.all_gather(keynorm, ("group", "expert"), axis=0, tiled=True),
        lax.all_gather(mixnorm, ("group", "expert"), axis=0, tiled=True),
    )
    full_query, full_key, full_value, full_output, full_router = (
        gathered[0],
        gathered[1],
        gathered[2],
        gathered[3],
        gathered[4],
    )
    attn_gain = gathered[5].astype(jnp.float32)
    query_gain = gathered[6].astype(jnp.float32)
    key_gain = gathered[7].astype(jnp.float32)
    mix_gain = gathered[8].astype(jnp.float32)
    tokens_in = tokens.astype(jnp.float32)
    normed_r = rms_scale(tokens_in, attn_gain).astype(jnp.bfloat16)
    query_pre = jnp.dot(normed_r, full_query, preferred_element_type=jnp.float32)
    key_pre = jnp.dot(normed_r, full_key, preferred_element_type=jnp.float32)
    value_pre = jnp.dot(normed_r, full_value, preferred_element_type=jnp.float32)
    queries_r = rotate(
        rms_scale(query_pre, query_gain).reshape(row_count, HEADS, HEAD_DIM), cosine, sine_part
    ).astype(jnp.bfloat16)
    keys_r = rotate(
        rms_scale(key_pre, key_gain).reshape(row_count, HEADS, HEAD_DIM), cosine, sine_part
    ).astype(jnp.bfloat16)
    values_r = value_pre.astype(jnp.bfloat16).reshape(row_count, HEADS, HEAD_DIM)
    start_state = (
        jnp.full((HEADS, row_count), masked_score, jnp.float32),
        jnp.zeros((HEADS, row_count), jnp.float32),
        jnp.zeros((HEADS, row_count, HEAD_DIM), jnp.float32),
    )
    key_piece = lax.all_gather(keys_r, "expert", axis=0, tiled=True)
    value_piece = lax.all_gather(values_r, "expert", axis=0, tiled=True)
    piece_rows = key_piece.shape[0]
    block_len = block_size()

    def attend_one_block(running, offset):
        row_max, denominator, weighted = running
        key_block = lax.dynamic_slice_in_dim(key_piece, offset, block_len, 0)
        value_block = lax.dynamic_slice_in_dim(value_piece, offset, block_len, 0)
        key_index = offset + jnp.arange(block_len, dtype=jnp.int32)
        allowed = allowed_pairs(my_index, key_index, length_row, order_row)[None]
        scores = (
            jnp.einsum("qhd,khd->hqk", queries_r, key_block, preferred_element_type=jnp.float32)
            * scale_factor
        )
        new_max = jnp.maximum(row_max, jnp.max(jnp.where(allowed, scores, masked_score), axis=2))
        weights = jnp.where(allowed, jnp.exp(scores - new_max[:, :, None]), 0.0)
        factor = jnp.exp(row_max - new_max)
        denominator = denominator * factor + jnp.sum(weights, axis=2)
        weighted = weighted * factor[:, :, None] + jnp.einsum(
            "hqk,khd->hqd",
            weights.astype(jnp.bfloat16),
            value_block,
            preferred_element_type=jnp.float32,
        )
        return ((new_max, denominator, weighted), None)

    offsets = jnp.arange(piece_rows // block_len, dtype=jnp.int32) * block_len
    row_max, denominator, weighted = lax.scan(attend_one_block, start_state, offsets)[0]
    attended = jnp.transpose(weighted / denominator[:, :, None], (1, 0, 2))
    log_total = row_max + jnp.log(denominator)
    attended_r = attended.reshape(row_count, width).astype(jnp.bfloat16)
    middle = tokens_in + jnp.dot(attended_r, full_output, preferred_element_type=jnp.float32)
    mixed_r = rms_scale(middle, mix_gain).astype(jnp.bfloat16)
    logits = jnp.dot(mixed_r, full_router, preferred_element_type=jnp.float32)
    shifted = jnp.exp(logits - jnp.max(logits, axis=1, keepdims=True))
    share = shifted / jnp.sum(shifted, axis=1, keepdims=True)
    pair_count = row_count * TOP
    expert_of = routes.reshape(pair_count)
    onehot = (expert_of[:, None] == jnp.arange(ranks, dtype=jnp.int32)[None, :]).astype(jnp.int32)
    before = jnp.cumsum(onehot, axis=0) - onehot
    slot_of = expert_of * capacity + jnp.sum(before * onehot, axis=1)
    table = (
        jnp.full((ranks * capacity,), -1, jnp.int32)
        .at[slot_of]
        .set(jnp.arange(pair_count, dtype=jnp.int32))
    )
    filled = table >= 0
    source = jnp.maximum(table, 0)
    zero_bf = jnp.zeros((), jnp.bfloat16)
    send_rows = jnp.where(filled[:, None], mixed_r[source // TOP], zero_bf)
    received = lax.all_to_all(
        send_rows.reshape(ranks, capacity, width), "expert", split_axis=0, concat_axis=0, tiled=True
    )
    inputs = received.reshape(ranks * capacity, width)
    gate_pre = jnp.dot(inputs, gate_weight[0], preferred_element_type=jnp.float32)
    up_pre = jnp.dot(inputs, up_weight[0], preferred_element_type=jnp.float32)
    sigma = jax.nn.sigmoid(gate_pre)
    hidden_r = (gate_pre * sigma * up_pre).astype(jnp.bfloat16)
    expert_out = jnp.dot(hidden_r, down_weight[0], preferred_element_type=jnp.float32).astype(
        jnp.bfloat16
    )
    returned = lax.all_to_all(
        expert_out.reshape(ranks, capacity, width),
        "expert",
        split_axis=0,
        concat_axis=0,
        tiled=True,
    )
    pair_out = returned.reshape(ranks * capacity, width)[slot_of].reshape(row_count, TOP, width)
    pair_hot = onehot.reshape(row_count, TOP, ranks).astype(jnp.float32)
    gates = jnp.sum(share[:, None, :] * pair_hot, axis=2)
    mixture = jnp.sum(gates[:, :, None] * pair_out, axis=1)
    layer_result = (middle + mixture).astype(jnp.bfloat16)
    incoming = cotangent.astype(jnp.float32)
    dcopy = (
        (gates[:, :, None] * incoming[:, None, :]).astype(jnp.bfloat16).reshape(pair_count, width)
    )
    send_grads = jnp.where(filled[:, None], dcopy[source], zero_bf)
    grad_inputs = lax.all_to_all(
        send_grads.reshape(ranks, capacity, width),
        "expert",
        split_axis=0,
        concat_axis=0,
        tiled=True,
    ).reshape(ranks * capacity, width)
    dhidden = jnp.einsum(
        "rd,fd->rf", grad_inputs, down_weight[0], preferred_element_type=jnp.float32
    )
    dgate_r = (dhidden * up_pre * sigma * (1.0 + gate_pre * (1.0 - sigma))).astype(jnp.bfloat16)
    dup_r = (dhidden * gate_pre * sigma).astype(jnp.bfloat16)
    down_term = jnp.einsum("rf,rd->fd", hidden_r, grad_inputs, preferred_element_type=jnp.float32)
    gate_term = jnp.einsum("rd,rf->df", inputs, dgate_r, preferred_element_type=jnp.float32)
    up_term = jnp.einsum("rd,rf->df", inputs, dup_r, preferred_element_type=jnp.float32)
    dinputs = (
        jnp.einsum("rf,df->rd", dgate_r, gate_weight[0], preferred_element_type=jnp.float32)
        + jnp.einsum("rf,df->rd", dup_r, up_weight[0], preferred_element_type=jnp.float32)
    ).astype(jnp.bfloat16)
    dreturned = lax.all_to_all(
        dinputs.reshape(ranks, capacity, width), "expert", split_axis=0, concat_axis=0, tiled=True
    )
    dpairs = dreturned.reshape(ranks * capacity, width)[slot_of].reshape(row_count, TOP, width)
    dmixed = jnp.sum(dpairs.astype(jnp.float32), axis=1)
    dgates = jnp.sum(pair_out * incoming[:, None, :], axis=2)
    dshare = jnp.sum(dgates[:, :, None] * pair_hot, axis=1)
    dlogits_r = (share * (dshare - jnp.sum(share * dshare, axis=1, keepdims=True))).astype(
        jnp.bfloat16
    )
    router_term = jnp.einsum("rd,re->de", mixed_r, dlogits_r, preferred_element_type=jnp.float32)
    dmixed = dmixed + jnp.einsum(
        "re,de->rd", dlogits_r, full_router, preferred_element_type=jnp.float32
    )
    middle_part, mixnorm_term = jax.vjp(rms_scale, middle, mix_gain)[1](dmixed)
    dmiddle = incoming + middle_part
    dprojected_r = dmiddle.astype(jnp.bfloat16)
    output_term = jnp.einsum(
        "rd,re->de", attended_r, dprojected_r, preferred_element_type=jnp.float32
    )
    dattended_r = (
        jnp.einsum("re,de->rd", dprojected_r, full_output, preferred_element_type=jnp.float32)
        .astype(jnp.bfloat16)
        .reshape(row_count, HEADS, HEAD_DIM)
    )
    delta_rows = jnp.sum(dattended_r.astype(jnp.float32) * attended, axis=2)
    delta_heads = delta_rows.T
    back_start = (
        jnp.zeros((row_count, HEADS, HEAD_DIM), jnp.float32),
        jnp.zeros((group_rows, HEADS, HEAD_DIM), jnp.float32),
        jnp.zeros((group_rows, HEADS, HEAD_DIM), jnp.float32),
    )
    back_key_piece = lax.all_gather(keys_r, "expert", axis=0, tiled=True)
    back_value_piece = lax.all_gather(values_r, "expert", axis=0, tiled=True)
    piece_rows = back_key_piece.shape[0]
    back_block_len = block_size()

    def back_one_block(running, offset):
        dquery_acc, dkey_all, dvalue_all = running
        key_block = lax.dynamic_slice_in_dim(back_key_piece, offset, back_block_len, 0)
        value_block = lax.dynamic_slice_in_dim(back_value_piece, offset, back_block_len, 0)
        key_index = offset + jnp.arange(back_block_len, dtype=jnp.int32)
        allowed = allowed_pairs(my_index, key_index, length_row, order_row)
        probs_r, dscore = score_grads(
            queries_r,
            dattended_r,
            log_total,
            delta_heads,
            key_block,
            value_block,
            allowed,
            scale_factor,
        )
        dquery_acc = (
            dquery_acc
            + jnp.einsum("hqk,khd->qhd", dscore, key_block, preferred_element_type=jnp.float32)
            * scale_factor
        )
        dkey_block = (
            jnp.einsum("hqk,qhd->khd", dscore, queries_r, preferred_element_type=jnp.float32)
            * scale_factor
        )
        dvalue_block = jnp.einsum(
            "hqk,qhd->khd", probs_r, dattended_r, preferred_element_type=jnp.float32
        )
        dkey_all = lax.dynamic_update_slice_in_dim(
            dkey_all,
            lax.dynamic_slice_in_dim(dkey_all, offset, back_block_len, 0) + dkey_block,
            offset,
            0,
        )
        dvalue_all = lax.dynamic_update_slice_in_dim(
            dvalue_all,
            lax.dynamic_slice_in_dim(dvalue_all, offset, back_block_len, 0) + dvalue_block,
            offset,
            0,
        )
        return ((dquery_acc, dkey_all, dvalue_all), None)

    offsets = jnp.arange(piece_rows // back_block_len, dtype=jnp.int32) * back_block_len
    dquery, dkey_all, dvalue_all = lax.scan(back_one_block, back_start, offsets)[0]
    dkey, dvalue = (
        lax.psum_scatter(
            dkey_all.astype(jnp.bfloat16), "expert", scatter_dimension=0, tiled=True
        ).astype(jnp.float32),
        lax.psum_scatter(
            dvalue_all.astype(jnp.bfloat16), "expert", scatter_dimension=0, tiled=True
        ).astype(jnp.float32),
    )
    dquery_n = rotate(dquery, cosine, -sine_part).reshape(row_count, width)
    dkey_n = rotate(dkey, cosine, -sine_part).reshape(row_count, width)
    dquery_pre, querynorm_term = jax.vjp(rms_scale, query_pre, query_gain)[1](dquery_n)
    dkey_pre, keynorm_term = jax.vjp(rms_scale, key_pre, key_gain)[1](dkey_n)
    dquery_r = dquery_pre.astype(jnp.bfloat16)
    dkey_r = dkey_pre.astype(jnp.bfloat16)
    dvalue_r = dvalue.reshape(row_count, width).astype(jnp.bfloat16)
    query_term = jnp.einsum("rd,re->de", normed_r, dquery_r, preferred_element_type=jnp.float32)
    key_term = jnp.einsum("rd,re->de", normed_r, dkey_r, preferred_element_type=jnp.float32)
    value_term = jnp.einsum("rd,re->de", normed_r, dvalue_r, preferred_element_type=jnp.float32)
    dnormed = (
        jnp.einsum("re,de->rd", dquery_r, full_query, preferred_element_type=jnp.float32)
        + jnp.einsum("re,de->rd", dkey_r, full_key, preferred_element_type=jnp.float32)
        + jnp.einsum("re,de->rd", dvalue_r, full_value, preferred_element_type=jnp.float32)
    )
    dinput, attnorm_term = jax.vjp(rms_scale, tokens_in, attn_gain)[1](dnormed)
    tokens_grad = (dmiddle + dinput).astype(jnp.bfloat16)
    dense_terms = (
        query_term,
        key_term,
        value_term,
        output_term,
        router_term,
        attnorm_term,
        querynorm_term,
        keynorm_term,
        mixnorm_term,
    )
    dense_sums = (
        lax.psum_scatter(dense_terms[0], ("group", "expert"), scatter_dimension=0, tiled=True),
        lax.psum_scatter(dense_terms[1], ("group", "expert"), scatter_dimension=0, tiled=True),
        lax.psum_scatter(dense_terms[2], ("group", "expert"), scatter_dimension=0, tiled=True),
        lax.psum_scatter(dense_terms[3], ("group", "expert"), scatter_dimension=0, tiled=True),
        lax.psum_scatter(dense_terms[4], ("group", "expert"), scatter_dimension=0, tiled=True),
        lax.psum_scatter(dense_terms[5], ("group", "expert"), scatter_dimension=0, tiled=True),
        lax.psum_scatter(dense_terms[6], ("group", "expert"), scatter_dimension=0, tiled=True),
        lax.psum_scatter(dense_terms[7], ("group", "expert"), scatter_dimension=0, tiled=True),
        lax.psum_scatter(dense_terms[8], ("group", "expert"), scatter_dimension=0, tiled=True),
    )
    gate_sum, up_sum, down_sum = (
        lax.psum(gate_term[None].astype(jnp.bfloat16), "group").astype(jnp.float32),
        lax.psum(up_term[None].astype(jnp.bfloat16), "group").astype(jnp.float32),
        lax.psum(down_term[None].astype(jnp.bfloat16), "group").astype(jnp.float32),
    )
    return (
        layer_result,
        tokens_grad,
        dense_sums[0],
        dense_sums[1],
        dense_sums[2],
        dense_sums[3],
        dense_sums[4],
        dense_sums[5],
        dense_sums[6],
        dense_sums[7],
        dense_sums[8],
        gate_sum,
        up_sum,
        down_sum,
    )


def solution(mesh):
    placed = (
        P(("group", "expert"), None),
        P(("group", "expert"), None),
        P(("group", "expert"), None),
        P(("group", "expert"), None),
        P(("group", "expert"), None),
        P(("group", "expert"), None),
        P(("group", "expert")),
        P(("group", "expert")),
        P(("group", "expert")),
        P(("group", "expert")),
        P("expert", None, None),
        P("expert", None, None),
        P("expert", None, None),
        P(("group", "expert"), None),
        P("group", None),
        P("group", None),
        P(("group", "expert"), None),
    )
    return jax.shard_map(
        body,
        mesh=mesh,
        in_specs=placed,
        out_specs=(
            P(("group", "expert"), None),
            P(("group", "expert"), None),
            P(("group", "expert"), None),
            P(("group", "expert"), None),
            P(("group", "expert"), None),
            P(("group", "expert"), None),
            P(("group", "expert"), None),
            P(("group", "expert")),
            P(("group", "expert")),
            P(("group", "expert")),
            P(("group", "expert")),
            P("expert", None, None),
            P("expert", None, None),
            P("expert", None, None),
        ),
        check_vma=False,
    )
```

profile of v0, /device:TPU:25, one launch (start us, length us, event | category | flops | bytes accessed | tf_op | source)
XLA Modules:
  0.0 3459.5 jit_solution(9132532183473051332)
XLA Ops:
  12.9 40.2 %all-reduce.9 = (bf16[2048]{0:T(1024)(128)(2,1)S(1)}, bf16[2048]{0:T(1024)(128)(2,1)S(1)}, bf16[2048]{0:T(1024)(128)(2,1)S(1)}, bf16[2048]{0:T(1024)(128)(2,1)S(1)}) all-reduce(bf16[2048]{0:T(1024)(128)(2,1)S(1)} %dynamic-update-slice, bf16[2048]{0:T(1024)(128)(2,1)S(1)} %dynamic-update-slice.1, ...), channel_id=1, replica_groups=mesh['group'=4,'expert'=8] {'group','expert'}, use_global_device_ids=true, to_apply=%add | all-reduce | flops 8192 | bytes 32768
  57.7 31.2 all-gather.12.cloned.1.call-done
  98.0 69.8 %all-gather.8.cloned.1.call-done = bf16[2048,2048]{1,0:T(8,128)(2,1)} async-done(((bf16[64,2048]{1,0:T(8,128)(2,1)}), bf16[2048,2048]{1,0:T(8,128)(2,1)}) %all-gather.8.cloned.1.call-update) | async-done | bytes 8388624 | tf_op jit(solution)/shard_map/all_gather | solution.py:101
  181.8 64.9 %all-gather.14.cloned.1.call-done = bf16[2048,2048]{1,0:T(8,128)(2,1)} async-done(((bf16[64,2048]{1,0:T(8,128)(2,1)}), bf16[2048,2048]{1,0:T(8,128)(2,1)}) %all-gather.14.cloned.1.call-update) | async-done | bytes 8388624 | tf_op jit(solution)/shard_map/all_gather | solution.py:102
  277.6 36.6 %all-gather = bf16[32,64,8]{1,2,0:T(8,128)(2,1)S(1)} all-gather(bf16[1,64,8]{1,2,0:T(8,128)(2,1)S(1)} %bitcast.274), channel_id=1, replica_groups=mesh['group'=4,'expert'=8] {'group','expert'}, dimensions={0}, use_global_device_ids=true | all-gather | bytes 33792 | tf_op jit(solution)/shard_map/all_gather | solution.py:104
  314.5 48.5 %all-gather.10.cloned.1.call-done = bf16[3072,16,128]{2,0,1:T(8,128)(2,1)} async-done(((bf16[384,16,128]{2,0,1:T(8,128)(2,1)}), bf16[3072,16,128]{2,0,1:T(8,128)(2,1)}) %all-gather.10.cloned.1.call-update) | async-done | bytes 12582928 | tf_op jit(solution)/shard_map/all_gather | solution.py:138
  363.1 117.1 %all-gather.16.cloned.1.call-done = bf16[3072,16,128]{2,0,1:T(8,128)(2,1)} async-done(((bf16[384,16,128]{2,0,1:T(8,128)(2,1)}), bf16[3072,16,128]{2,0,1:T(8,128)(2,1)}) %all-gather.16.cloned.1.call-update) | async-done | bytes 12582928 | tf_op jit(solution)/shard_map/all_gather | solution.py:139
  480.1 192.2 %while.30 = (s32[]{:T(128)}, f32[16,384]{1,0:T(8,128)S(1)}, f32[16,384]{1,0:T(8,128)S(1)}, f32[16,384,128]{2,1,0:T(8,128)}, s32[6]{0:T(128)S(1)}, /*index=5*/s32...) while((s32[]{:T(128)}, f32[16,384]{1,0:T(8,128)S(1)}, ...), condition=%wide.region_13.14_spmd.clone, body=%wide.region_6.13_spmd.clone.sunk | while | flops 1648206336 | bytes 51005256 | solution.py:166
  722.7 141.9 %all_to_all.20 = bf16[8,192,2048]{2,1,0:T(8,128)(2,1)} all-to-all(bf16[8,192,2048]{2,1,0:T(8,128)(2,1)S(1)} %get-tuple-element.406), channel_id=1, replica_groups=mesh['group'=4,'expert'=8] {'expert'}, dimensions={0} | all-to-all | bytes 12582912 | tf_op jit(solution)/shard_map/all_to_all | solution.py:189
  892.8 116.0 %all-to-all-done.2 = bf16[8,192,2048]{2,1,0:T(8,128)(2,1)} async-done(((bf16[8,192,2048]{2,1,0:T(8,128)(2,1)}), bf16[8,192,2048]{2,1,0:T(8,128)(2,1)}, u32[]{:S(2)}, u32[]{:S(2)}) %all-to-all-start.2) | async-done | bytes 6291488 | tf_op jit(solution)/shard_map/all_to_all | solution.py:217
  1069.0 125.7 %all-to-all-done.3 = bf16[8,192,2048]{2,1,0:T(8,128)(2,1)} async-done(((bf16[8,192,2048]{2,1,0:T(8,128)(2,1)}), bf16[8,192,2048]{2,1,0:T(8,128)(2,1)}, u32[]{:S(2)}, u32[]{:S(2)}) %all-to-all-start.3) | async-done | bytes 6291488 | tf_op jit(solution)/shard_map/all_to_all | solution.py:236
  1220.1 118.4 %all-to-all-done.1 = bf16[8,192,2048]{2,1,0:T(8,128)(2,1)} async-done(((bf16[8,192,2048]{2,1,0:T(8,128)(2,1)}), bf16[8,192,2048]{2,1,0:T(8,128)(2,1)}, u32[]{:S(2)}, u32[]{:S(2)}) %all-to-all-start.1) | async-done | bytes 6291488 | tf_op jit(solution)/shard_map/all_to_all | solution.py:200
  1426.0 626.8 %while.31 = (s32[]{:T(128)}, f32[384,16,128]{0,2,1:T(8,128)}, f32[3072,16,128]{2,0,1:T(8,128)}, f32[3072,16,128]{0,2,1:T(8,128)}, s32[6]{0:T(128)S(1)}, /*index=...) while((s32[]{:T(128)}, f32[384,16,128]{0,2,1:T(8,128)}, ...), condition=%wide.region_34.35_spmd.clone, body=%wide.region_29.34_spmd.clone.sunk | while | flops 4064094720 | bytes 160065424 | solution.py:316
  1462.0 21.1 dynamic_update_slice.10
  1509.7 20.3 dynamic_update_slice.11
  1567.0 21.1 dynamic_update_slice.10
  1614.7 20.3 dynamic_update_slice.11
  1672.0 21.1 dynamic_update_slice.10
  1719.6 20.3 dynamic_update_slice.11
  1776.9 21.1 dynamic_update_slice.10
  1824.6 20.3 dynamic_update_slice.11
  1881.9 21.1 dynamic_update_slice.10
  1929.6 20.3 dynamic_update_slice.11
  2157.0 36.5 %reduce-scatter.12.cloned.1.call-done = bf16[384,16,128]{2,0,1:T(8,128)(2,1)} async-done(((bf16[3072,16,128]{2,0,1:T(8,128)(2,1)}), bf16[384,16,128]{2,0,1:T(8,128)(2,1)}) %reduce-scatter.12.cloned.1.call-update) | async-done | bytes 1572880 | tf_op jit(solution)/shard_map/reduce_scatter | solution.py:318
  2228.2 95.2 %reduce-scatter.22.cloned.1.call-done = bf16[384,2048]{1,0:T(8,128)(2,1)} async-done(((bf16[3072,2048]{1,0:T(8,128)(2,1)}), bf16[384,2048]{1,0:T(8,128)(2,1)}) %reduce-scatter.22.cloned.1.call-update) | async-done | bytes 1572880 | tf_op jit(solution)/shard_map/convert_element_type | solution.py:331
  2333.3 111.4 %reduce-scatter.24.cloned.1.call-done = f32[64,8]{1,0:T(8,128)} async-done(((f32[2048,8]{1,0:T(8,128)}), f32[64,8]{1,0:T(8,128)}) %reduce-scatter.24.cloned.1.call-update) | async-done | bytes 2064
  2446.2 257.6 %all-reduce.13.cloned.1.call-done = (bf16[1,2048,1024]{2,1,0:T(8,128)(2,1)}, bf16[1,2048,1024]{2,1,0:T(8,128)(2,1)}, bf16[1,1024,2048]{2,1,0:T(8,128)(2,1)}) async-done(((bf16[1,2048,1024]{2,1,0:T(8,128)(2,1)}, bf16[1,2048,1024]{2,1,0:T(8,128)(2,1)}, bf16[1,1024,2048]{2,1,0:T(8,128)(2,1)}), (bf16[1,2048,1024]{2,1,0:T(8,128)(2,1)}, bf16[1,2048,1024]{2,1,0:T(8,128)(2,1)}, ...) | async-done | bytes 12582928 | tf_op jit(solution)/shard_map/psum | solution.py:365
  2740.2 40.6 %all-reduce.8 = (f32[2048]{0:T(1024)S(1)}, f32[2048]{0:T(1024)S(1)}, f32[2048]{0:T(1024)S(1)}, f32[2048]{0:T(1024)S(1)}) all-reduce(f32[2048]{0:T(1024)S(1)} %get-tuple-element.318, f32[2048]{0:T(1024)S(1)} %get-tuple-element.314, f32[2048]{0:T(1024)S(1)} %get-tuple-element.312, ...), channel_id=9, replica_groups=mesh['group'=4,'expert'=8] {'group','expert'}, use_global_device_ids=true, to_apply=%region_46.47.clone | all-reduce | flops 8192 | bytes 65536
  2788.1 102.9 %reduce-scatter.20.cloned.1.call-done = f32[64,2048]{1,0:T(8,128)} async-done(((f32[2048,2048]{1,0:T(8,128)}), f32[64,2048]{1,0:T(8,128)}) %reduce-scatter.20.cloned.1.call-update) | async-done | bytes 524304 | tf_op jit(solution)/shard_map/reduce_scatter | solution.py:357
  2891.0 187.2 %reduce-scatter.14.cloned.1.call-done = f32[64,2048]{1,0:T(8,128)} async-done(((f32[2048,2048]{1,0:T(8,128)}), f32[64,2048]{1,0:T(8,128)}) %reduce-scatter.14.cloned.1.call-update) | async-done | bytes 524304 | tf_op jit(solution)/shard_map/reduce_scatter | solution.py:354
  3078.2 187.4 %reduce-scatter.16.cloned.1.call-done = f32[64,2048]{1,0:T(8,128)} async-done(((f32[2048,2048]{1,0:T(8,128)}), f32[64,2048]{1,0:T(8,128)}) %reduce-scatter.16.cloned.1.call-update) | async-done | bytes 524304 | tf_op jit(solution)/shard_map/reduce_scatter | solution.py:355
  3265.6 187.2 %reduce-scatter.18.cloned.1.call-done = f32[64,2048]{1,0:T(8,128)} async-done(((f32[2048,2048]{1,0:T(8,128)}), f32[64,2048]{1,0:T(8,128)}) %reduce-scatter.18.cloned.1.call-update) | async-done | bytes 524304 | tf_op jit(solution)/shard_map/reduce_scatter | solution.py:356
  (577 shorter events, 1097.1 us)
Async XLA Ops:
  7.2 81.8 %copy-start.6 = (bf16[384,2048]{1,0:T(8,128)(2,1)S(1)}, bf16[384,2048]{1,0:T(8,128)(2,1)}, u32[]{:S(2)}) copy-start(bf16[384,2048]{1,0:T(8,128)(2,1)} %param.21) | copy-start | bytes 4718596
  7.2 81.7 %all-gather.12.cloned.1.call-start = ((), (), s32[]{:S(2)}) async-start(), calls=%async_computation.13 | async-start | bytes 8650752 | tf_op jit(solution)/shard_map/all_gather | solution.py:100
  7.9 159.9 %all-gather.8.cloned.1.call-start = ((), (), s32[]{:S(2)}) async-start(), calls=%async_computation.11 | async-start | bytes 8650752 | tf_op jit(solution)/shard_map/all_gather | solution.py:101
  8.7 238.0 %all-gather.14.cloned.1.call-start = ((), (), s32[]{:S(2)}) async-start(), calls=%async_computation.14 | async-start | bytes 8650752 | tf_op jit(solution)/shard_map/all_gather | solution.py:102
  9.4 353.6 %all-gather.10.cloned.1.call-start = ((), (), s32[]{:S(2)}) async-start(), calls=%async_computation.12 | async-start | bytes 14155776 | tf_op jit(solution)/shard_map/all_gather | solution.py:138
  53.0 193.7 %copy-start.40 = (f32[2048]{0:T(1024)}, f32[2048]{0:T(1024)S(1)}, u32[]{:S(2)}) copy-start(f32[2048]{0:T(1024)S(1)} %convert_element_type.188) | copy-start | bytes 24580
  53.1 121.0 %copy-start.53 = (f32[2048]{0:T(1024)}, f32[2048]{0:T(1024)S(1)}, u32[]{:S(2)}) copy-start(f32[2048]{0:T(1024)S(1)} %convert_element_type.193) | copy-start | bytes 24580
  53.1 121.0 %copy-start.51 = (f32[2048]{0:T(1024)}, f32[2048]{0:T(1024)S(1)}, u32[]{:S(2)}) copy-start(f32[2048]{0:T(1024)S(1)} %convert_element_type.190) | copy-start | bytes 24580
  55.8 122.9 %copy-start.32 = (f32[384,128]{1,0:T(8,128)}, f32[384,128]{1,0:T(8,128)S(1)}, u32[]{:S(2)}) copy-start(f32[384,128]{1,0:T(8,128)S(1)} %get-tuple-element.402) | copy-start | bytes 589828
  57.7 39.8 %copy-start.70 = (f32[384]{0:T(512)}, f32[384]{0:T(512)S(1)}, u32[]{:S(2)}) copy-start(f32[384]{0:T(512)S(1)} %fusion.66) | copy-start | bytes 4612
  57.7 189.0 %copy-start.47 = (f32[384]{0:T(512)}, f32[384]{0:T(512)S(1)}, u32[]{:S(2)}) copy-start(f32[384]{0:T(512)S(1)} %fusion.94) | copy-start | bytes 4612
  98.0 76.1 %copy-start.68 = (f32[384]{0:T(512)}, f32[384]{0:T(512)S(1)}, u32[]{:S(2)}) copy-start(f32[384]{0:T(512)S(1)} %fusion.96) | copy-start | bytes 4612
  181.5 298.6 %all-gather.16.cloned.1.call-start = ((), (), s32[]{:S(2)}) async-start(), calls=%async_computation.15 | async-start | bytes 14155776 | tf_op jit(solution)/shard_map/all_gather | solution.py:139
  255.2 423.5 %all-gather.18.cloned.1.call-start = ((), (), s32[]{:S(2)}) async-start(), calls=%async_computation.16 | async-start | bytes 8650752 | tf_op jit(solution)/shard_map/all_gather | solution.py:103
  262.3 423.0 %copy-start.49 = (f32[2048]{0:T(1024)}, f32[2048]{0:T(1024)S(1)}, u32[]{:S(2)}) copy-start(f32[2048]{0:T(1024)S(1)} %convert_element_type.198) | copy-start | bytes 24580
  269.0 211.1 %copy-start.84 = (s32[1,4]{1,0:T(1,128)S(1)}, s32[1,4]{1,0:T(1,128)}, u32[]{:S(2)}) copy-start(s32[1,4]{1,0:T(1,128)} %param.36) | copy-start | bytes 52
  269.0 211.1 %copy-start.86 = (s32[1,4]{1,0:T(1,128)S(1)}, s32[1,4]{1,0:T(1,128)}, u32[]{:S(2)}) copy-start(s32[1,4]{1,0:T(1,128)} %param.35) | copy-start | bytes 52
  314.4 371.8 %copy-start.45 = (bf16[2048,8]{0,1:T(8,128)(2,1)}, bf16[2048,8]{0,1:T(8,128)(2,1)S(1)}, u32[]{:S(2)}) copy-start(bf16[2048,8]{0,1:T(8,128)(2,1)S(1)} %reshape.596) | copy-start | bytes 98308
  864.6 19.7 slice-start.2
  864.7 144.2 %all-to-all-start.2 = ((bf16[8,192,2048]{2,1,0:T(8,128)(2,1)}), bf16[8,192,2048]{2,1,0:T(8,128)(2,1)}, u32[]{:S(2)}, u32[]{:S(2)}) async-start(bf16[8,192,2048]{2,1,0:T(8,128)(2,1)} %get-tuple-element.405), calls=%async_computation.2 | async-start | bytes 12582912 | tf_op jit(solution)/shard_map/all_to_all | solution.py:217
  1008.8 18.2 copy-start.81
  1050.6 144.0 %all-to-all-start.3 = ((bf16[8,192,2048]{2,1,0:T(8,128)(2,1)}), bf16[8,192,2048]{2,1,0:T(8,128)(2,1)}, u32[]{:S(2)}, u32[]{:S(2)}) async-start(bf16[8,192,2048]{2,1,0:T(8,128)(2,1)} %bitcast.263), calls=%async_computation.3 | async-start | bytes 12582912 | tf_op jit(solution)/shard_map/all_to_all | solution.py:236
  1194.6 143.8 %all-to-all-start.1 = ((bf16[8,192,2048]{2,1,0:T(8,128)(2,1)}), bf16[8,192,2048]{2,1,0:T(8,128)(2,1)}, u32[]{:S(2)}, u32[]{:S(2)}) async-start(bf16[8,192,2048]{2,1,0:T(8,128)(2,1)} %bitcast.262), calls=%async_computation.1 | async-start | bytes 12582912 | tf_op jit(solution)/shard_map/all_to_all | solution.py:200
  1202.1 991.4 %reduce-scatter.12.cloned.1.call-start = ((), (), s32[]{:S(2)}) async-start(), calls=%async_computation.17 | async-start | bytes 14155776 | tf_op jit(solution)/shard_map/reduce_scatter | solution.py:318
  2066.4 257.0 %reduce-scatter.22.cloned.1.call-start = ((), (), s32[]{:S(2)}) async-start(), calls=%async_computation.22 | async-start | bytes 14155776 | tf_op jit(solution)/shard_map/convert_element_type | solution.py:331
  2096.9 347.9 %reduce-scatter.24.cloned.1.call-start = ((), (), s32[]{:S(2)}) async-start(), calls=%async_computation.23 | async-start | bytes 1081344
  2123.2 580.6 %all-reduce.13.cloned.1.call-start = ((), (), s32[]{:S(2)}) async-start(), calls=%async_computation.24 | async-start | bytes 25165824 | tf_op jit(solution)/shard_map/psum | solution.py:365
  2135.0 756.0 %reduce-scatter.20.cloned.1.call-start = ((), (), s32[]{:S(2)}) async-start(), calls=%async_computation.21 | async-start | bytes 17301504 | tf_op jit(solution)/shard_map/reduce_scatter | solution.py:357
  2147.0 931.2 %reduce-scatter.14.cloned.1.call-start = ((), (), s32[]{:S(2)}) async-start(), calls=%async_computation.18 | async-start | bytes 17301504 | tf_op jit(solution)/shard_map/reduce_scatter | solution.py:354
  2212.6 1053.0 %reduce-scatter.16.cloned.1.call-start = ((), (), s32[]{:S(2)}) async-start(), calls=%async_computation.19 | async-start | bytes 17301504 | tf_op jit(solution)/shard_map/reduce_scatter | solution.py:355
  2228.2 1224.6 %reduce-scatter.18.cloned.1.call-start = ((), (), s32[]{:S(2)}) async-start(), calls=%async_computation.20 | async-start | bytes 17301504 | tf_op jit(solution)/shard_map/reduce_scatter | solution.py:356
  2730.0 53.2 %copy-start.71 = (f32[384]{0:T(512)S(1)}, f32[384]{0:T(512)}, u32[]{:S(2)}) copy-start(f32[384]{0:T(512)} %copy-done.70) | copy-start | bytes 4612
  (93 other events, 567.2 us)
Sparse Core Ops, SparseCore 0:
  11.0 77.8 all-gather.11
  91.9 75.8 all-gather.7
  170.8 75.8 all-gather.13
  248.7 114.2 all-gather.9
  365.1 114.9 all-gather.15
  483.0 77.1 all-gather.17
  2066.5 126.9 reduce-scatter.11
  2195.8 127.5 reduce-scatter.21
  2325.6 119.0 reduce-scatter.23
  2449.6 254.1 all-reduce.12
  2706.8 184.1 reduce-scatter.19
  2893.8 184.3 reduce-scatter.13
  3081.2 184.3 reduce-scatter.15
  3268.4 184.3 reduce-scatter.17
where the time goes:
time: 3480 us; the launch traced here: 3460 us
  waiting for transfers between devices  1860 us (53%)
  matrix products  584 us (17%)
  local copies, waits for them, and re-layouts  506 us (15%)
  blocking collectives  259 us (7%)
  other arithmetic  187 us (5%)
    psum x1, waiting for transfers between devices, body(): lax.psum(gate_term[None].astype(jnp.bfloat16), 'group').astype(jnp.float32)  258 us
    reduce_scatter x1, waiting for transfers between devices, body(): lax.psum_scatter(dense_terms[1], ('group', 'expert'), scatter_dimension=0...  187 us
    reduce_scatter x1, waiting for transfers between devices, body(): lax.psum_scatter(dense_terms[2], ('group', 'expert'), scatter_dimension=0...  187 us
    reduce_scatter x1, waiting for transfers between devices, body(): lax.psum_scatter(dense_terms[0], ('group', 'expert'), scatter_dimension=0...  187 us
    dynamic_update_slice x12, local copies, waits for them, and re-layouts, back_one_block(): lax.dynamic_update_slice_in_dim(dvalue_all, lax.dynamic_slice_in_dim(dval...  153 us
    all_to_all x1, blocking collectives, body(): lax.all_to_all(send_rows.reshape(ranks, capacity, width), 'expert', split...  142 us
    dynamic_update_slice x6, local copies, waits for them, and re-layouts, back_one_block(): lax.dynamic_update_slice_in_dim(dkey_all, lax.dynamic_slice_in_dim(dkey_a...  126 us
    all_to_all x1, waiting for transfers between devices, body(): lax.all_to_all(dinputs.reshape(ranks, capacity, width), 'expert', split_a...  126 us
  transfers between devices with their start and end apart: 17, of which 16 were waited for; matrix products, arithmetic and copies ran while one was open for 13% of the time, Pallas kernels for 0%

commit v1 on v0

v1 whole, which is shorter than its diff:
```python
import functools

import jax
import jax.numpy as jnp
from jax import lax
from jax.experimental import pallas as pl
from jax.experimental.pallas import tpu as pltpu
from jax.sharding import PartitionSpec as P

HEADS = 16
HEAD_DIM = 128
TOP = 2
EPS = 1e-05
NEG = -1e30
MESH = pl.DeviceIdType.MESH
BF = jnp.bfloat16
F32 = jnp.float32


def share_all(block, collective_id):
    groups, ranks = lax.axis_size("group"), lax.axis_size("expert")
    total = groups * ranks

    def kernel(x_ref, o_ref, send_sem, recv_sem):
        me = lax.axis_index("group") * ranks + lax.axis_index("expert")

        def place(step):
            flat = lax.rem(me + step, total)
            return (flat // ranks, lax.rem(flat, ranks))

        barrier = pltpu.get_barrier_semaphore()

        def greet(step, carry):
            pl.semaphore_signal(barrier, inc=1, device_id=place(step), device_id_type=MESH)
            return carry

        lax.fori_loop(1, total, greet, 0)
        pl.semaphore_wait(barrier, total - 1)

        def copy(step):
            return pltpu.make_async_remote_copy(
                src_ref=x_ref,
                dst_ref=o_ref.at[me],
                send_sem=send_sem.at[step],
                recv_sem=recv_sem.at[step],
                device_id=place(step),
                device_id_type=MESH,
            )

        def send(step, carry):
            copy(step).start()
            return carry

        lax.fori_loop(1, total, send, 0)
        o_ref[me] = x_ref[...]

        def settle(step, carry):
            copy(step).wait()
            return carry

        lax.fori_loop(1, total, settle, 0)

    return pl.pallas_call(
        kernel,
        out_shape=jax.ShapeDtypeStruct((total,) + block.shape, block.dtype),
        in_specs=[pl.BlockSpec(memory_space=pltpu.VMEM)],
        out_specs=pl.BlockSpec(memory_space=pltpu.VMEM),
        scratch_shapes=[pltpu.SemaphoreType.DMA((total,)), pltpu.SemaphoreType.DMA((total,))],
        compiler_params=pltpu.CompilerParams(collective_id=collective_id, has_side_effects=True),
        name="share_all",
    )(block)


def share_group(block, collective_id, add=False):
    ranks = lax.axis_size("expert")

    def kernel(x_ref, o_ref, *scratch):
        if add:
            land, send_sem, recv_sem = scratch
        else:
            send_sem, recv_sem = scratch
            land = o_ref
        me = lax.axis_index("expert")
        barrier = pltpu.get_barrier_semaphore()
        for step in range(1, ranks):
            pl.semaphore_signal(
                barrier,
                inc=1,
                device_id={"expert": lax.rem(me + step, ranks)},
                device_id_type=MESH,
            )
        pl.semaphore_wait(barrier, ranks - 1)
        copies = []
        for step in range(1, ranks):
            copy = pltpu.make_async_remote_copy(
                src_ref=x_ref,
                dst_ref=land.at[me],
                send_sem=send_sem.at[step],
                recv_sem=recv_sem.at[step],
                device_id={"expert": lax.rem(me + step, ranks)},
                device_id_type=MESH,
            )
            copy.start()
            copies.append(copy)
        land[me] = x_ref[...]
        for copy in copies:
            copy.wait()
        if add:
            total = land[0]
            for rank in range(1, ranks):
                total = total + land[rank]
            o_ref[...] = total

    landing = (ranks,) + block.shape
    scratch = [pltpu.SemaphoreType.DMA((ranks,)), pltpu.SemaphoreType.DMA((ranks,))]
    if add:
        scratch = [pltpu.VMEM(landing, block.dtype)] + scratch
    return pl.pallas_call(
        kernel,
        out_shape=jax.ShapeDtypeStruct(block.shape if add else landing, block.dtype),
        in_specs=[pl.BlockSpec(memory_space=pltpu.VMEM)],
        out_specs=pl.BlockSpec(memory_space=pltpu.VMEM),
        scratch_shapes=scratch,
        compiler_params=pltpu.CompilerParams(collective_id=collective_id, has_side_effects=True),
        name="sum_group" if add else "share_group",
    )(block)


def partner_swap(block):
    ranks = lax.axis_size("expert")
    return lax.ppermute(block, "expert", [(i, i ^ 1) for i in range(ranks)])


def chip_shift(block, step=1):
    ranks = lax.axis_size("expert")
    return lax.ppermute(block, "expert", [(i, (i + 2 * step) % ranks) for i in range(ranks)])


def ring_gather(block, axis):
    ranks = lax.axis_size("expert")
    chips = ranks // 2
    me = lax.axis_index("expert")
    chip, core = me // 2, me % 2
    size = block.shape[axis]
    shape = list(block.shape)
    shape[axis] = size * ranks
    whole = jnp.zeros(shape, block.dtype)
    moving = block
    for step in range(chips):
        if step:
            moving = chip_shift(moving)
        other = partner_swap(moving)
        source = lax.rem(chip - step + chips, chips) * 2
        whole = lax.dynamic_update_slice_in_dim(whole, moving, (source + core) * size, axis)
        whole = lax.dynamic_update_slice_in_dim(whole, other, (source + 1 - core) * size, axis)
    return whole


def ring_scatter(partial):
    ranks = lax.axis_size("expert")
    chips = ranks // 2
    me = lax.axis_index("expert")
    chip, core = me // 2, me % 2
    rows, width = partial.shape[0] // ranks, partial.shape[1]
    halves = partial.reshape(chips, 2, rows, width)
    away = lax.dynamic_index_in_dim(halves, 1 - core, 1, keepdims=False)
    mine = lax.dynamic_index_in_dim(halves, core, 1, keepdims=False)
    pair = (mine.astype(F32) + partner_swap(away).astype(F32)).astype(BF)

    def for_chip(step):
        return lax.dynamic_index_in_dim(
            pair, lax.rem(chip - step + chips, chips), 0, keepdims=False
        )

    moving = for_chip(1)
    for step in range(2, chips):
        moving = (chip_shift(moving).astype(F32) + for_chip(step).astype(F32)).astype(BF)
    return chip_shift(moving).astype(F32) + for_chip(0).astype(F32)


def attention_forward(queries, keys, values, starts, lowest):
    rows = queries.shape[0]
    heads = queries.shape[1] // HEAD_DIM
    blocks, _, block = starts.shape
    scale = HEAD_DIM ** (-0.5)

    def kernel(low_ref, start_ref, q_ref, k_ref, v_ref, o_ref, lse_ref):
        i = pl.program_id(1)
        q = q_ref[...]
        start = start_ref[0]
        q_index = i * block + lax.broadcasted_iota(jnp.int32, (1, block), 1)
        k_local = lax.broadcasted_iota(jnp.int32, (block, block), 0)

        def step(j, carry):
            top, total, acc = carry
            at = pl.multiple_of(j * block, block)
            k = k_ref[pl.ds(at, block), :]
            v = v_ref[pl.ds(at, block), :]
            s = (
                lax.dot_general(k, q, (((1,), (1,)), ((), ())), preferred_element_type=F32)
                * scale
            )
            k_index = k_local + j * block
            s = jnp.where((k_index <= q_index) & (k_index >= start), s, NEG)
            new_top = jnp.maximum(top, jnp.max(s, axis=0, keepdims=True))
            p = jnp.exp(s - new_top)
            shrink = jnp.exp(top - new_top)
            total = total * shrink + jnp.sum(p, axis=0, keepdims=True)
            acc = acc * shrink + lax.dot_general(
                v, p.astype(BF), (((0,), (0,)), ((), ())), preferred_element_type=F32
            )
            return (new_top, total, acc)

        top, total, acc = lax.fori_loop(
            low_ref[i],
            i + 1,
            step,
            (
                jnp.full((1, block), NEG, F32),
                jnp.zeros((1, block), F32),
                jnp.zeros((HEAD_DIM, block), F32),
            ),
        )
        o_ref[...] = (acc / total).T.astype(BF)
        lse_ref[0, 0] = top + jnp.log(total)

    return pl.pallas_call(
        kernel,
        out_shape=(
            jax.ShapeDtypeStruct((rows, heads * HEAD_DIM), BF),
            jax.ShapeDtypeStruct((heads, blocks, 1, block), F32),
        ),
        grid_spec=pltpu.PrefetchScalarGridSpec(
            num_scalar_prefetch=1,
            grid=(heads, blocks),
            in_specs=[
                pl.BlockSpec((1, 1, block), lambda h, i, low: (i, 0, 0)),
                pl.BlockSpec((block, HEAD_DIM), lambda h, i, low: (i, h)),
                pl.BlockSpec((rows, HEAD_DIM), lambda h, i, low: (0, h)),
                pl.BlockSpec((rows, HEAD_DIM), lambda h, i, low: (0, h)),
            ],
            out_specs=[
                pl.BlockSpec((block, HEAD_DIM), lambda h, i, low: (i, h)),
                pl.BlockSpec((1, 1, 1, block), lambda h, i, low: (h, i, 0, 0)),
            ],
        ),
        compiler_params=pltpu.CompilerParams(vmem_limit_bytes=48 << 20),
        cost_estimate=pl.CostEstimate(
            flops=2 * rows * rows * HEAD_DIM * heads,
            bytes_accessed=8 * rows * heads * HEAD_DIM,
            transcendentals=rows * rows * heads // 2,
        ),
        name="attention_forward",
    )(lowest, starts, queries, keys, values)


def attention_backward(queries, keys, values, douts, lse, delta, starts, highest):
    rows = queries.shape[0]
    heads = queries.shape[1] // HEAD_DIM
    blocks, _, block = starts.shape
    scale = HEAD_DIM ** (-0.5)

    def kernel(
        high_ref, start_ref, q_ref, do_ref, k_ref, v_ref, lse_ref, delta_ref, dq_ref, dk_ref, dv_ref
    ):
        j = pl.program_id(1)

        @pl.when(j == 0)
        def _():
            dq_ref[...] = jnp.zeros_like(dq_ref)

        k = k_ref[...]
        v = v_ref[...]
        k_index = j * block + lax.broadcasted_iota(jnp.int32, (block, block), 0)
        q_local = lax.broadcasted_iota(jnp.int32, (1, block), 1)

        def step(i, carry):
            dk, dv = carry
            at = pl.multiple_of(i * block, block)
            q = q_ref[pl.ds(at, block), :]
            do = do_ref[pl.ds(at, block), :]
            s = (
                lax.dot_general(k, q, (((1,), (1,)), ((), ())), preferred_element_type=F32)
                * scale
            )
            allowed = (k_index <= q_local + i * block) & (k_index >= start_ref[i])
            p = jnp.exp(jnp.where(allowed, s, NEG) - lse_ref[0, i])
            dv = dv + jnp.dot(p.astype(BF), do, preferred_element_type=F32)
            dp = lax.dot_general(v, do, (((1,), (1,)), ((), ())), preferred_element_type=F32)
            ds = (p * (dp - delta_ref[0, i])).astype(BF)
            dk = dk + jnp.dot(ds, q, preferred_element_type=F32)
            dq_ref[pl.ds(at, block), :] += (
                lax.dot_general(ds, k, (((0,), (0,)), ((), ())), preferred_element_type=F32)
                * scale
            )
            return (dk, dv)

        zero = jnp.zeros((block, HEAD_DIM), F32)
        dk, dv = lax.fori_loop(j, high_ref[j] + 1, step, (zero, zero))
        dk_ref[...] = dk * scale
        dv_ref[...] = dv

    whole = pl.BlockSpec((rows, HEAD_DIM), lambda h, j, high: (0, h))
    part = pl.BlockSpec((block, HEAD_DIM), lambda h, j, high: (j, h))
    line = pl.BlockSpec((1, blocks, 1, block), lambda h, j, high: (h, 0, 0, 0))
    shape = jax.ShapeDtypeStruct((rows, heads * HEAD_DIM), F32)
    return pl.pallas_call(
        kernel,
        out_shape=(shape, shape, shape),
        grid_spec=pltpu.PrefetchScalarGridSpec(
            num_scalar_prefetch=1,
            grid=(heads, blocks),
            in_specs=[
                pl.BlockSpec((blocks, 1, block), lambda h, j, high: (0, 0, 0)),
                whole,
                whole,
                part,
                part,
                line,
                line,
            ],
            out_specs=[whole, part, part],
        ),
        compiler_params=pltpu.CompilerParams(vmem_limit_bytes=48 << 20),
        cost_estimate=pl.CostEstimate(
            flops=5 * rows * rows * HEAD_DIM * heads,
            bytes_accessed=20 * rows * heads * HEAD_DIM,
            transcendentals=rows * rows * heads // 2,
        ),
        name="attention_backward",
    )(highest, starts, queries, douts, keys, values, lse, delta)


def inverse_rms(total, width):
    return lax.rsqrt(total / width + EPS)


def spin(values, cosine, sine):
    half = HEAD_DIM // 2
    pieces = []
    for at in range(0, values.shape[1], HEAD_DIM):
        low, high = values[:, at : at + half], values[:, at + half : at + HEAD_DIM]
        pieces += [low * cosine - high * sine, high * cosine + low * sine]
    return jnp.concatenate(pieces, axis=1)


def norm_back(values, inverse, gain, grad):
    scaled = values * inverse
    weighted = grad * gain
    mean = jnp.mean(scaled * weighted, axis=-1, keepdims=True)
    return inverse * (weighted - scaled * mean), jnp.sum(grad * scaled, axis=0)


def dot_nt(a, b):
    return lax.dot_general(a, b, (((1,), (1,)), ((), ())), preferred_element_type=F32)


def dot_tn(a, b):
    return lax.dot_general(a, b, (((0,), (0,)), ((), ())), preferred_element_type=F32)


def dot_nn(a, b):
    return jnp.dot(a, b, preferred_element_type=F32)


def layout_of(lengths, seq_order, rows):
    length_row, order_row = lengths[0], seq_order[0]
    count = order_row.shape[0]
    chosen = (order_row[:, None] == jnp.arange(count, dtype=jnp.int32)[None, :]).astype(jnp.int32)
    placed = jnp.sum(chosen * length_row[None, :], axis=1)
    ends = jnp.sum(
        jnp.where(jnp.arange(count)[None, :] <= jnp.arange(count)[:, None], placed[None, :], 0),
        axis=1,
    )
    index = jnp.arange(rows, dtype=jnp.int32)
    passed = (index[:, None] >= ends[None, :]).astype(jnp.int32)
    begin = jnp.sum(passed * placed[None, :], axis=1)
    segment = jnp.sum(passed, axis=1)
    inside = (segment[:, None] == jnp.arange(count, dtype=jnp.int32)[None, :]).astype(jnp.int32)
    final = jnp.sum(inside * ends[None, :], axis=1) - 1
    return index, begin, final


def body(
    tokens,
    query_weight,
    key_weight,
    value_weight,
    output_weight,
    router_weight,
    attnorm,
    querynorm,
    keynorm,
    mixnorm,
    gate_weight,
    up_weight,
    down_weight,
    routes,
    lengths,
    seq_order,
    cotangent,
):
    rows, width = tokens.shape
    ranks = lax.axis_size("expert")
    groups = lax.axis_size("group")
    me = lax.axis_index("expert")
    all_rows = rows * ranks
    capacity = 2 * rows * TOP // ranks
    columns = width // ranks
    shard = query_weight.shape[0]
    experts = router_weight.shape[1]
    block = rows
    blocks = all_rows // block

    small = jnp.concatenate(
        [attnorm, querynorm, keynorm, mixnorm, router_weight.T.reshape(-1)], axis=0
    )
    packed = jnp.zeros((2048,), BF).at[: small.shape[0]].set(small).reshape(16, 128)
    everyone = share_all(packed, 1).reshape(groups * ranks, 2048)
    attn_gain = everyone[:, :shard].reshape(width).astype(F32)
    query_gain = everyone[:, shard : 2 * shard].reshape(width).astype(F32)
    key_gain = everyone[:, 2 * shard : 3 * shard].reshape(width).astype(F32)
    mix_gain = everyone[:, 3 * shard : 4 * shard].reshape(width).astype(F32)
    router_t = (
        everyone[:, 4 * shard : (4 + experts) * shard]
        .reshape(groups * ranks, experts, shard)
        .transpose(1, 0, 2)
        .reshape(experts, width)
    )
    my_query_gain = lax.dynamic_slice_in_dim(query_gain, me * columns, columns)
    my_key_gain = lax.dynamic_slice_in_dim(key_gain, me * columns, columns)

    stacked = jnp.concatenate(
        [
            part.reshape(shard, ranks, columns).transpose(1, 0, 2)
            for part in (query_weight, key_weight, value_weight)
        ],
        axis=2,
    )
    stacked = lax.all_to_all(stacked, "expert", split_axis=0, concat_axis=0, tiled=True)
    in_weight = lax.all_gather(stacked.reshape(ranks * shard, 3 * columns), "group", axis=0, tiled=True)
    full_output = lax.all_gather(output_weight, ("group", "expert"), axis=0, tiled=True)

    index, begin, final = layout_of(lengths, seq_order, all_rows)
    starts = begin.reshape(blocks, 1, block)
    lowest = begin.reshape(blocks, block)[:, 0] // block
    highest = final.reshape(blocks, block)[:, block - 1] // block
    position = (index - begin).astype(F32)
    frequency = 10000.0 ** (-(jnp.arange(HEAD_DIM // 2, dtype=F32) * 2.0 / HEAD_DIM))
    angles = position[:, None] * frequency[None, :]
    cosine, sine = jnp.cos(angles), jnp.sin(angles)

    all_routes = share_group(
        jnp.zeros((8, 128), jnp.int32)
        .reshape(-1)
        .at[: rows * TOP]
        .set(routes.T.reshape(-1))
        .reshape(8, 128),
        2,
    )
    all_routes = all_routes.reshape(ranks, -1)[:, : rows * TOP].reshape(ranks, TOP, rows)
    named = jnp.any(all_routes == me, axis=1)
    counted = jnp.cumsum(named.astype(jnp.int32), axis=1) - 1
    slot_of = jnp.where(named, counted, -1)
    pick = (
        slot_of[:, None, :] == jnp.arange(capacity, dtype=jnp.int32)[None, :, None]
    ).astype(BF)

    def select(array):
        return jnp.einsum(
            "rst,rtd->rsd",
            pick,
            array.reshape(ranks, rows, -1),
            preferred_element_type=F32,
        ).astype(BF).reshape(ranks * capacity, -1)

    def place(array):
        return jnp.einsum(
            "rst,rsd->rtd",
            pick,
            array.reshape(ranks, capacity, -1),
            preferred_element_type=F32,
        ).astype(BF).reshape(all_rows, -1)

    all_tokens = ring_gather(tokens, 0)
    tokens_f = all_tokens.astype(F32)
    token_inverse = lax.rsqrt(jnp.mean(tokens_f * tokens_f, axis=-1, keepdims=True) + EPS)
    normed = (tokens_f * token_inverse * attn_gain).astype(BF)
    pre = dot_nn(normed, in_weight)
    query_pre, key_pre, value_pre = (
        pre[:, :columns],
        pre[:, columns : 2 * columns],
        pre[:, 2 * columns :],
    )
    squares = jnp.stack([jnp.sum(query_pre * query_pre, axis=1), jnp.sum(key_pre * key_pre, axis=1)])
    squares = share_group(squares.reshape(-1, 128), 3, add=True).reshape(2, all_rows)
    query_inverse = lax.rsqrt(squares[0] / width + EPS)[:, None]
    key_inverse = lax.rsqrt(squares[1] / width + EPS)[:, None]
    queries = spin(query_pre * query_inverse * my_query_gain, cosine, sine).astype(BF)
    keys = spin(key_pre * key_inverse * my_key_gain, cosine, sine).astype(BF)
    values = value_pre.astype(BF)
    attended_mine, lse = attention_forward(queries, keys, values, starts, lowest)
    all_cot = ring_gather(cotangent, 0)
    attended = ring_gather(attended_mine, 1)

    def own_rows(array):
        return lax.dynamic_slice_in_dim(array, me * rows, rows, 0)

    own_attended = own_rows(attended)
    middle = tokens.astype(F32) + dot_nn(own_attended, full_output)
    middle_inverse = lax.rsqrt(jnp.mean(middle * middle, axis=-1, keepdims=True) + EPS)
    mixed = (middle * middle_inverse * mix_gain).astype(BF)
    logits = dot_nt(mixed, router_t)
    shifted = jnp.exp(logits - jnp.max(logits, axis=1, keepdims=True))
    share = shifted / jnp.sum(shifted, axis=1, keepdims=True)

    middle_e = select(all_tokens).astype(F32) + dot_nn(select(attended), full_output)
    inverse_e = lax.rsqrt(jnp.mean(middle_e * middle_e, axis=-1, keepdims=True) + EPS)
    mixed_e = (middle_e * inverse_e * mix_gain).astype(BF)
    logits_e = dot_nt(mixed_e, router_t)
    shifted_e = jnp.exp(logits_e - jnp.max(logits_e, axis=1, keepdims=True))
    mine_hot = (jnp.arange(experts, dtype=jnp.int32) == me).astype(F32)
    gates_e = (
        jnp.sum(shifted_e * mine_hot, axis=1, keepdims=True)
        / jnp.sum(shifted_e, axis=1, keepdims=True)
    )
    gate_pre = dot_nn(mixed_e, gate_weight[0])
    up_pre = dot_nn(mixed_e, up_weight[0])
    sigma = jax.nn.sigmoid(gate_pre)
    hidden = (gate_pre * sigma * up_pre).astype(BF)
    expert_out = dot_nn(hidden, down_weight[0]).astype(BF)
    out_f = expert_out.astype(F32)
    layer_result = (middle + ring_scatter(place((gates_e * out_f).astype(BF)))).astype(BF)

    cot_e = select(all_cot).astype(F32)
    dcopy = (gates_e * cot_e).astype(BF)
    dgates_e = jnp.sum(out_f * cot_e, axis=1)
    dhidden = dot_nt(dcopy, down_weight[0])
    dgate_pre = (dhidden * up_pre * sigma * (1.0 + gate_pre * (1.0 - sigma))).astype(BF)
    dup_pre = (dhidden * gate_pre * sigma).astype(BF)
    dinputs = (dot_nt(dgate_pre, gate_weight[0]) + dot_nt(dup_pre, up_weight[0])).astype(BF)
    dmixed = ring_scatter(place(dinputs))
    down_term = dot_tn(hidden, dcopy).astype(BF)
    gate_term = dot_tn(mixed_e, dgate_pre).astype(BF)
    up_term = dot_tn(mixed_e, dup_pre).astype(BF)
    gate_sum, up_sum, down_sum = (
        lax.psum(gate_term, "group").astype(F32)[None],
        lax.psum(up_term, "group").astype(F32)[None],
        lax.psum(down_term, "group").astype(F32)[None],
    )

    dgates_t = jnp.sum(
        pick.astype(F32) * dgates_e.reshape(ranks, capacity)[:, :, None], axis=1
    ).reshape(-1, 128)
    dshare = own_rows(share_group(dgates_t, 4).reshape(experts, all_rows).T)
    dlogits = (share * (dshare - jnp.sum(share * dshare, axis=1, keepdims=True))).astype(BF)
    router_term = dot_tn(dlogits, mixed)
    dmixed = dmixed + dot_nn(dlogits, router_t)
    middle_part, mixnorm_term = norm_back(middle, middle_inverse, mix_gain, dmixed)
    dmiddle = cotangent.astype(F32) + middle_part
    dprojected = dmiddle.astype(BF)
    output_term = dot_tn(own_attended, dprojected)
    output_sum = lax.psum_scatter(
        output_term.astype(BF), ("group", "expert"), scatter_dimension=0, tiled=True
    ).astype(F32)
    dattended_own = dot_nt(dprojected, full_output).astype(BF)
    dattended = lax.all_to_all(
        dattended_own.reshape(rows, ranks, columns).transpose(1, 0, 2),
        "expert",
        split_axis=0,
        concat_axis=0,
        tiled=True,
    ).reshape(all_rows, columns)

    heads = columns // HEAD_DIM
    delta = jnp.stack(
        [
            jnp.sum(
                dattended[:, h * HEAD_DIM : (h + 1) * HEAD_DIM].astype(F32)
                * attended_mine[:, h * HEAD_DIM : (h + 1) * HEAD_DIM].astype(F32),
                axis=1,
            )
            for h in range(heads)
        ]
    ).reshape(heads, blocks, 1, block)
    dquery, dkey, dvalue = attention_backward(
        queries, keys, values, dattended, lse, delta, starts, highest
    )
    dquery_n = spin(dquery, cosine, -sine)
    dkey_n = spin(dkey, cosine, -sine)
    query_n = query_pre * query_inverse
    key_n = key_pre * key_inverse
    query_w = dquery_n * my_query_gain
    key_w = dkey_n * my_key_gain
    means = jnp.stack([jnp.sum(query_n * query_w, axis=1), jnp.sum(key_n * key_w, axis=1)])
    means = share_group(means.reshape(-1, 128), 5, add=True).reshape(2, all_rows) / width
    querynorm_term = jnp.sum(dquery_n * query_n, axis=0)
    keynorm_term = jnp.sum(dkey_n * key_n, axis=0)
    dquery_pre = query_inverse * (query_w - query_n * means[0][:, None])
    dkey_pre = key_inverse * (key_w - key_n * means[1][:, None])
    dpre = jnp.concatenate([dquery_pre.astype(BF), dkey_pre.astype(BF), dvalue.astype(BF)], axis=1)
    dnormed = ring_scatter(dot_nt(dpre, in_weight).astype(BF))
    in_term = dot_tn(normed, dpre).astype(BF)
    in_sum = lax.psum_scatter(in_term, "group", scatter_dimension=0, tiled=True)
    in_sum = lax.all_to_all(
        in_sum.reshape(ranks, shard, 3 * columns), "expert", split_axis=0, concat_axis=0, tiled=True
    )
    query_sum, key_sum, value_sum = (
        in_sum[:, :, i * columns : (i + 1) * columns]
        .transpose(1, 0, 2)
        .reshape(shard, width)
        .astype(F32)
        for i in range(3)
    )
    own_f = tokens.astype(F32)
    dinput, attnorm_term = norm_back(own_f, own_rows(token_inverse), attn_gain, dnormed)
    tokens_grad = (dmiddle + dinput).astype(BF)

    def spread(part):
        return lax.dynamic_update_slice(jnp.zeros((width,), F32), part, (me * columns,))

    terms = jnp.concatenate(
        [
            router_term,
            attnorm_term[None],
            spread(querynorm_term)[None],
            spread(keynorm_term)[None],
            mixnorm_term[None],
        ],
        axis=0,
    )
    sums = lax.psum_scatter(terms.T, ("group", "expert"), scatter_dimension=0, tiled=True)
    router_sum = sums[:, :experts]
    gains = sums[:, experts:].T
    return (
        layer_result,
        tokens_grad,
        query_sum,
        key_sum,
        value_sum,
        output_sum,
        router_sum,
        gains[0],
        gains[1],
        gains[2],
        gains[3],
        gate_sum,
        up_sum,
        down_sum,
    )


def solution(mesh):
    rows = P(("group", "expert"), None)
    line = P(("group", "expert"))
    expert = P("expert", None, None)
    group = P("group", None)
    return jax.shard_map(
        body,
        mesh=mesh,
        in_specs=(
            (rows,) * 6 + (line,) * 4 + (expert,) * 3 + (rows, group, group, rows)
        ),
        out_specs=(rows,) * 7 + (line,) * 4 + (expert,) * 3,
        check_vma=False,
    )
```

time: 3480 us -> 1610 us (0.46)
  waiting for transfers between devices: 1860 us -> 686 us
  local copies, waits for them, and re-layouts: 506 us -> 127 us
  matrix products: 584 us -> 243 us
  Pallas kernels: 0 us -> 279 us
  blocking collectives: 259 us -> 23.6 us
  other arithmetic: 187 us -> 135 us
  starting transfers between devices: 23.7 us -> 75 us
    reduce_scatter x5 -> x2, waiting for transfers between devices: 701 us -> 149 us  [the longest x1 149 us: body(): lax.psum_scatter(output_term.astype(BF), ('group', 'expert'), scatter_dim...]
    dot_general x65 -> x25, matrix products: 582 us -> 243 us  [the longest x7 73.9 us: dot_nn(): return jnp.dot(a, b, preferred_element_type=F32)]
    all_to_all x3 -> x2, waiting for transfers between devices: 360 us -> 23.3 us  [the longest x1 23.2 us: body(): lax.all_to_all(dattended_own.reshape(rows, ranks, columns).transpose(1, 0...]
    all_gather x5 -> x1, waiting for transfers between devices: 332 us -> 0.02 us  [body(): lax.all_gather(stacked.reshape(ranks * shard, 3 * columns), 'group', axis...]
    ppermute x0 -> x33, waiting for transfers between devices: none -> 309 us  [the longest x18 308 us: chip_shift(): lax.ppermute(block, 'expert', [(i, (i + 2 * step) % ranks) for i in range...]
    pallas_call x0 -> x7, Pallas kernels: none -> 279 us  [the longest x4 128 us: share_group(): pl.pallas_call(kernel, out_shape=jax.ShapeDtypeStruct(block.shape if add...]
    dynamic_update_slice x18 -> x26, local copies, waits for them, and re-layouts: 279 us -> 53.3 us  [the longest x12 27.4 us: ring_gather(): lax.dynamic_update_slice_in_dim(whole, other, (source + 1 - core) * size,...]
    psum x1, waiting for transfers between devices: 258 us -> 109 us  [body(): lax.psum(gate_term, 'group').astype(F32)[None]]
  transfers between devices with their start and end apart: 17 -> 41, of which waited for: 16 -> 16; matrix products, arithmetic and copies ran while one was open for 13% -> 21% of each run, Pallas kernels for 0% -> 14%
where the time goes in v1:
time: 1610 us; the launch traced here: 1580 us
  waiting for transfers between devices  686 us (43%)
  Pallas kernels  279 us (17%)
  matrix products  243 us (15%)
  other arithmetic  135 us (8%)
  local copies, waits for them, and re-layouts  127 us (8%)
  starting transfers between devices  75 us (5%)
  blocking collectives  23.6 us (1%)
    ppermute x18, waiting for transfers between devices, chip_shift(): lax.ppermute(block, 'expert', [(i, (i + 2 * step) % ranks) for i in range...  308 us
    reduce_scatter x1, waiting for transfers between devices, body(): lax.psum_scatter(output_term.astype(BF), ('group', 'expert'), scatter_dim...  149 us
    pallas_call x4, Pallas kernels, share_group(): pl.pallas_call(kernel, out_shape=jax.ShapeDtypeStruct(block.shape if add...  128 us
    psum x1, waiting for transfers between devices, body(): lax.psum(gate_term, 'group').astype(F32)[None]  109 us
    unnamed x7, waiting for transfers between devices  96.9 us
    dot_general x7, matrix products, dot_nn(): return jnp.dot(a, b, preferred_element_type=F32)  73.9 us
    pallas_call x1, Pallas kernels, share_all(): pl.pallas_call(kernel, out_shape=jax.ShapeDtypeStruct((total,) + block.sh...  70.2 us
    dot_general x6, matrix products, dot_tn(): lax.dot_general(a, b, (((0,), (0,)), ((), ())), preferred_element_type=F32)  60.1 us
  transfers between devices with their start and end apart: 41, of which 16 were waited for; matrix products, arithmetic and copies ran while one was open for 21% of the time, Pallas kernels for 14%

profile of v1, /device:TPU:25, one launch (start us, length us, event | category | flops | bytes accessed | tf_op | source)
XLA Modules:
  0.0 1584.4 jit_solution(9821407990517910832)
XLA Ops:
  10.7 23.6 %all_to_all.15 = bf16[8,64,768]{2,1,0:T(8,128)(2,1)} all-to-all(bf16[8,64,768]{2,1,0:T(8,128)(2,1)S(1)} %copy.72), channel_id=1, replica_groups=mesh['group'=4,'expert'=8] {'expert'}, dimensions={0} | all-to-all | bytes 1572864 | tf_op jit(solution)/shard_map/all_to_all | solution.py:440
  36.2 33.9 %collective-permute-done.1 = bf16[384,2048]{1,0:T(8,128)(2,1)} collective-permute-done((bf16[384,2048]{1,0:T(8,128)(2,1)S(1)}, bf16[384,2048]{1,0:T(8,128)(2,1)}, u32[]{:S(2)}, u32[]{:S(2)}) %collective-permute-start.1) | collective-permute-done | bytes 1572896 | tf_op jit(solution)/shard_map/ppermute | solution.py:136
  75.5 35.1 %collective-permute-done.3 = bf16[384,2048]{1,0:T(8,128)(2,1)} collective-permute-done((bf16[384,2048]{1,0:T(8,128)(2,1)}, bf16[384,2048]{1,0:T(8,128)(2,1)}, u32[]{:S(2)}, u32[]{:S(2)}) %collective-permute-start.3) | collective-permute-done | bytes 1572896 | tf_op jit(solution)/shard_map/ppermute | solution.py:136
  115.6 70.2 %share_all.1 = bf16[32,16,128]{2,1,0:T(8,128)(2,1)} custom-call(bf16[16,128]{1,0:T(8,128)(2,1)} %pad_bitcast_fusion.1.x_ref), custom_call_target="tpu_custom_call" | custom-call | tf_op jit(solution)/shard_map/share_all/pallas_call | solution.py:63
  225.0 13.7 fusion.25
  243.9 18.8 %sum_group.2 = f32[48,128]{1,0:T(8,128)} custom-call(f32[48,128]{1,0:T(8,128)} %reshape.415.x_ref), custom_call_target="tpu_custom_call" | custom-call | tf_op jit(solution)/shard_map/sum_group/pallas_call | solution.py:118
  281.5 34.8 %attention_forward.1 = (bf16[3072,256]{1,0:T(8,128)(2,1)S(1)}, f32[2,8,1,384]{3,2,1,0:T(1,128)S(1)}) custom-call(s32[8]{0:T(128)S(1)} %add_select_fusion.1.low_ref, s32[8,1,384]{2,1,0:T(1,128)S(1)} %bitcast.235, bf16[3072,256]{1,0:T(8,128)(2,1)S(1)} %pad_maximum_fusion.5.q_ref, bf16[3072,256]{1,0:T(8,128)(2,1)S(1)} %pad_maximum_fusion.6.k_ref, ...), custom_call_target="tpu_custom_call" | custom-call | flops 4831838208 | bytes 6291456 | tf_op jit(solution)/shard_map/attention_forward/pallas_call | solution.py:227
  318.3 37.4 %share_group.2 = s32[8,8,128]{2,1,0:T(8,128)} custom-call(s32[8,128]{1,0:T(8,128)} %pad_bitcast_fusion.x_ref), custom_call_target="tpu_custom_call" | custom-call | tf_op jit(solution)/shard_map/share_group/pallas_call | solution.py:118
  378.8 15.2 collective-permute-done.23
  402.1 25.5 %collective-permute-done.10 = bf16[3072,256]{1,0:T(8,128)(2,1)S(1)} collective-permute-done((bf16[3072,256]{1,0:T(8,128)(2,1)}, bf16[3072,256]{1,0:T(8,128)(2,1)S(1)}, u32[]{:S(2)}, u32[]{:S(2)}) %collective-permute-start.10) | collective-permute-done | bytes 1572896 | tf_op jit(solution)/shard_map/ppermute | solution.py:136
  485.4 20.0 %multiply_reduce_fusion = (f32[1536]{0:T(1024)S(1)}, f32[1536,2048]{1,0:T(8,128)S(1)}) fusion(bf16[8,192,2048]{2,1,0:T(8,128)(2,1)} %convolution_convert_fusion.7, bf16[1536,2048]{1,0:T(8,128)(2,1)} %bitcast.255, bf16[2048,2048]{1,0:T(8,128)(2,1)} %all-gather.5.cloned.1.call-done), kind=kOutput, calls=%fused_computation.22 | convolution fusion | flops 12897482752 | bytes 33560576 | tf_op jit(solution)/shard_map/dot_general | solution.py:363
  510.9 11.8 fusion.18
  538.1 17.2 %multiply_convert_fusion.1 = (bf16[1536,1024]{1,0:T(8,128)(2,1)}, bf16[1536,1024]{1,0:T(8,128)(2,1)S(1)}, bf16[1536,1024]{1,0:T(8,128)(2,1)S(1)}) fusion(f32[1536,1024]{1,0:T(8,128)} %fusion.18, f32[1536,1024]{1,0:T(8,128)} %fusion.14, bf16[1536,2048]{1,0:T(8,128)(2,1)} %bitcast.254, bf16[1,1024,2048]{2,1,0:T(8,128)(2,1)} %param.33), kind=kOutput, calls=%fused_computation.30 | convolution fusion | flops 6467616768 | bytes 32505856 | tf_op jit(solution)/shard_map/dot_general | solution.py:355
  564.6 13.0 add_convert_fusion
  595.3 12.6 fusion.9
  657.4 20.3 %collective-permute-done.26 = bf16[384,2048]{1,0:T(8,128)(2,1)S(1)} collective-permute-done((bf16[384,2048]{1,0:T(8,128)(2,1)}, bf16[384,2048]{1,0:T(8,128)(2,1)S(1)}, u32[]{:S(2)}, u32[]{:S(2)}) %collective-permute-start.26) | collective-permute-done | bytes 1572896 | tf_op jit(solution)/shard_map/ppermute | solution.py:136
  684.0 27.3 %collective-permute-done.15 = bf16[384,2048]{1,0:T(8,128)(2,1)S(1)} collective-permute-done((bf16[384,2048]{1,0:T(8,128)(2,1)}, bf16[384,2048]{1,0:T(8,128)(2,1)S(1)}, u32[]{:S(2)}, u32[]{:S(2)}) %collective-permute-start.15) | collective-permute-done | bytes 1572896 | tf_op jit(solution)/shard_map/ppermute | solution.py:136
  725.0 20.0 %collective-permute-done.27 = bf16[384,2048]{1,0:T(8,128)(2,1)S(1)} collective-permute-done((bf16[384,2048]{1,0:T(8,128)(2,1)S(1)}, bf16[384,2048]{1,0:T(8,128)(2,1)S(1)}, u32[]{:S(2)}, u32[]{:S(2)}) %collective-permute-start.27) | collective-permute-done | bytes 1572896 | tf_op jit(solution)/shard_map/ppermute | solution.py:136
  753.8 25.0 %collective-permute-done.16 = bf16[384,2048]{1,0:T(8,128)(2,1)} collective-permute-done((bf16[384,2048]{1,0:T(8,128)(2,1)}, bf16[384,2048]{1,0:T(8,128)(2,1)}, u32[]{:S(2)}, u32[]{:S(2)}) %collective-permute-start.16) | collective-permute-done | bytes 1572896 | tf_op jit(solution)/shard_map/ppermute | solution.py:136
  787.7 61.8 %share_group.3 = f32[8,24,128]{2,1,0:T(8,128)} custom-call(f32[24,128]{1,0:T(8,128)} %reshape.428.x_ref), custom_call_target="tpu_custom_call" | custom-call | tf_op jit(solution)/shard_map/share_group/pallas_call | solution.py:118
  885.1 23.2 %all-to-all-done.1 = bf16[8,384,256]{2,1,0:T(8,128)(2,1)S(1)} async-done(((bf16[8,384,256]{2,1,0:T(8,128)(2,1)}), bf16[8,384,256]{2,1,0:T(8,128)(2,1)S(1)}, u32[]{:S(2)}, u32[]{:S(2)}) %all-to-all-start.1) | async-done | bytes 1572896 | tf_op jit(solution)/shard_map/all_to_all | solution.py:567
  910.2 46.4 %attention_backward.1 = (f32[3072,256]{1,0:T(8,128)}, f32[3072,256]{1,0:T(8,128)}, f32[3072,256]{1,0:T(8,128)}) custom-call(s32[8]{0:T(128)S(1)} %add_select_fusion.high_ref, s32[8,1,384]{2,1,0:T(1,128)S(1)} %bitcast.236, bf16[3072,256]{1,0:T(8,128)(2,1)S(1)} %copy-done.3, bf16[3072,256]{1,0:T(8,128)(2,1)S(1)} %bitcast.234, bf16[3072,256]{1,0:T(8,128)(2,1)S(1)} %copy-done.5, ...), custom_call_target="tpu_custom_call" | custom-call | flops 12079595520 | bytes 15728640 | tf_op jit(solution)/shard_map/attention_backward/pallas_call | solution.py:307
  996.4 15.4 fusion.27
  1012.0 11.6 convert_bitcast_fusion.1
  1023.5 12.5 convolution_convert_fusion
  1064.0 35.0 %collective-permute-done.30 = bf16[384,2048]{1,0:T(8,128)(2,1)S(1)} collective-permute-done((bf16[384,2048]{1,0:T(8,128)(2,1)S(1)}, bf16[384,2048]{1,0:T(8,128)(2,1)S(1)}, u32[]{:S(2)}, u32[]{:S(2)}) %collective-permute-start.30) | collective-permute-done | bytes 1572896 | tf_op jit(solution)/shard_map/ppermute | solution.py:136
  1101.9 33.0 %collective-permute-done.31 = bf16[384,2048]{1,0:T(8,128)(2,1)S(1)} collective-permute-done((bf16[384,2048]{1,0:T(8,128)(2,1)S(1)}, bf16[384,2048]{1,0:T(8,128)(2,1)S(1)}, u32[]{:S(2)}, u32[]{:S(2)}) %collective-permute-start.31) | collective-permute-done | bytes 1572896 | tf_op jit(solution)/shard_map/ppermute | solution.py:136
  1139.3 31.0 %collective-permute-done.32 = bf16[384,2048]{1,0:T(8,128)(2,1)S(1)} collective-permute-done((bf16[384,2048]{1,0:T(8,128)(2,1)S(1)}, bf16[384,2048]{1,0:T(8,128)(2,1)S(1)}, u32[]{:S(2)}, u32[]{:S(2)}) %collective-permute-start.32) | collective-permute-done | bytes 1572896 | tf_op jit(solution)/shard_map/ppermute | solution.py:136
  1183.4 11.4 all-to-all-start.2
  1194.8 109.2 %all-reduce.5.cloned.1.call-done = (bf16[1,2048,1024]{2,1,0:T(8,128)(2,1)}, bf16[1,2048,1024]{2,1,0:T(8,128)(2,1)}, bf16[1,1024,2048]{2,1,0:T(8,128)(2,1)}) async-done(((bf16[1,2048,1024]{2,1,0:T(8,128)(2,1)}, bf16[1,2048,1024]{2,1,0:T(8,128)(2,1)}, bf16[1,1024,2048]{2,1,0:T(8,128)(2,1)}), (bf16[1,2048,1024]{2,1,0:T(8,128)(2,1)}, bf16[1,2048,1024]{2,1,0:T(8,128)(2,1)}, ...) | async-done | bytes 12582928 | tf_op jit(solution)/shard_map/psum | solution.py:547
  1327.5 96.8 %reduce-scatter.10.cloned.1.call-done = f32[64,12]{1,0:T(8,128)} async-done(((f32[2048,12]{1,0:T(8,128)}), f32[64,12]{1,0:T(8,128)}) %reduce-scatter.10.cloned.1.call-update) | async-done | bytes 3088
  1427.1 148.6 %reduce-scatter.8.cloned.1.call-done = bf16[64,2048]{1,0:T(8,128)(2,1)} async-done(((bf16[2048,2048]{1,0:T(8,128)(2,1)}), bf16[64,2048]{1,0:T(8,128)(2,1)}) %reduce-scatter.8.cloned.1.call-update) | async-done | bytes 262160 | tf_op jit(solution)/shard_map/reduce_scatter | solution.py:563
  (410 shorter events, 457.7 us)
Async XLA Ops:
  7.2 217.8 %all-gather.3.cloned.1.call-start = ((), (), s32[]{:S(2)}) async-start(), calls=%async_computation.6 | async-start | bytes 3932160 | tf_op jit(solution)/shard_map/all_gather | solution.py:441
  34.4 451.0 %all-gather.5.cloned.1.call-start = ((), (), s32[]{:S(2)}) async-start(), calls=%async_computation.7 | async-start | bytes 8650752 | tf_op jit(solution)/shard_map/all_gather | solution.py:442
  34.4 35.7 %collective-permute-start.1 = (bf16[384,2048]{1,0:T(8,128)(2,1)S(1)}, bf16[384,2048]{1,0:T(8,128)(2,1)}, u32[]{:S(2)}, u32[]{:S(2)}) collective-permute-start(bf16[384,2048]{1,0:T(8,128)(2,1)S(1)} %copy-done.18), channel_id=1, source_target_pairs={{0,2},{1,3},{2,4},{3,5},{4,6},{5,7},{6,0},{7,1},{8,10},{9,11},{10,... | collective-permute-start | bytes 4718600 | tf_op jit(solution)/shard_map/ppermute | solution.py:136
  70.1 40.5 %collective-permute-start.3 = (bf16[384,2048]{1,0:T(8,128)(2,1)}, bf16[384,2048]{1,0:T(8,128)(2,1)}, u32[]{:S(2)}, u32[]{:S(2)}) collective-permute-start(bf16[384,2048]{1,0:T(8,128)(2,1)} %collective-permute-done.1), channel_id=1, source_target_pairs={{0,2},{1,3},{2,4},{3,5},{4,6},{5,7},{6,0},{7,1},{8,10},{9,11},{10,... | collective-permute-start | bytes 4718600 | tf_op jit(solution)/shard_map/ppermute | solution.py:136
  72.9 127.1 %collective-permute-start = (bf16[384,2048]{1,0:T(8,128)(2,1)S(1)}, bf16[384,2048]{1,0:T(8,128)(2,1)}, u32[]{:S(2)}, u32[]{:S(2)}) collective-permute-start(bf16[384,2048]{1,0:T(8,128)(2,1)S(1)} %copy-done.18), channel_id=1, source_target_pairs={{0,1},{1,0},{2,3},{3,2},{4,5},{5,4},{6,7},{7,6},{8,9},{9,8},{10,11... | collective-permute-start | bytes 4718600 | tf_op jit(solution)/shard_map/ppermute | solution.py:131
  75.2 121.0 %collective-permute-start.19 = (bf16[384,2048]{1,0:T(8,128)(2,1)S(1)}, bf16[384,2048]{1,0:T(8,128)(2,1)}, u32[]{:S(2)}, u32[]{:S(2)}) collective-permute-start(bf16[384,2048]{1,0:T(8,128)(2,1)S(1)} %copy-done.26), channel_id=1, source_target_pairs={{0,2},{1,3},{2,4},{3,5},{4,6},{5,7},{6,0},{7,1},{8,10},{9,11},{10,... | collective-permute-start | bytes 4718600 | tf_op jit(solution)/shard_map/ppermute | solution.py:136
  110.6 88.7 %collective-permute-start.5 = (bf16[384,2048]{1,0:T(8,128)(2,1)}, bf16[384,2048]{1,0:T(8,128)(2,1)}, u32[]{:S(2)}, u32[]{:S(2)}) collective-permute-start(bf16[384,2048]{1,0:T(8,128)(2,1)} %collective-permute-done.3), channel_id=1, source_target_pairs={{0,2},{1,3},{2,4},{3,5},{4,6},{5,7},{6,0},{7,1},{8,10},{9,11},{10,... | collective-permute-start | bytes 4718600 | tf_op jit(solution)/shard_map/ppermute | solution.py:136
  196.1 161.8 %collective-permute-start.21 = (bf16[384,2048]{1,0:T(8,128)(2,1)}, bf16[384,2048]{1,0:T(8,128)(2,1)}, u32[]{:S(2)}, u32[]{:S(2)}) collective-permute-start(bf16[384,2048]{1,0:T(8,128)(2,1)} %collective-permute-done.19), channel_id=1, source_target_pairs={{0,2},{1,3},{2,4},{3,5},{4,6},{5,7},{6,0},{7,1},{8,10},{9,11},{10,... | collective-permute-start | bytes 4718600 | tf_op jit(solution)/shard_map/ppermute | solution.py:136
  316.3 51.0 %collective-permute-start.8 = (bf16[3072,256]{1,0:T(8,128)(2,1)S(1)}, bf16[3072,256]{1,0:T(8,128)(2,1)}, u32[]{:S(2)}, u32[]{:S(2)}) collective-permute-start(bf16[3072,256]{1,0:T(8,128)(2,1)S(1)} %get-tuple-element.43), channel_id=1, source_target_pairs={{0,2},{1,3},{2,4},{3,5},{4,6},{5,7},{6,0},{7,1},{8,10},{9,11},{10,... | collective-permute-start | bytes 4718600 | tf_op jit(solution)/shard_map/ppermute | solution.py:136
  317.4 50.3 %collective-permute-start.18 = (bf16[384,2048]{1,0:T(8,128)(2,1)S(1)}, bf16[384,2048]{1,0:T(8,128)(2,1)}, u32[]{:S(2)}, u32[]{:S(2)}) collective-permute-start(bf16[384,2048]{1,0:T(8,128)(2,1)S(1)} %copy-done.26), channel_id=1, source_target_pairs={{0,1},{1,0},{2,3},{3,2},{4,5},{5,4},{6,7},{7,6},{8,9},{9,8},{10,11... | collective-permute-start | bytes 4718600 | tf_op jit(solution)/shard_map/ppermute | solution.py:131
  357.9 38.1 %collective-permute-start.22 = (bf16[384,2048]{1,0:T(8,128)(2,1)}, bf16[384,2048]{1,0:T(8,128)(2,1)}, u32[]{:S(2)}, u32[]{:S(2)}) collective-permute-start(bf16[384,2048]{1,0:T(8,128)(2,1)} %collective-permute-done.21), channel_id=1, source_target_pairs={{0,1},{1,0},{2,3},{3,2},{4,5},{5,4},{6,7},{7,6},{8,9},{9,8},{10,11... | collective-permute-start | bytes 4718600 | tf_op jit(solution)/shard_map/ppermute | solution.py:131
  358.1 35.9 %collective-permute-start.23 = (bf16[384,2048]{1,0:T(8,128)(2,1)}, bf16[384,2048]{1,0:T(8,128)(2,1)}, u32[]{:S(2)}, u32[]{:S(2)}) collective-permute-start(bf16[384,2048]{1,0:T(8,128)(2,1)} %collective-permute-done.21), channel_id=1, source_target_pairs={{0,2},{1,3},{2,4},{3,5},{4,6},{5,7},{6,0},{7,1},{8,10},{9,11},{10,... | collective-permute-start | bytes 4718600 | tf_op jit(solution)/shard_map/ppermute | solution.py:136
  367.3 60.3 %collective-permute-start.10 = (bf16[3072,256]{1,0:T(8,128)(2,1)}, bf16[3072,256]{1,0:T(8,128)(2,1)S(1)}, u32[]{:S(2)}, u32[]{:S(2)}) collective-permute-start(bf16[3072,256]{1,0:T(8,128)(2,1)} %collective-permute-done.8), channel_id=1, source_target_pairs={{0,2},{1,3},{2,4},{3,5},{4,6},{5,7},{6,0},{7,1},{8,10},{9,11},{10,... | collective-permute-start | bytes 4718600 | tf_op jit(solution)/shard_map/ppermute | solution.py:136
  394.0 56.3 %collective-permute-start.24 = (bf16[384,2048]{1,0:T(8,128)(2,1)}, bf16[384,2048]{1,0:T(8,128)(2,1)}, u32[]{:S(2)}, u32[]{:S(2)}) collective-permute-start(bf16[384,2048]{1,0:T(8,128)(2,1)} %collective-permute-done.23), channel_id=1, source_target_pairs={{0,1},{1,0},{2,3},{3,2},{4,5},{5,4},{6,7},{7,6},{8,9},{9,8},{10,11... | collective-permute-start | bytes 4718600 | tf_op jit(solution)/shard_map/ppermute | solution.py:131
  398.8 54.3 %collective-permute-start.7 = (bf16[3072,256]{1,0:T(8,128)(2,1)S(1)}, bf16[3072,256]{1,0:T(8,128)(2,1)}, u32[]{:S(2)}, u32[]{:S(2)}) collective-permute-start(bf16[3072,256]{1,0:T(8,128)(2,1)S(1)} %get-tuple-element.43), channel_id=1, source_target_pairs={{0,1},{1,0},{2,3},{3,2},{4,5},{5,4},{6,7},{7,6},{8,9},{9,8},{10,11... | collective-permute-start | bytes 4718600 | tf_op jit(solution)/shard_map/ppermute | solution.py:131
  401.6 66.3 %collective-permute-start.9 = (bf16[3072,256]{1,0:T(8,128)(2,1)}, bf16[3072,256]{1,0:T(8,128)(2,1)S(1)}, u32[]{:S(2)}, u32[]{:S(2)}) collective-permute-start(bf16[3072,256]{1,0:T(8,128)(2,1)} %collective-permute-done.8), channel_id=1, source_target_pairs={{0,1},{1,0},{2,3},{3,2},{4,5},{5,4},{6,7},{7,6},{8,9},{9,8},{10,11... | collective-permute-start | bytes 4718600 | tf_op jit(solution)/shard_map/ppermute | solution.py:131
  427.6 35.3 %collective-permute-start.12 = (bf16[3072,256]{1,0:T(8,128)(2,1)S(1)}, bf16[3072,256]{1,0:T(8,128)(2,1)S(1)}, u32[]{:S(2)}, u32[]{:S(2)}) collective-permute-start(bf16[3072,256]{1,0:T(8,128)(2,1)S(1)} %collective-permute-done.10), channel_id=1, source_target_pairs={{0,2},{1,3},{2,4},{3,5},{4,6},{5,7},{6,0},{7,1},{8,10},{9,11},{10,... | collective-permute-start | bytes 4718600 | tf_op jit(solution)/shard_map/ppermute | solution.py:136
  639.5 38.2 %collective-permute-start.26 = (bf16[384,2048]{1,0:T(8,128)(2,1)}, bf16[384,2048]{1,0:T(8,128)(2,1)S(1)}, u32[]{:S(2)}, u32[]{:S(2)}) collective-permute-start(bf16[384,2048]{1,0:T(8,128)(2,1)} %dynamic-slice_bitcast_fusion.4), channel_id=1, source_target_pairs={{0,2},{1,3},{2,4},{3,5},{4,6},{5,7},{6,0},{7,1},{8,10},{9,11},{10,... | collective-permute-start | bytes 4718600 | tf_op jit(solution)/shard_map/ppermute | solution.py:136
  657.4 54.0 %collective-permute-start.15 = (bf16[384,2048]{1,0:T(8,128)(2,1)}, bf16[384,2048]{1,0:T(8,128)(2,1)S(1)}, u32[]{:S(2)}, u32[]{:S(2)}) collective-permute-start(bf16[384,2048]{1,0:T(8,128)(2,1)} %dynamic-slice_bitcast_fusion.5), channel_id=1, source_target_pairs={{0,2},{1,3},{2,4},{3,5},{4,6},{5,7},{6,0},{7,1},{8,10},{9,11},{10,... | collective-permute-start | bytes 4718600 | tf_op jit(solution)/shard_map/ppermute | solution.py:136
  679.7 65.3 %collective-permute-start.27 = (bf16[384,2048]{1,0:T(8,128)(2,1)S(1)}, bf16[384,2048]{1,0:T(8,128)(2,1)S(1)}, u32[]{:S(2)}, u32[]{:S(2)}) collective-permute-start(bf16[384,2048]{1,0:T(8,128)(2,1)S(1)} %fusion.40), channel_id=1, source_target_pairs={{0,2},{1,3},{2,4},{3,5},{4,6},{5,7},{6,0},{7,1},{8,10},{9,11},{10,... | collective-permute-start | bytes 4718600 | tf_op jit(solution)/shard_map/ppermute | solution.py:136
  714.6 64.2 %collective-permute-start.16 = (bf16[384,2048]{1,0:T(8,128)(2,1)}, bf16[384,2048]{1,0:T(8,128)(2,1)}, u32[]{:S(2)}, u32[]{:S(2)}) collective-permute-start(bf16[384,2048]{1,0:T(8,128)(2,1)} %fusion.44), channel_id=1, source_target_pairs={{0,2},{1,3},{2,4},{3,5},{4,6},{5,7},{6,0},{7,1},{8,10},{9,11},{10,... | collective-permute-start | bytes 4718600 | tf_op jit(solution)/shard_map/ppermute | solution.py:136
  748.2 104.8 %collective-permute-start.28 = (bf16[384,2048]{1,0:T(8,128)(2,1)}, bf16[384,2048]{1,0:T(8,128)(2,1)}, u32[]{:S(2)}, u32[]{:S(2)}) collective-permute-start(bf16[384,2048]{1,0:T(8,128)(2,1)} %fusion.39), channel_id=1, source_target_pairs={{0,2},{1,3},{2,4},{3,5},{4,6},{5,7},{6,0},{7,1},{8,10},{9,11},{10,... | collective-permute-start | bytes 4718600 | tf_op jit(solution)/shard_map/ppermute | solution.py:136
  782.5 73.9 %collective-permute-start.17 = (bf16[384,2048]{1,0:T(8,128)(2,1)}, bf16[384,2048]{1,0:T(8,128)(2,1)}, u32[]{:S(2)}, u32[]{:S(2)}) collective-permute-start(bf16[384,2048]{1,0:T(8,128)(2,1)} %fusion.43), channel_id=1, source_target_pairs={{0,2},{1,3},{2,4},{3,5},{4,6},{5,7},{6,0},{7,1},{8,10},{9,11},{10,... | collective-permute-start | bytes 4718600 | tf_op jit(solution)/shard_map/ppermute | solution.py:136
  866.3 42.1 %all-to-all-start.1 = ((bf16[8,384,256]{2,1,0:T(8,128)(2,1)}), bf16[8,384,256]{2,1,0:T(8,128)(2,1)S(1)}, u32[]{:S(2)}, u32[]{:S(2)}) async-start(bf16[8,384,256]{2,1,0:T(8,128)(2,1)} %bitcast.227), calls=%async_computation.1 | async-start | bytes 3145728 | tf_op jit(solution)/shard_map/all_to_all | solution.py:567
  873.2 310.2 %reduce-scatter.6.cloned.1.call-start = ((), (), s32[]{:S(2)}) async-start(), calls=%async_computation.8 | async-start | bytes 3932160 | tf_op jit(solution)/shard_map/reduce_scatter | solution.py:604
  1011.9 292.1 %all-reduce.5.cloned.1.call-start = ((), (), s32[]{:S(2)}) async-start(), calls=%async_computation.11 | async-start | bytes 25165824 | tf_op jit(solution)/shard_map/psum | solution.py:547
  1054.4 369.8 %reduce-scatter.10.cloned.1.call-start = ((), (), s32[]{:S(2)}) async-start(), calls=%async_computation.10 | async-start | bytes 1081344
  1062.9 36.1 %collective-permute-start.30 = (bf16[384,2048]{1,0:T(8,128)(2,1)S(1)}, bf16[384,2048]{1,0:T(8,128)(2,1)S(1)}, u32[]{:S(2)}, u32[]{:S(2)}) collective-permute-start(bf16[384,2048]{1,0:T(8,128)(2,1)S(1)} %dynamic-slice_bitcast_fusion.3), channel_id=1, source_target_pairs={{0,2},{1,3},{2,4},{3,5},{4,6},{5,7},{6,0},{7,1},{8,10},{9,11},{10,... | collective-permute-start | bytes 4718600 | tf_op jit(solution)/shard_map/ppermute | solution.py:136
  1099.6 35.3 %collective-permute-start.31 = (bf16[384,2048]{1,0:T(8,128)(2,1)S(1)}, bf16[384,2048]{1,0:T(8,128)(2,1)S(1)}, u32[]{:S(2)}, u32[]{:S(2)}) collective-permute-start(bf16[384,2048]{1,0:T(8,128)(2,1)S(1)} %fusion.37), channel_id=1, source_target_pairs={{0,2},{1,3},{2,4},{3,5},{4,6},{5,7},{6,0},{7,1},{8,10},{9,11},{10,... | collective-permute-start | bytes 4718600 | tf_op jit(solution)/shard_map/ppermute | solution.py:136
  1135.5 34.7 %collective-permute-start.32 = (bf16[384,2048]{1,0:T(8,128)(2,1)S(1)}, bf16[384,2048]{1,0:T(8,128)(2,1)S(1)}, u32[]{:S(2)}, u32[]{:S(2)}) collective-permute-start(bf16[384,2048]{1,0:T(8,128)(2,1)S(1)} %fusion.36), channel_id=1, source_target_pairs={{0,2},{1,3},{2,4},{3,5},{4,6},{5,7},{6,0},{7,1},{8,10},{9,11},{10,... | collective-permute-start | bytes 4718600 | tf_op jit(solution)/shard_map/ppermute | solution.py:136
  1173.0 402.7 %reduce-scatter.8.cloned.1.call-start = ((), (), s32[]{:S(2)}) async-start(), calls=%async_computation.9 | async-start | bytes 8650752 | tf_op jit(solution)/shard_map/reduce_scatter | solution.py:563
  1183.4 136.2 %all-to-all-start.2 = ((bf16[8,64,768]{2,1,0:T(8,128)(2,1)}), bf16[8,64,768]{2,1,0:T(8,128)(2,1)}, u32[]{:S(2)}, u32[]{:S(2)}) async-start(bf16[8,64,768]{2,1,0:T(8,128)(2,1)} %bitcast.261), calls=%async_computation.3 | async-start | bytes 1572864 | tf_op jit(solution)/shard_map/all_to_all | solution.py:605
  (94 other events, 2859.0 us)
Sparse Core Ops, SparseCore 0:
  34.5 44.7 all-gather.2
  82.2 172.8 all-gather.4
  1012.0 46.6 reduce-scatter.5
  1063.0 240.9 all-reduce.4
  1306.1 118.1 reduce-scatter.9
  1426.5 149.1 reduce-scatter.7

commit v2 on v1

v2 whole, which is shorter than its diff:
```python
import functools

import jax
import jax.numpy as jnp
from jax import lax
from jax.experimental import pallas as pl
from jax.experimental.pallas import tpu as pltpu
from jax.sharding import PartitionSpec as P

HEADS = 16
HEAD_DIM = 128
TOP = 2
EPS = 1e-05
NEG = -1e30
MESH = pl.DeviceIdType.MESH
BF = jnp.bfloat16
F32 = jnp.float32


def cost(microseconds):
    return pl.CostEstimate(
        flops=int(microseconds * 1e6), bytes_accessed=1 << 16, transcendentals=0
    )


def row_sums(x):
    ones = jnp.ones((8, x.shape[1]), BF)
    high = x.astype(BF)
    low = (x - high.astype(F32)).astype(BF)
    contract = (((1,), (1,)), ((), ()))
    return (
        lax.dot_general(ones, high, contract, preferred_element_type=F32)
        + lax.dot_general(ones, low, contract, preferred_element_type=F32)
    )[:1]


def exchange_small(collective_id, world=None, group=None, added=None):
    groups, ranks = lax.axis_size("group"), lax.axis_size("expert")
    total = groups * ranks
    near_blocks = [block for block in (group, added) if block is not None]
    count = len(near_blocks)

    def kernel(*refs):
        refs = list(refs)
        world_in = refs.pop(0) if world is not None else None
        near_in = [refs.pop(0) for _ in range(count)]
        world_out = refs.pop(0) if world is not None else None
        near_out = [refs.pop(0) for _ in range(count)]
        rank = lax.axis_index("expert")
        me = lax.axis_index("group") * ranks + rank
        barrier = pltpu.get_barrier_semaphore()

        def far(step):
            flat = lax.rem(me + step, total)
            return (flat // ranks, lax.rem(flat, ranks))

        def near(step):
            return {"expert": lax.rem(rank + step, ranks)}

        if world is not None:

            def greet(step, carry):
                pl.semaphore_signal(barrier, inc=1, device_id=far(step), device_id_type=MESH)
                return carry

            lax.fori_loop(1, total, greet, 0)
            pl.semaphore_wait(barrier, total - 1)
        else:
            for step in range(1, ranks):
                pl.semaphore_signal(barrier, inc=1, device_id=near(step), device_id_type=MESH)
            pl.semaphore_wait(barrier, ranks - 1)
        lands = list(near_out)
        if added is not None:
            lands[-1] = refs.pop(0)
        if count:
            near_send, near_recv = refs.pop(0), refs.pop(0)
        near_copies = []
        for which in range(count):
            for step in range(1, ranks):
                copy = pltpu.make_async_remote_copy(
                    src_ref=near_in[which],
                    dst_ref=lands[which].at[rank],
                    send_sem=near_send.at[which, step],
                    recv_sem=near_recv.at[which, step],
                    device_id=near(step),
                    device_id_type=MESH,
                )
                copy.start()
                near_copies.append(copy)
            lands[which][rank] = near_in[which][...]
        if world is not None:
            far_send, far_recv = refs.pop(0), refs.pop(0)

            def far_copy(step):
                return pltpu.make_async_remote_copy(
                    src_ref=world_in,
                    dst_ref=world_out.at[me],
                    send_sem=far_send.at[step],
                    recv_sem=far_recv.at[step],
                    device_id=far(step),
                    device_id_type=MESH,
                )

            def send(step, carry):
                far_copy(step).start()
                return carry

            lax.fori_loop(1, total, send, 0)
            world_out[me] = world_in[...]

            def settle(step, carry):
                far_copy(step).wait()
                return carry

            lax.fori_loop(1, total, settle, 0)
        for copy in near_copies:
            copy.wait()
        if added is not None:
            summed = lands[-1][0]
            for other in range(1, ranks):
                summed = summed + lands[-1][other]
            near_out[-1][...] = summed

    inputs, outputs, scratch = [], [], []
    if world is not None:
        inputs.append(world)
        outputs.append(jax.ShapeDtypeStruct((total,) + world.shape, world.dtype))
    if group is not None:
        inputs.append(group)
        outputs.append(jax.ShapeDtypeStruct((ranks,) + group.shape, group.dtype))
    if added is not None:
        inputs.append(added)
        outputs.append(jax.ShapeDtypeStruct(added.shape, added.dtype))
        scratch.append(pltpu.VMEM((ranks,) + added.shape, added.dtype))
    if count:
        scratch += [pltpu.SemaphoreType.DMA((count, ranks))] * 2
    if world is not None:
        scratch += [pltpu.SemaphoreType.DMA((total,)), pltpu.SemaphoreType.DMA((total,))]
    vmem = pl.BlockSpec(memory_space=pltpu.VMEM)
    return pl.pallas_call(
        kernel,
        out_shape=tuple(outputs),
        in_specs=[vmem] * len(inputs),
        out_specs=tuple([vmem] * len(outputs)),
        scratch_shapes=scratch,
        compiler_params=pltpu.CompilerParams(collective_id=collective_id, has_side_effects=True),
        name="exchange_small",
    )(*inputs)


def tie(*trees):
    leaves, shape = jax.tree.flatten(trees)
    return jax.tree.unflatten(shape, lax.optimization_barrier(leaves))


def partner_swap(block):
    ranks = lax.axis_size("expert")
    return lax.ppermute(block, "expert", [(i, i ^ 1) for i in range(ranks)])


def chip_shift(block, step=1):
    ranks = lax.axis_size("expert")
    return lax.ppermute(block, "expert", [(i, (i + 2 * step) % ranks) for i in range(ranks)])


def place_of():
    ranks = lax.axis_size("expert")
    me = lax.axis_index("expert")
    return ranks // 2, me // 2, me % 2


def source_chip(step):
    chips, chip, _ = place_of()
    return lax.rem(chip - step + chips, chips)


def assemble(pieces, axis):
    _, _, core = place_of()
    first = pieces[0][0]
    size = first.shape[axis]
    shape = list(first.shape)
    shape[axis] = size * 2 * len(pieces)
    whole = jnp.zeros(shape, first.dtype)
    for step, (mine, other) in enumerate(pieces):
        at = source_chip(step) * 2
        whole = lax.dynamic_update_slice_in_dim(whole, mine, (at + core) * size, axis)
        whole = lax.dynamic_update_slice_in_dim(whole, other, (at + 1 - core) * size, axis)
    return whole


def exchange_chips(blocks):
    chips, chip, core = place_of()
    pairs = blocks.reshape((chips, 2) + blocks.shape[1:])
    keep, give = [], []
    for step in range(chips):
        pair = lax.dynamic_index_in_dim(pairs, lax.rem(chip + step, chips), 0, keepdims=False)
        if step:
            pair = chip_shift(pair, step)
        keep.append(lax.dynamic_index_in_dim(pair, core, 0))
        give.append(lax.dynamic_index_in_dim(pair, 1 - core, 0))
    return keep, jnp.concatenate(give, axis=0)


def exchange_cores(keep, give):
    given = partner_swap(give)
    return assemble([(part, given[i : i + 1]) for i, part in enumerate(keep)], 0)


def rank_exchange(blocks):
    return exchange_cores(*exchange_chips(blocks))


def add3(arrived, mine, swapped):
    return (arrived.astype(F32) + mine.astype(F32) + swapped.astype(F32)).astype(BF)


def add2(mine, swapped):
    return (mine.astype(F32) + swapped.astype(F32)).astype(BF)


def attention_forward(queries, keys, values, starts, lowest):
    rows = queries.shape[0]
    heads = queries.shape[1] // HEAD_DIM
    blocks, _, block = starts.shape
    scale = HEAD_DIM ** (-0.5)

    def kernel(low_ref, start_ref, q_ref, k_ref, v_ref, o_ref, lse_ref):
        i = pl.program_id(1)
        q = q_ref[...]
        start = start_ref[0]
        q_index = i * block + lax.broadcasted_iota(jnp.int32, (1, block), 1)
        k_local = lax.broadcasted_iota(jnp.int32, (block, block), 0)

        def step(j, carry):
            top, total, acc = carry
            at = pl.multiple_of(j * block, block)
            k = k_ref[pl.ds(at, block), :]
            v = v_ref[pl.ds(at, block), :]
            s = (
                lax.dot_general(k, q, (((1,), (1,)), ((), ())), preferred_element_type=F32)
                * scale
            )
            k_index = k_local + j * block
            s = jnp.where((k_index <= q_index) & (k_index >= start), s, NEG)
            new_top = jnp.maximum(top, jnp.max(s, axis=0, keepdims=True))
            p = jnp.exp(s - new_top)
            shrink = jnp.exp(top - new_top)
            total = total * shrink + jnp.sum(p, axis=0, keepdims=True)
            acc = acc * shrink + lax.dot_general(
                v, p.astype(BF), (((0,), (0,)), ((), ())), preferred_element_type=F32
            )
            return (new_top, total, acc)

        top, total, acc = lax.fori_loop(
            low_ref[i],
            i + 1,
            step,
            (
                jnp.full((1, block), NEG, F32),
                jnp.zeros((1, block), F32),
                jnp.zeros((HEAD_DIM, block), F32),
            ),
        )
        o_ref[...] = (acc / total).T.astype(BF)
        lse_ref[0, 0] = top + jnp.log(total)

    return pl.pallas_call(
        kernel,
        out_shape=(
            jax.ShapeDtypeStruct((rows, heads * HEAD_DIM), BF),
            jax.ShapeDtypeStruct((heads, blocks, 1, block), F32),
        ),
        grid_spec=pltpu.PrefetchScalarGridSpec(
            num_scalar_prefetch=1,
            grid=(heads, blocks),
            in_specs=[
                pl.BlockSpec((1, 1, block), lambda h, i, low: (i, 0, 0)),
                pl.BlockSpec((block, HEAD_DIM), lambda h, i, low: (i, h)),
                pl.BlockSpec((rows, HEAD_DIM), lambda h, i, low: (0, h)),
                pl.BlockSpec((rows, HEAD_DIM), lambda h, i, low: (0, h)),
            ],
            out_specs=[
                pl.BlockSpec((block, HEAD_DIM), lambda h, i, low: (i, h)),
                pl.BlockSpec((1, 1, 1, block), lambda h, i, low: (h, i, 0, 0)),
            ],
        ),
        compiler_params=pltpu.CompilerParams(vmem_limit_bytes=48 << 20),
        cost_estimate=cost(35),
        name="attention_forward",
    )(lowest, starts, queries, keys, values)


def attention_backward(queries, keys, values, douts, lse, delta, starts, highest):
    rows = queries.shape[0]
    heads = queries.shape[1] // HEAD_DIM
    blocks, _, block = starts.shape
    scale = HEAD_DIM ** (-0.5)

    def kernel(
        high_ref,
        start_ref,
        q_ref,
        do_ref,
        k_ref,
        v_ref,
        lse_ref,
        delta_ref,
        dq_ref,
        dk_ref,
        dv_ref,
        q_sum_ref,
        k_sum_ref,
    ):
        j = pl.program_id(1)

        @pl.when(j == 0)
        def _():
            dq_ref[...] = jnp.zeros_like(dq_ref)

        k = k_ref[...]
        v = v_ref[...]
        k_index = j * block + lax.broadcasted_iota(jnp.int32, (block, block), 0)
        q_local = lax.broadcasted_iota(jnp.int32, (1, block), 1)

        def step(i, carry):
            dk, dv = carry
            at = pl.multiple_of(i * block, block)
            q = q_ref[pl.ds(at, block), :]
            do = do_ref[pl.ds(at, block), :]
            s = (
                lax.dot_general(k, q, (((1,), (1,)), ((), ())), preferred_element_type=F32)
                * scale
            )
            allowed = (k_index <= q_local + i * block) & (k_index >= start_ref[i])
            p = jnp.exp(jnp.where(allowed, s, NEG) - lse_ref[0, i])
            dv = dv + jnp.dot(p.astype(BF), do, preferred_element_type=F32)
            dp = lax.dot_general(v, do, (((1,), (1,)), ((), ())), preferred_element_type=F32)
            ds = (p * (dp - delta_ref[0, i])).astype(BF)
            dk = dk + jnp.dot(ds, q, preferred_element_type=F32)
            dq_ref[pl.ds(at, block), :] += (
                lax.dot_general(ds, k, (((0,), (0,)), ((), ())), preferred_element_type=F32)
                * scale
            )
            return (dk, dv)

        zero = jnp.zeros((block, HEAD_DIM), F32)
        dk, dv = lax.fori_loop(j, high_ref[j] + 1, step, (zero, zero))
        dk = dk * scale
        dk_ref[...] = dk
        dv_ref[...] = dv.astype(BF)
        k_sum_ref[0, 0] = row_sums(k.astype(F32) * dk)

        @pl.when(j == pl.num_programs(1) - 1)
        def _():
            for i in range(blocks):
                at = slice(i * block, (i + 1) * block)
                q_sum_ref[0, i] = row_sums(q_ref[at, :].astype(F32) * dq_ref[at, :])

    whole = pl.BlockSpec((rows, HEAD_DIM), lambda h, j, high: (0, h))
    part = pl.BlockSpec((block, HEAD_DIM), lambda h, j, high: (j, h))
    line = pl.BlockSpec((1, blocks, 1, block), lambda h, j, high: (h, 0, 0, 0))
    shape = jax.ShapeDtypeStruct((rows, heads * HEAD_DIM), F32)
    return pl.pallas_call(
        kernel,
        out_shape=(
            shape,
            shape,
            jax.ShapeDtypeStruct(shape.shape, BF),
            jax.ShapeDtypeStruct((heads, blocks, 1, block), F32),
            jax.ShapeDtypeStruct((heads, blocks, 1, block), F32),
        ),
        grid_spec=pltpu.PrefetchScalarGridSpec(
            num_scalar_prefetch=1,
            grid=(heads, blocks),
            in_specs=[
                pl.BlockSpec((blocks, 1, block), lambda h, j, high: (0, 0, 0)),
                whole,
                whole,
                part,
                part,
                line,
                line,
            ],
            out_specs=[
                whole,
                part,
                part,
                line,
                pl.BlockSpec((1, 1, 1, block), lambda h, j, high: (h, j, 0, 0)),
            ],
        ),
        compiler_params=pltpu.CompilerParams(vmem_limit_bytes=48 << 20),
        cost_estimate=cost(46),
        name="attention_backward",
    )(highest, starts, queries, douts, keys, values, lse, delta)


def gather_heads(tokens, pick, mine, other, source, core, out_weight, whole):
    ranks, capacity, rows = pick.shape
    columns = mine.shape[1]
    width = out_weight.shape[1]
    first = whole is None
    pair = 2 * capacity

    def kernel(at_ref, base_ref, pick_ref, mine_ref, other_ref, w_ref, out_ref, parts):
        core = at_ref[1]
        for half in range(2):
            at = half * capacity
            chosen = pick_ref[half]
            spots = slice(half * rows, (half + 1) * rows)
            if first:
                out_ref[at : at + capacity, :] = jnp.dot(
                    chosen, base_ref[spots, :], preferred_element_type=F32
                )
            for part_ref, which in ((mine_ref, core), (other_ref, 1 - core)):
                parts[
                    at : at + capacity, pl.ds(pl.multiple_of(which * columns, columns), columns)
                ] = jnp.dot(chosen, part_ref[spots, :], preferred_element_type=F32).astype(BF)
        base = out_ref if first else base_ref
        out_ref[...] = base[...] + jnp.dot(
            parts[...], w_ref[...], preferred_element_type=F32
        )

    heads_spec = pl.BlockSpec((2 * rows, columns), lambda r, at: (r, 0))
    total_spec = pl.BlockSpec((pair, width), lambda r, at: (r, 0))
    return pl.pallas_call(
        kernel,
        out_shape=jax.ShapeDtypeStruct((ranks * capacity, width), F32),
        grid_spec=pltpu.PrefetchScalarGridSpec(
            num_scalar_prefetch=1,
            grid=(ranks // 2,),
            in_specs=[
                pl.BlockSpec((2 * rows, width), lambda r, at: (r, 0)) if first else total_spec,
                pl.BlockSpec((2, capacity, rows), lambda r, at: (r, 0, 0)),
                heads_spec,
                heads_spec,
                pl.BlockSpec((2 * columns, width), lambda r, at: (at[0], 0)),
            ],
            out_specs=total_spec,
            scratch_shapes=[pltpu.VMEM((pair, 2 * columns), BF)],
        ),
        input_output_aliases={} if first else {1: 0},
        compiler_params=pltpu.CompilerParams(vmem_limit_bytes=40 << 20),
        cost_estimate=cost(8),
        name="gather_heads",
    )(
        jnp.stack([source, core]).astype(jnp.int32),
        tokens if first else whole,
        pick,
        mine,
        other,
        out_weight,
    )


def expert_forward(
    order, whole, pick, pick_t, mine, other, out_weight, mix_gain, router, hot, gate_w, up_w, down_w
):
    ranks, capacity, rows = pick.shape
    columns = mine.shape[1]
    width = out_weight.shape[1]
    hidden_width = gate_w.shape[1]
    chips = ranks // 2
    pair = 2 * capacity

    def kernel(
        order_ref,
        base_ref,
        pick_ref,
        turned_ref,
        mine_ref,
        other_ref,
        wo_ref,
        gain_ref,
        router_ref,
        hot_ref,
        wg_ref,
        wu_ref,
        wd_ref,
        mixed_ref,
        gates_ref,
        gate_ref,
        up_ref,
        hidden_ref,
        out_ref,
        own_ref,
        away_ref,
        scratch,
        parts,
    ):
        core = order_ref[2 * chips + 1]
        for half in range(2):
            at = half * capacity
            for part_ref, which in ((mine_ref, core), (other_ref, 1 - core)):
                parts[
                    at : at + capacity, pl.ds(pl.multiple_of(which * columns, columns), columns)
                ] = jnp.dot(
                    pick_ref[half],
                    part_ref[half * rows : (half + 1) * rows, :],
                    preferred_element_type=F32,
                ).astype(BF)
        total = base_ref[...] + jnp.dot(parts[...], wo_ref[...], preferred_element_type=F32)
        inverse = lax.rsqrt(jnp.mean(total * total, axis=1, keepdims=True) + EPS)
        mixed = (total * inverse * gain_ref[...]).astype(BF)
        mixed_ref[...] = mixed
        logits = lax.dot_general(
            mixed, router_ref[...], (((1,), (1,)), ((), ())), preferred_element_type=F32
        )
        lane = lax.broadcasted_iota(jnp.int32, logits.shape, 1)
        logits = jnp.where(lane < ranks, logits, NEG)
        shifted = jnp.exp(logits - jnp.max(logits, axis=1, keepdims=True))
        gates = jnp.sum(shifted * hot_ref[...], axis=1, keepdims=True) / jnp.sum(
            shifted, axis=1, keepdims=True
        )
        gates_ref[...] = jnp.broadcast_to(gates, gates_ref.shape)
        gate = jnp.dot(mixed, wg_ref[...], preferred_element_type=F32)
        gate_ref[...] = gate
        up = jnp.dot(mixed, wu_ref[...], preferred_element_type=F32)
        up_ref[...] = up
        hidden = (gate * jax.nn.sigmoid(gate) * up).astype(BF)
        hidden_ref[...] = hidden
        result = jnp.dot(hidden, wd_ref[...], preferred_element_type=F32).astype(BF)
        out_ref[...] = result
        scratch[...] = (gates * result.astype(F32)).astype(BF)
        for half, place_ref in ((core, own_ref), (1 - core, away_ref)):
            at = pl.ds(pl.multiple_of(half * capacity, capacity), capacity)
            place_ref[0] = jnp.dot(
                turned_ref[half], scratch[at, :], preferred_element_type=F32
            ).astype(BF)

    def chip_rows(n, m):
        return pl.BlockSpec((n, m), lambda i, order: (order[i], 0))

    def fixed(n, m):
        return pl.BlockSpec((n, m), lambda i, order: (0, 0), pipeline_mode=pl.Buffered(1))

    def slot(i, order):
        return (order[chips + i], 0, 0)

    all_slots = ranks * capacity
    return pl.pallas_call(
        kernel,
        out_shape=(
            jax.ShapeDtypeStruct((all_slots, width), BF),
            jax.ShapeDtypeStruct((all_slots, 128), F32),
            jax.ShapeDtypeStruct((all_slots, hidden_width), F32),
            jax.ShapeDtypeStruct((all_slots, hidden_width), F32),
            jax.ShapeDtypeStruct((all_slots, hidden_width), BF),
            jax.ShapeDtypeStruct((all_slots, width), BF),
            jax.ShapeDtypeStruct((chips, rows, width), BF),
            jax.ShapeDtypeStruct((chips, rows, width), BF),
        ),
        grid_spec=pltpu.PrefetchScalarGridSpec(
            num_scalar_prefetch=1,
            grid=(chips,),
            in_specs=[
                chip_rows(pair, width),
                pl.BlockSpec((2, capacity, rows), lambda i, order: (order[i], 0, 0)),
                pl.BlockSpec((2, rows, capacity), lambda i, order: (order[i], 0, 0)),
                chip_rows(2 * rows, columns),
                chip_rows(2 * rows, columns),
                pl.BlockSpec(
                    (2 * columns, width),
                    lambda i, order: (order[2 * chips], 0),
                    pipeline_mode=pl.Buffered(1),
                ),
                fixed(1, width),
                fixed(128, width),
                fixed(1, 128),
                fixed(width, hidden_width),
                fixed(width, hidden_width),
                fixed(hidden_width, width),
            ],
            out_specs=[
                chip_rows(pair, width),
                chip_rows(pair, 128),
                chip_rows(pair, hidden_width),
                chip_rows(pair, hidden_width),
                chip_rows(pair, hidden_width),
                chip_rows(pair, width),
                pl.BlockSpec((1, rows, width), slot),
                pl.BlockSpec((1, rows, width), slot),
            ],
            scratch_shapes=[pltpu.VMEM((pair, width), BF), pltpu.VMEM((pair, 2 * columns), BF)],
        ),
        compiler_params=pltpu.CompilerParams(vmem_limit_bytes=58 << 20),
        cost_estimate=cost(45),
        name="expert_forward",
    )(
        order.astype(jnp.int32),
        whole,
        pick,
        pick_t,
        mine,
        other,
        out_weight,
        mix_gain,
        router,
        hot,
        gate_w,
        up_w,
        down_w,
    )


def expert_backward(
    sources, core, rank, pick, pick_t, cotangents, gates, gate, up, hidden, result, weights, whole
):
    ranks, capacity, rows = pick.shape
    count = len(sources)
    width = cotangents[0][0].shape[1]
    hidden_width = weights[0].shape[1]
    pair = 2 * capacity
    wide = width + 128

    def kernel(at_ref, pick_ref, turned_ref, *refs):
        cots = refs[: 2 * count]
        gates_ref, gate_ref, up_ref, out_ref, wg_ref, wu_ref, wd_ref = refs[2 * count : 2 * count + 7]
        own_ref, away_ref, dcopy_ref, dgate_ref, dup_ref, rows_s, back_s, gates_s = refs[-8:]
        core, rank = at_ref[count], at_ref[count + 1]
        step = pl.program_id(0)

        for which in range(count):

            @pl.when(step == which)
            def _(which=which):
                for half, part_ref in ((core, cots[2 * which]), (1 - core, cots[2 * which + 1])):
                    at = pl.ds(pl.multiple_of(half * capacity, capacity), capacity)
                    rows_s[at, :] = jnp.dot(
                        pick_ref[half], part_ref[...], preferred_element_type=F32
                    )

        incoming = rows_s[...]
        dgates = jnp.sum(out_ref[...].astype(F32) * incoming, axis=1, keepdims=True)
        high = dgates.astype(BF)
        low = (dgates - high.astype(F32)).astype(BF)
        lane = lax.broadcasted_iota(jnp.int32, (pair, 128), 1)
        gates_s[...] = jnp.where(
            lane == rank,
            high.astype(F32),
            jnp.where(lane == rank + ranks, low.astype(F32), 0.0),
        ).astype(BF)
        dcopy = (gates_ref[:, :1] * incoming).astype(BF)
        dcopy_ref[...] = dcopy
        dhidden = lax.dot_general(
            dcopy, wd_ref[...], (((1,), (1,)), ((), ())), preferred_element_type=F32
        )
        gate, up = gate_ref[...], up_ref[...]
        sigma = jax.nn.sigmoid(gate)
        scaled = dhidden * sigma
        dgate = (scaled * up * (1.0 + gate * (1.0 - sigma))).astype(BF)
        dup = (scaled * gate).astype(BF)
        dgate_ref[...] = dgate
        dup_ref[...] = dup
        back_s[...] = (
            lax.dot_general(
                dgate, wg_ref[...], (((1,), (1,)), ((), ())), preferred_element_type=F32
            )
            + lax.dot_general(
                dup, wu_ref[...], (((1,), (1,)), ((), ())), preferred_element_type=F32
            )
        ).astype(BF)
        for half, place_ref in ((core, own_ref), (1 - core, away_ref)):
            at = pl.ds(pl.multiple_of(half * capacity, capacity), capacity)
            turned = turned_ref[half]
            place_ref[0, :, :width] = jnp.dot(
                turned, back_s[at, :], preferred_element_type=F32
            ).astype(BF)
            place_ref[0, :, width:] = jnp.dot(
                turned, gates_s[at, :], preferred_element_type=F32
            ).astype(BF)

    def chip_rows(n, m):
        return pl.BlockSpec((n, m), lambda i, at: (at[i], 0))

    def fixed(n, m):
        return pl.BlockSpec((n, m), lambda i, at: (0, 0), pipeline_mode=pl.Buffered(1))

    extra = [] if whole is None else list(whole)
    all_slots = ranks * capacity
    piece = pl.BlockSpec((1, rows, wide), lambda i, at: (i, 0, 0))
    return pl.pallas_call(
        kernel,
        out_shape=(
            jax.ShapeDtypeStruct((count, rows, wide), BF),
            jax.ShapeDtypeStruct((count, rows, wide), BF),
            jax.ShapeDtypeStruct((all_slots, width), BF),
            jax.ShapeDtypeStruct((all_slots, hidden_width), BF),
            jax.ShapeDtypeStruct((all_slots, hidden_width), BF),
        ),
        grid_spec=pltpu.PrefetchScalarGridSpec(
            num_scalar_prefetch=1,
            grid=(count,),
            in_specs=[
                pl.BlockSpec((2, capacity, rows), lambda i, at: (at[i], 0, 0)),
                pl.BlockSpec((2, rows, capacity), lambda i, at: (at[i], 0, 0)),
            ]
            + [fixed(rows, width)] * (2 * count)
            + [
                chip_rows(pair, 128),
                chip_rows(pair, hidden_width),
                chip_rows(pair, hidden_width),
                chip_rows(pair, width),
                fixed(width, hidden_width),
                fixed(width, hidden_width),
                fixed(hidden_width, width),
            ]
            + [pl.BlockSpec(memory_space=pl.ANY)] * len(extra),
            out_specs=[
                piece,
                piece,
                chip_rows(pair, width),
                chip_rows(pair, hidden_width),
                chip_rows(pair, hidden_width),
            ],
            scratch_shapes=[
                pltpu.VMEM((pair, width), F32),
                pltpu.VMEM((pair, width), BF),
                pltpu.VMEM((pair, 128), BF),
            ],
        ),
        input_output_aliases={10 + 2 * count + i: 2 + i for i in range(len(extra))},
        compiler_params=pltpu.CompilerParams(vmem_limit_bytes=60 << 20),
        cost_estimate=cost(12 * count),
        name="expert_backward",
    )(
        jnp.stack(list(sources) + [core, rank]).astype(jnp.int32),
        pick,
        pick_t,
        *[part for parts in cotangents for part in parts],
        gates,
        gate,
        up,
        result,
        *weights,
        *extra,
    )


def owner_backward(
    arrived, mine, swapped, share, router, middle, inverse, mix_gain, cotangent, out_weight
):
    rows, width = middle.shape
    ranks = lax.axis_size("expert")
    columns = width // ranks
    wide = arrived.shape[1]
    tile = rows // 2

    def kernel(
        arrived_ref,
        mine_ref,
        swapped_ref,
        share_ref,
        router_ref,
        middle_ref,
        inverse_ref,
        gain_ref,
        cot_ref,
        w_ref,
        dlogits_ref,
        norm_ref,
        dmiddle_ref,
        dprojected_ref,
        dattended_ref,
    ):
        @pl.when(pl.program_id(0) == 0)
        def _():
            norm_ref[...] = jnp.zeros_like(norm_ref)

        total = (
            arrived_ref[...].astype(F32)
            + mine_ref[...].astype(F32)
            + swapped_ref[...].astype(F32)
        )
        share = share_ref[...]
        dshare = total[:, width:]
        dshare = dshare + pltpu.roll(dshare, 128 - ranks, 1)
        dlogits = (
            share * (dshare - jnp.sum(share * dshare, axis=1, keepdims=True))
        ).astype(BF)
        dlogits_ref[...] = dlogits
        dmixed = total[:, :width] + jnp.dot(
            dlogits, router_ref[...], preferred_element_type=F32
        )
        inverse = inverse_ref[:, :1]
        scaled = middle_ref[...] * inverse
        weighted = dmixed * gain_ref[...]
        norm_ref[:1, :] += jnp.sum(dmixed * scaled, axis=0, keepdims=True)
        mean = jnp.mean(scaled * weighted, axis=1, keepdims=True)
        dmiddle = cot_ref[...].astype(F32) + inverse * (weighted - scaled * mean)
        dmiddle_ref[...] = dmiddle
        dprojected = dmiddle.astype(BF)
        dprojected_ref[...] = dprojected
        dattended = lax.dot_general(
            dprojected, w_ref[...], (((1,), (1,)), ((), ())), preferred_element_type=F32
        ).astype(BF)
        for rank in range(ranks):
            dattended_ref[rank] = dattended[:, rank * columns : (rank + 1) * columns]

    def rows_of(n):
        return pl.BlockSpec((tile, n), lambda i: (i, 0))

    def fixed(n, m):
        return pl.BlockSpec((n, m), lambda i: (0, 0))

    return pl.pallas_call(
        kernel,
        out_shape=(
            jax.ShapeDtypeStruct((rows, 128), BF),
            jax.ShapeDtypeStruct((8, width), F32),
            jax.ShapeDtypeStruct((rows, width), F32),
            jax.ShapeDtypeStruct((rows, width), BF),
            jax.ShapeDtypeStruct((ranks, rows, columns), BF),
        ),
        grid=(rows // tile,),
        in_specs=[
            rows_of(wide),
            rows_of(wide),
            rows_of(wide),
            rows_of(128),
            fixed(128, width),
            rows_of(width),
            rows_of(128),
            fixed(1, width),
            rows_of(width),
            fixed(width, width),
        ],
        out_specs=(
            rows_of(128),
            fixed(8, width),
            rows_of(width),
            rows_of(width),
            pl.BlockSpec((ranks, tile, columns), lambda i: (0, i, 0)),
        ),
        compiler_params=pltpu.CompilerParams(vmem_limit_bytes=48 << 20),
        cost_estimate=cost(14),
        name="owner_backward",
    )(
        arrived, mine, swapped, share, router, middle, inverse, mix_gain, cotangent, out_weight
    )


def project_in(mine, other, chip, core, weight, whole):
    rows, width = mine.shape
    columns = weight.shape[1] // 3
    ranks = lax.axis_size("expert")

    def kernel(at_ref, mine_ref, other_ref, w_ref, *refs):
        x_out, n_out, p_out, v_out, s_out = refs[-5:]
        core = at_ref[1]

        def handle(x_ref, half):
            at = pl.ds(pl.multiple_of(half * rows, rows), rows)
            x = x_ref[...]
            xf = x.astype(F32)
            n = (xf * lax.rsqrt(jnp.mean(xf * xf, axis=1, keepdims=True) + EPS)).astype(BF)
            x_out[at, :] = x
            n_out[at, :] = n
            product = jnp.dot(n, w_ref[...], preferred_element_type=F32)
            p_out[at, :] = product[:, : 2 * columns]
            v_out[at, :] = product[:, 2 * columns :].astype(BF)
            for which in range(2):
                part = product[:, which * columns : (which + 1) * columns]
                s_out[half, which : which + 1, :] = row_sums(part * part)

        handle(mine_ref, core)
        handle(other_ref, 1 - core)

    shapes = (
        jax.ShapeDtypeStruct((rows * ranks, width), BF),
        jax.ShapeDtypeStruct((rows * ranks, width), BF),
        jax.ShapeDtypeStruct((rows * ranks, 2 * columns), F32),
        jax.ShapeDtypeStruct((rows * ranks, columns), BF),
        jax.ShapeDtypeStruct((ranks, 2, rows), F32),
    )
    out_specs = [
        pl.BlockSpec((2 * rows, shape.shape[1]), lambda i, at: (at[0], 0)) for shape in shapes[:4]
    ] + [pl.BlockSpec((2, 2, rows), lambda i, at: (at[0], 0, 0))]
    extra = [] if whole is None else list(whole)
    full = pl.BlockSpec((rows, width), lambda i, at: (0, 0))
    return pl.pallas_call(
        kernel,
        out_shape=shapes,
        grid_spec=pltpu.PrefetchScalarGridSpec(
            num_scalar_prefetch=1,
            grid=(1,),
            in_specs=[full, full, pl.BlockSpec((width, 3 * columns), lambda i, at: (0, 0))]
            + [pl.BlockSpec(memory_space=pl.ANY)] * len(extra),
            out_specs=out_specs,
        ),
        input_output_aliases={4 + i: i for i in range(len(extra))},
        compiler_params=pltpu.CompilerParams(vmem_limit_bytes=48 << 20),
        cost_estimate=cost(8),
        name="project_in",
    )(jnp.stack([chip, core]).astype(jnp.int32), mine, other, weight, *extra)


def column_of(pair, function):
    pair = function(pair)
    return jnp.concatenate([pair, jnp.zeros((6, pair.shape[1]), F32)], axis=0).T


def make_heads(products, squares, gains, cosine, sine, width):
    rows = products.shape[0]
    columns = products.shape[1] // 2
    tile = squares.shape[2]

    def kernel(p_ref, s_ref, g_ref, c_ref, n_ref, q_ref, k_ref):
        cos, sin = c_ref[...], n_ref[...]
        inverses = column_of(s_ref[0], lambda total: lax.rsqrt(total / width + EPS))
        for which, out in ((0, q_ref), (1, k_ref)):
            inverse = inverses[:, which : which + 1]
            for h in range(0, columns, HEAD_DIM):
                x = p_ref[:, which * columns + h : which * columns + h + HEAD_DIM]
                x = x * inverse * g_ref[which : which + 1, h : h + HEAD_DIM]
                out[:, h : h + HEAD_DIM] = (
                    x * cos + pltpu.roll(x, HEAD_DIM // 2, 1) * sin
                ).astype(BF)

    def rows_of(n):
        return pl.BlockSpec((tile, n), lambda i: (i, 0))

    shape = jax.ShapeDtypeStruct((rows, columns), BF)
    return pl.pallas_call(
        kernel,
        out_shape=(shape, shape),
        grid=(rows // tile,),
        in_specs=[
            rows_of(2 * columns),
            pl.BlockSpec((1, 2, tile), lambda i: (i, 0, 0)),
            pl.BlockSpec((2, columns), lambda i: (0, 0)),
            rows_of(HEAD_DIM),
            rows_of(HEAD_DIM),
        ],
        out_specs=[rows_of(columns)] * 2,
        cost_estimate=cost(8),
        name="make_heads",
    )(products, squares, gains, cosine, sine)


def project_back(
    sources, core, products, squares, gains, cosine, sine, dq, dk, dv, means, weight, whole
):
    all_rows = products.shape[0]
    columns = products.shape[1] // 2
    rows = squares.shape[2]
    width = weight.shape[0]
    count = len(sources)

    def kernel(at_ref, p_ref, s_ref, m_ref, g_ref, c_ref, n_ref, dq_ref, dk_ref, dv_ref, w_ref, *refs):
        out_ref, own_ref, away_ref, gain_ref = refs[-4:]
        core = at_ref[count]

        @pl.when(pl.program_id(0) == 0)
        def _():
            gain_ref[...] = jnp.zeros_like(gain_ref)

        for half, place_ref in ((core, own_ref), (1 - core, away_ref)):
            at = pl.ds(pl.multiple_of(half * rows, rows), rows)
            cos, sin = c_ref[at, :], n_ref[at, :]
            inverses = column_of(s_ref[half], lambda total: lax.rsqrt(total / width + EPS))
            mean = column_of(m_ref[half], lambda total: total / width)
            for which, d_ref in ((0, dq_ref), (1, dk_ref)):
                inverse = inverses[:, which : which + 1]
                for h in range(0, columns, HEAD_DIM):
                    here = which * columns + h
                    scaled = p_ref[at, here : here + HEAD_DIM] * inverse
                    d = d_ref[at, h : h + HEAD_DIM]
                    d = d * cos - pltpu.roll(d, HEAD_DIM // 2, 1) * sin
                    weighted = d * g_ref[which : which + 1, h : h + HEAD_DIM]
                    gain_ref[which : which + 1, h : h + HEAD_DIM] += jnp.sum(
                        d * scaled, axis=0, keepdims=True
                    )
                    out_ref[at, here : here + HEAD_DIM] = (
                        inverse * (weighted - scaled * mean[:, which : which + 1])
                    ).astype(BF)
            out_ref[at, 2 * columns :] = dv_ref[at, :]
            place_ref[0] = lax.dot_general(
                out_ref[at, :], w_ref[...], (((1,), (1,)), ((), ())), preferred_element_type=F32
            ).astype(BF)

    def chip_rows(n):
        return pl.BlockSpec((2 * rows, n), lambda i, at: (at[i], 0))

    pair = pl.BlockSpec((2, 2, rows), lambda i, at: (at[i], 0, 0))
    piece = pl.BlockSpec((1, rows, width), lambda i, at: (i, 0, 0))
    extra = [] if whole is None else [whole]
    return pl.pallas_call(
        kernel,
        out_shape=(
            jax.ShapeDtypeStruct((all_rows, 3 * columns), BF),
            jax.ShapeDtypeStruct((count, rows, width), BF),
            jax.ShapeDtypeStruct((count, rows, width), BF),
            jax.ShapeDtypeStruct((8, columns), F32),
        ),
        grid_spec=pltpu.PrefetchScalarGridSpec(
            num_scalar_prefetch=1,
            grid=(count,),
            in_specs=[
                chip_rows(2 * columns),
                pair,
                pair,
                pl.BlockSpec((2, columns), lambda i, at: (0, 0)),
                chip_rows(HEAD_DIM),
                chip_rows(HEAD_DIM),
                chip_rows(columns),
                chip_rows(columns),
                chip_rows(columns),
                pl.BlockSpec((width, 3 * columns), lambda i, at: (0, 0)),
            ]
            + [pl.BlockSpec(memory_space=pl.ANY)] * len(extra),
            out_specs=[
                chip_rows(3 * columns),
                piece,
                piece,
                pl.BlockSpec((8, columns), lambda i, at: (0, 0)),
            ],
        ),
        input_output_aliases={11: 0} if extra else {},
        compiler_params=pltpu.CompilerParams(vmem_limit_bytes=48 << 20),
        cost_estimate=cost(8 * count),
        name="project_back",
    )(
        jnp.stack(list(sources) + [core]).astype(jnp.int32),
        products,
        squares,
        means,
        gains,
        cosine,
        sine,
        dq,
        dk,
        dv,
        weight,
        *extra,
    )


def norm_back(values, inverse, gain, grad):
    scaled = values * inverse
    weighted = grad * gain
    mean = jnp.mean(scaled * weighted, axis=-1, keepdims=True)
    return inverse * (weighted - scaled * mean), jnp.sum(grad * scaled, axis=0)


def dot_nt(a, b):
    return lax.dot_general(a, b, (((1,), (1,)), ((), ())), preferred_element_type=F32)


def dot_tn(a, b):
    return lax.dot_general(a, b, (((0,), (0,)), ((), ())), preferred_element_type=F32)


def dot_nn(a, b):
    return jnp.dot(a, b, preferred_element_type=F32)


def layout_of(lengths, seq_order, rows):
    length_row, order_row = lengths[0], seq_order[0]
    count = order_row.shape[0]
    chosen = (order_row[:, None] == jnp.arange(count, dtype=jnp.int32)[None, :]).astype(jnp.int32)
    placed = jnp.sum(chosen * length_row[None, :], axis=1)
    ends = jnp.sum(
        jnp.where(jnp.arange(count)[None, :] <= jnp.arange(count)[:, None], placed[None, :], 0),
        axis=1,
    )
    index = jnp.arange(rows, dtype=jnp.int32)
    passed = (index[:, None] >= ends[None, :]).astype(jnp.int32)
    begin = jnp.sum(passed * placed[None, :], axis=1)
    segment = jnp.sum(passed, axis=1)
    inside = (segment[:, None] == jnp.arange(count, dtype=jnp.int32)[None, :]).astype(jnp.int32)
    final = jnp.sum(inside * ends[None, :], axis=1) - 1
    return index, begin, final


def body(
    tokens,
    query_weight,
    key_weight,
    value_weight,
    output_weight,
    router_weight,
    attnorm,
    querynorm,
    keynorm,
    mixnorm,
    gate_weight,
    up_weight,
    down_weight,
    routes,
    lengths,
    seq_order,
    cotangent,
):
    rows, width = tokens.shape
    ranks = lax.axis_size("expert")
    groups = lax.axis_size("group")
    me = lax.axis_index("expert")
    chips, _, core = place_of()
    all_rows = rows * ranks
    capacity = 2 * rows * TOP // ranks
    columns = width // ranks
    shard = query_weight.shape[0]
    experts = router_weight.shape[1]
    block = rows
    blocks = all_rows // block
    heads = columns // HEAD_DIM

    own_gain = attnorm.astype(F32)[:, None]
    stacked = jnp.concatenate(
        [
            (part.astype(F32) * own_gain)
            .astype(BF)
            .reshape(shard, ranks, columns)
            .transpose(1, 0, 2)
            for part in (query_weight, key_weight, value_weight)
        ],
        axis=2,
    )
    tok, tok_other = [tokens, chip_shift(tokens)], [partner_swap(tokens)]
    stacked = rank_exchange(stacked)
    in_weight = lax.all_gather(
        stacked.reshape(ranks * shard, 3 * columns), "group", axis=0, tiled=True
    )

    small = jnp.concatenate(
        [querynorm, keynorm, mixnorm, router_weight.T.reshape(-1)], axis=0
    )
    packed = jnp.zeros((2048,), BF).at[: small.shape[0]].set(small).reshape(16, 128)
    packed_routes = (
        jnp.zeros((1024,), jnp.int32)
        .at[: rows * TOP]
        .set(routes.T.reshape(-1))
        .reshape(8, 128)
    )
    packed, packed_routes, _ = tie(packed, packed_routes, stacked)
    everyone, all_routes = exchange_small(1, world=packed, group=packed_routes)
    everyone = everyone.reshape(groups * ranks, 2048)
    query_gain = everyone[:, :shard].reshape(width).astype(F32)
    key_gain = everyone[:, shard : 2 * shard].reshape(width).astype(F32)
    mix_gain = everyone[:, 2 * shard : 3 * shard].reshape(1, width).astype(F32)
    router = jnp.pad(
        everyone[:, 3 * shard : (3 + experts) * shard]
        .reshape(groups * ranks, experts, shard)
        .transpose(1, 0, 2)
        .reshape(experts, width),
        ((0, 128 - experts), (0, 0)),
    )
    my_gains = jnp.stack(
        [
            lax.dynamic_slice_in_dim(query_gain, me * columns, columns),
            lax.dynamic_slice_in_dim(key_gain, me * columns, columns),
        ]
    )

    index, begin, final = layout_of(lengths, seq_order, all_rows)
    starts = begin.reshape(blocks, 1, block)
    lowest = begin.reshape(blocks, block)[:, 0] // block
    highest = final.reshape(blocks, block)[:, block - 1] // block
    position = (index - begin).astype(F32)
    frequency = 10000.0 ** (-(jnp.arange(HEAD_DIM // 2, dtype=F32) * 2.0 / HEAD_DIM))
    angles = position[:, None] * frequency[None, :]
    cosine, sine = jnp.cos(angles), jnp.sin(angles)
    cosine = jnp.concatenate([cosine, cosine], axis=1)
    sine = jnp.concatenate([-sine, sine], axis=1)

    all_routes = all_routes.reshape(ranks, -1)[:, : rows * TOP].reshape(ranks, TOP, rows)
    named = jnp.any(all_routes == me, axis=1)
    counted = jnp.cumsum(named.astype(jnp.int32), axis=1) - 1
    slot_of = jnp.where(named, counted, -1)
    slots = jnp.arange(capacity, dtype=jnp.int32)
    pick = (slot_of[:, None, :] == slots[None, :, None]).astype(BF)
    pick_t = (slot_of[:, :, None] == slots[None, None, :]).astype(BF)

    tables = (my_gains, mix_gain, router, starts, lowest, highest, cosine, sine, pick, pick_t)
    state, ready = None, 0
    for step in range(1, chips):
        tok, tok_other, state, tables = tie(tok, tok_other, state, tables)
        tok_other.append(partner_swap(tok[step]))
        if step + 1 < chips:
            tok.append(chip_shift(tok[step]))
        while ready <= step:
            state = project_in(
                tok[ready], tok_other[ready], source_chip(ready), core, in_weight, state
            )
            ready += 1
    my_gains, mix_gain, router, starts, lowest, highest, cosine, sine, pick, pick_t = tables
    output_weight_, _ = tie(output_weight, tok)
    full_output = lax.all_gather(output_weight_, ("group", "expert"), axis=0, tiled=True)
    all_tokens, normed, products, values, squares = state
    (squares,) = exchange_small(2, added=squares)
    queries, keys = make_heads(products, squares, my_gains, cosine, sine, width)

    cotangent_, _ = tie(cotangent, squares)
    cot = [cotangent_, chip_shift(cotangent_)]
    attended_mine, lse = attention_forward(queries, keys, values, starts, lowest)
    att = [attended_mine]
    att, cot = tie(att, cot)
    att_other = [partner_swap(att[0])]
    att.append(chip_shift(att[0]))
    att, att_other = tie(att, att_other)
    middle_e, ready = None, 0
    for step in range(1, chips):
        att_other.append(partner_swap(att[step]))
        if step + 1 < chips:
            att.append(chip_shift(att[step]))
            while ready < step or (ready == step and step + 2 == chips):
                middle_e = gather_heads(
                    all_tokens,
                    pick,
                    att[ready],
                    att_other[ready],
                    source_chip(ready),
                    core,
                    full_output,
                    middle_e,
                )
                ready += 1
            att, att_other, middle_e = tie(att, att_other, middle_e)

    cot, middle_e = tie(cot, middle_e)
    cot_other = [partner_swap(cot[0]), partner_swap(cot[1])]
    cot, _ = tie(cot, att)
    cot += [chip_shift(cot[1])] + [chip_shift(cot[0], step) for step in range(3, chips)]
    order = [source_chip(step % chips) for step in range(1, chips + 1)]
    order += [jnp.int32(step % chips) for step in range(1, chips + 1)]
    order += [source_chip(chips - 1), core]
    hot = (jnp.arange(128, dtype=jnp.int32) == me).astype(F32)[None]
    weights = (gate_weight[0], up_weight[0], down_weight[0])
    mixed_e, gates_e, gate_pre, up_pre, hidden, expert_out, out_own, out_away = expert_forward(
        jnp.stack(order),
        middle_e,
        pick,
        pick_t,
        att[-1],
        att_other[-1],
        full_output,
        mix_gain,
        router,
        hot,
        *weights,
    )
    forward = (gates_e, gate_pre, up_pre, hidden, expert_out)

    own_1, away_1, *saved = expert_backward(
        [source_chip(1)],
        core,
        me,
        pick,
        pick_t,
        [(cot[1], cot_other[1])],
        *forward,
        weights,
        None,
    )
    cot, cot_other, own_1, away_1, saved = tie(cot, cot_other, own_1, away_1, saved)
    cot_other += [partner_swap(cot[step]) for step in range(2, chips)]
    dmixed_moving = add2(own_1[0], partner_swap(away_1[0]))
    cot_other, dmixed_moving, own_att_pieces = tie(
        cot_other, dmixed_moving, (att, att_other)
    )
    dmixed_moving = chip_shift(dmixed_moving)
    rest = list(range(2, chips)) + [0]
    own, away, *saved = expert_backward(
        [source_chip(step) for step in rest],
        core,
        me,
        pick,
        pick_t,
        [(cot[step], cot_other[step]) for step in rest],
        *forward,
        weights,
        saved,
    )
    dmixed_moving, own, away, saved, out_away = tie(dmixed_moving, own, away, saved, out_away)
    swapped = [partner_swap(away[i]) for i in range(chips - 1)]
    out_first = partner_swap(out_away[1])
    dmixed_moving = add3(dmixed_moving, own[0], swapped[0])
    dmixed_moving, saved = tie(dmixed_moving, saved)
    dmixed_moving = chip_shift(dmixed_moving)
    dcopy, dgate_pre, dup_pre = saved
    sums = [
        dot_tn(hidden, dcopy).astype(BF),
        dot_tn(mixed_e, dgate_pre).astype(BF),
        dot_tn(mixed_e, dup_pre).astype(BF),
    ]
    dmixed_moving, sums = tie(dmixed_moving, sums)
    down_sum, gate_sum, up_sum = (lax.psum(term, "group") for term in sums)
    for step in range(3, chips):
        dmixed_moving = add3(dmixed_moving, own[step - 2], swapped[step - 2])
        dmixed_moving, att_pieces = tie(dmixed_moving, own_att_pieces)
        dmixed_moving = chip_shift(dmixed_moving)

    own_attended = jnp.zeros((rows, width), BF)
    for step in range(chips):
        at = source_chip(step) * 2
        for pieces, rank in ((att_pieces[0], at + core), (att_pieces[1], at + 1 - core)):
            piece = lax.dynamic_slice_in_dim(pieces[step], me * rows, rows, 0)
            own_attended = lax.dynamic_update_slice(own_attended, piece, (0, rank * columns))
    middle = tokens.astype(F32) + dot_nn(own_attended, full_output)
    middle_inverse = lax.rsqrt(jnp.mean(middle * middle, axis=-1, keepdims=True) + EPS)
    mixed = (middle * middle_inverse * mix_gain).astype(BF)
    logits = dot_nt(mixed, router)
    logits = jnp.where(jnp.arange(128, dtype=jnp.int32)[None] < experts, logits, NEG)
    shifted = jnp.exp(logits - jnp.max(logits, axis=1, keepdims=True))
    share = shifted / jnp.sum(shifted, axis=1, keepdims=True)
    middle_inverse = jnp.broadcast_to(middle_inverse, (rows, 128))
    halves = own_attended.reshape(rows, groups * chips, 2, shard)
    att_mine = lax.dynamic_index_in_dim(halves, core, 2, keepdims=False).reshape(rows, -1)
    att_away = lax.dynamic_index_in_dim(halves, 1 - core, 2, keepdims=False).reshape(rows, -1)
    out_moving = add2(out_own[1], out_first)
    dmixed_moving, middle, middle_inverse, mixed, share, att_mine, att_away, out_moving = tie(
        dmixed_moving, middle, middle_inverse, mixed, share, att_mine, att_away, out_moving
    )
    out_moving = chip_shift(out_moving)
    dlogits, mixnorm_term, dmiddle, dprojected, dattended_own = owner_backward(
        dmixed_moving,
        own[chips - 2],
        swapped[chips - 2],
        share,
        router,
        middle,
        middle_inverse,
        mix_gain,
        cotangent,
        full_output,
    )

    pairs = dattended_own.reshape(chips, 2, rows, columns)
    _, chip, _ = place_of()
    parts = [
        lax.dynamic_index_in_dim(pairs, lax.rem(chip + step, chips), 0, keepdims=False)
        for step in range(chips)
    ]
    parts, dprojected = tie(parts, dprojected)
    parts = parts[:1] + [chip_shift(parts[step], step) for step in range(1, chips)]
    output_mine = dot_tn(att_mine, dprojected).astype(BF)
    output_away = dot_tn(att_away, dprojected).astype(BF)
    parts, output_mine, output_away, out_moving = tie(parts, output_mine, output_away, out_moving)
    kept = [lax.dynamic_index_in_dim(part, core, 0) for part in parts]
    given = [lax.dynamic_index_in_dim(part, 1 - core, 0) for part in parts]
    dattended = exchange_cores(kept, jnp.concatenate(given, axis=0)).reshape(all_rows, columns)
    out_second = partner_swap(out_away[2])
    delta = jnp.stack(
        [
            jnp.sum(
                dattended[:, h * HEAD_DIM : (h + 1) * HEAD_DIM].astype(F32)
                * attended_mine[:, h * HEAD_DIM : (h + 1) * HEAD_DIM].astype(F32),
                axis=1,
            )
            for h in range(heads)
        ]
    ).reshape(heads, blocks, 1, block)
    out_moving = add3(out_moving, out_own[2], out_second)

    out_moving, dattended, delta, output_mine, output_away = tie(
        out_moving, dattended, delta, output_mine, output_away
    )
    out_moving = chip_shift(out_moving)
    out_swapped = [partner_swap(out_away[step]) for step in (3, 0)]
    output_pair = add2(output_mine, partner_swap(output_away))
    dquery, dkey, dvalue, query_part, key_part = attention_backward(
        queries, keys, values, dattended, lse, delta, starts, highest
    )
    out_moving, out_swapped, output_pair, dquery, dkey, dvalue, query_part, key_part = tie(
        out_moving, out_swapped, output_pair, dquery, dkey, dvalue, query_part, key_part
    )
    partials = jnp.stack(
        [jnp.sum(query_part[:, :, 0], axis=0), jnp.sum(key_part[:, :, 0], axis=0)], axis=1
    )
    (means,) = exchange_small(3, added=partials)
    out_moving = add3(out_moving, out_own[3], out_swapped[0])
    out_moving, means = tie(out_moving, means)
    out_moving = chip_shift(out_moving)
    back = (products, squares, my_gains, cosine, sine, dquery, dkey, dvalue)
    dpre, dn_own_1, dn_away_1, gains_1 = project_back(
        [source_chip(1)], core, *back, means, in_weight, None
    )
    dnormed_moving = add2(dn_own_1[0], partner_swap(dn_away_1[0]))
    dnormed_moving, dpre, down_sum, gate_sum, up_sum = tie(
        dnormed_moving, dpre, down_sum, gate_sum, up_sum
    )
    dnormed_moving = chip_shift(dnormed_moving)
    output_pair, _ = tie(output_pair, down_sum)
    output_pair = lax.psum_scatter(
        output_pair, "group", scatter_dimension=0, tiled=True
    ).reshape(chips, shard, width)
    dpre, dn_own, dn_away, gains_2 = project_back(
        [source_chip(step) for step in rest], core, *back, means, in_weight, dpre
    )
    in_term = jnp.concatenate(
        [
            dot_tn(normed, dpre).astype(BF),
            dot_tn(mixed, dlogits).astype(BF)[:, :experts],
            mixnorm_term[0].astype(BF)[:, None],
            jnp.zeros((width, 128 - experts - 1), BF),
        ],
        axis=1,
    )
    dnormed_moving, dn_own, dn_away, in_term, out_moving = tie(
        dnormed_moving, dn_own, dn_away, in_term, out_moving
    )
    in_sum = lax.psum_scatter(in_term, "group", scatter_dimension=0, tiled=True)
    dn_swapped = [partner_swap(dn_away[i]) for i in range(chips - 1)]
    dnormed_moving = add3(dnormed_moving, dn_own[0], dn_swapped[0])
    gain_terms = gains_1 + gains_2
    dnormed_moving, gain_terms, out_moving, down_sum, gate_sum, up_sum = tie(
        dnormed_moving, gain_terms, out_moving, down_sum, gate_sum, up_sum
    )
    dnormed_moving = chip_shift(dnormed_moving)
    layer_result = (
        middle
        + out_moving.astype(F32)
        + out_own[0].astype(F32)
        + out_swapped[1].astype(F32)
    ).astype(BF)
    down_sum, gate_sum, up_sum = (
        term.astype(F32)[None] for term in (down_sum, gate_sum, up_sum)
    )
    (gain_shares,) = exchange_small(4, world=gain_terms)
    dnormed_moving, dn_swapped, down_sum, gate_sum, up_sum, gain_shares, layer_result = tie(
        dnormed_moving, dn_swapped, down_sum, gate_sum, up_sum, gain_shares, layer_result
    )
    dnormed_moving = add3(dnormed_moving, dn_own[1], dn_swapped[1])
    dnormed_moving, output_pair = tie(dnormed_moving, output_pair)
    dnormed_moving = chip_shift(dnormed_moving)

    def to_chip(step):
        part = lax.dynamic_index_in_dim(
            output_pair, source_chip(chips - step), 0, keepdims=False
        )
        return chip_shift(part, step)

    output_parts = [to_chip(step) for step in range(1, chips)]
    kept, given = exchange_chips(in_sum.reshape(ranks, shard, 3 * columns + 128))
    output_sum = sum(
        [part.astype(F32) for part in output_parts],
        lax.dynamic_index_in_dim(output_pair, source_chip(0), 0, keepdims=False).astype(F32),
    )
    kept, given, dnormed_moving, output_sum = tie(kept, given, dnormed_moving, output_sum)
    in_sum = exchange_cores(kept, given)
    dnormed = (
        dnormed_moving.astype(F32)
        + dn_own[chips - 2].astype(F32)
        + dn_swapped[chips - 2].astype(F32)
    )

    norm_grads = jnp.sum(
        gain_shares.reshape(groups, ranks, 8, columns)[:, :, :2], axis=0
    )
    norm_grads = norm_grads.transpose(1, 0, 2).reshape(2, width)
    flat = lax.axis_index("group") * ranks + me
    norm_grads = lax.dynamic_slice_in_dim(norm_grads, flat * shard, shard, 1)
    raw = [
        in_sum[:, :, i * columns : (i + 1) * columns]
        .transpose(1, 0, 2)
        .reshape(shard, width)
        .astype(F32)
        for i in range(3)
    ]
    others = jnp.sum(in_sum[:, :, 3 * columns :].astype(F32), axis=0)
    attnorm_grad = sum(
        jnp.sum(grad * weight.astype(F32), axis=1)
        for grad, weight in zip(raw, (query_weight, key_weight, value_weight))
    )
    query_sum, key_sum, value_sum = (grad * own_gain for grad in raw)
    own_f = tokens.astype(F32)
    own_inverse = lax.rsqrt(jnp.mean(own_f * own_f, axis=-1, keepdims=True) + EPS)
    scaled = own_f * own_inverse
    dinput = own_inverse * (dnormed - scaled * jnp.mean(scaled * dnormed, axis=-1, keepdims=True))
    tokens_grad = (dmiddle + dinput).astype(BF)
    return (
        layer_result,
        tokens_grad,
        query_sum,
        key_sum,
        value_sum,
        output_sum,
        others[:, :experts],
        attnorm_grad,
        norm_grads[0],
        norm_grads[1],
        others[:, experts],
        gate_sum,
        up_sum,
        down_sum,
    )


def solution(mesh):
    rows = P(("group", "expert"), None)
    line = P(("group", "expert"))
    expert = P("expert", None, None)
    group = P("group", None)
    return jax.shard_map(
        body,
        mesh=mesh,
        in_specs=(
            (rows,) * 6 + (line,) * 4 + (expert,) * 3 + (rows, group, group, rows)
        ),
        out_specs=(rows,) * 7 + (line,) * 4 + (expert,) * 3,
        check_vma=False,
    )
```

time: 1610 us -> 1110 us (0.69)
  waiting for transfers between devices: 686 us -> 382 us
  matrix products: 243 us -> 58.9 us
  Pallas kernels: 279 us -> 385 us
  local copies, waits for them, and re-layouts: 127 us -> 75.8 us
  other arithmetic: 135 us -> 103 us
  blocking collectives: 23.6 us -> 0 us
    reduce_scatter x1, waiting for transfers between devices: 149 us -> 0.01 us  [body(): lax.psum_scatter(output_pair, 'group', scatter_dimension=0, tiled=True)]
    pallas_call x6 -> x19, Pallas kernels: 244 us -> 349 us  [the longest x4 72.8 us: exchange_small(): pl.pallas_call(kernel, out_shape=tuple(outputs), in_specs=[vmem] * len(in...]
    unnamed x7 -> x5, waiting for transfers between devices: 96.9 us -> 0.08 us
    psum x1, waiting for transfers between devices: 109 us -> 36.8 us  [body(): down_sum, gate_sum, up_sum = (lax.psum(term, 'group') for term in sums)]
    dot_general x7 -> x1, matrix products: 73.9 us -> 6.08 us  [dot_nn(): return jnp.dot(a, b, preferred_element_type=F32)]
    dot_general x7 -> x1, matrix products: 59 us -> 0.66 us  [dot_nt(): lax.dot_general(a, b, (((1,), (1,)), ((), ())), preferred_element_type=F32)]
    dot_general x5 -> x0, matrix products: 49.7 us -> none  [the longest x3 28 us: select(): jnp.einsum('rst,rtd->rsd', pick, array.reshape(ranks, rows, -1), preferre...]
    dynamic_update_slice x26 -> x31, local copies, waits for them, and re-layouts: 53.3 us -> 7.54 us  [the longest x11 4.53 us: assemble(): lax.dynamic_update_slice_in_dim(whole, mine, (at + core) * size, axis)]
  transfers between devices with their start and end apart: 41 -> 63, of which waited for: 16 -> 25; matrix products, arithmetic and copies ran while one was open for 21% -> 19% of each run, Pallas kernels for 14% -> 35%
where the time goes in v2:
time: 1110 us; the launch traced here: 1100 us
  Pallas kernels  385 us (35%)
  waiting for transfers between devices  382 us (34%)
  other arithmetic  103 us (9%)
  starting transfers between devices  79.4 us (7%)
  local copies, waits for them, and re-layouts  75.8 us (7%)
  matrix products  58.9 us (5%)
  between operations  15.6 us (1%)
    ppermute x30, waiting for transfers between devices, chip_shift(): lax.ppermute(block, 'expert', [(i, (i + 2 * step) % ranks) for i in range...  317 us
    pallas_call x4, Pallas kernels, exchange_small(): pl.pallas_call(kernel, out_shape=tuple(outputs), in_specs=[vmem] * len(in...  72.8 us
    ppermute x30, starting transfers between devices, chip_shift(): lax.ppermute(block, 'expert', [(i, (i + 2 * step) % ranks) for i in range...  54.6 us
    pallas_call x2, Pallas kernels, expert_backward(): pl.pallas_call(kernel, out_shape=(jax.ShapeDtypeStruct((count, rows, wide...  54 us
    pallas_call x1, Pallas kernels, attention_backward(): pl.pallas_call(kernel, out_shape=(shape, shape, jax.ShapeDtypeStruct(shap...  52.5 us
    dot_general x7, matrix products, dot_tn(): lax.dot_general(a, b, (((0,), (0,)), ((), ())), preferred_element_type=F32)  52.2 us
    pallas_call x1, Pallas kernels, expert_forward(): pl.pallas_call(kernel, out_shape=(jax.ShapeDtypeStruct((all_slots, width)...  46.1 us
    pallas_call x4, Pallas kernels, project_in(): pl.pallas_call(kernel, out_shape=shapes, grid_spec=pltpu.PrefetchScalarGr...  38.9 us
  transfers between devices with their start and end apart: 63, of which 25 were waited for; matrix products, arithmetic and copies ran while one was open for 19% of the time, Pallas kernels for 35%

profile of v2, /device:TPU:25, one launch (start us, length us, event | category | flops | bytes accessed | tf_op | source)
XLA Modules:
  0.0 1099.2 jit_solution(2803393827808785544)
XLA Ops:
  16.3 30.5 %collective-permute-done.4 = bf16[2,64,768]{2,1,0:T(8,128)(2,1)S(1)} collective-permute-done((bf16[2,64,768]{2,1,0:T(8,128)(2,1)S(1)}, bf16[2,64,768]{2,1,0:T(8,128)(2,1)S(1)}, u32[]{:S(2)}, u32[]{:S(2)}) %collective-permute-start.4) | collective-permute-done | bytes 196640 | tf_op jit(solution)/shard_map/ppermute | solution.py:163
  77.1 14.1 %exchange_small.4 = (bf16[32,16,128]{2,1,0:T(8,128)(2,1)}, s32[8,8,128]{2,1,0:T(8,128)}) custom-call(bf16[16,128]{1,0:T(8,128)(2,1)} %fusion.47.refs_0_, s32[8,128]{1,0:T(8,128)} %pad_bitcast_fusion.refs_1_), custom_call_target="tpu_custom_call" | custom-call | tf_op jit(solution)/shard_map/exchange_small/pallas_call | solution.py:140
  102.7 14.1 %all-gather.3.cloned.1.call-done.w_ref = bf16[2048,768]{1,0:T(8,128)(2,1)} async-done(((bf16[512,768]{1,0:T(8,128)(2,1)}), bf16[2048,768]{1,0:T(8,128)(2,1)}) %all-gather.3.cloned.1.call-update) | async-done | bytes 3145744 | tf_op jit(solution)/shard_map/all_gather | solution.py:1122
  128.8 10.2 project_in.5
  152.6 23.3 %collective-permute-done.8.mine_ref = bf16[384,2048]{1,0:T(8,128)(2,1)} collective-permute-done((bf16[384,2048]{1,0:T(8,128)(2,1)}, bf16[384,2048]{1,0:T(8,128)(2,1)}, u32[]{:S(2)}, u32[]{:S(2)}) %collective-permute-start.8) | collective-permute-done | bytes 1572896 | tf_op jit(solution)/shard_map/ppermute | solution.py:163
  190.7 11.7 %exchange_small.5.s_ref = f32[8,2,384]{2,1,0:T(2,128)} custom-call(f32[8,2,384]{2,1,0:T(2,128)} %copy-done.18), custom_call_target="tpu_custom_call" | custom-call | tf_op jit(solution)/shard_map/exchange_small/pallas_call | solution.py:140
  215.4 35.9 %attention_forward.1 = (bf16[3072,256]{1,0:T(8,128)(2,1)S(1)}, f32[2,8,1,384]{3,2,1,0:T(1,128)S(1)}) custom-call(s32[8]{0:T(128)S(1)} %add_select_fusion.1.low_ref, s32[8,1,384]{2,1,0:T(1,128)S(1)} %bitcast.209, bf16[3072,256]{1,0:T(8,128)(2,1)S(1)} %copy-done.8, bf16[3072,256]{1,0:T(8,128)(2,1)S(1)} %copy-done.10, bf16[3072,256]{1,0:T(8,128)(2,1)} %copy-done.2), custom_call_target="tpu_custom_call" | custom-call | flops 35000000 | bytes 65536 | tf_op jit(solution)/shard_map/attention_forward/pallas_call | solution.py:267
  251.3 20.3 %collective-permute-done.11.refs_0_ = bf16[384,2048]{1,0:T(8,128)(2,1)} collective-permute-done((bf16[384,2048]{1,0:T(8,128)(2,1)}, bf16[384,2048]{1,0:T(8,128)(2,1)}, u32[]{:S(2)}, u32[]{:S(2)}) %collective-permute-start.11) | collective-permute-done | bytes 1572896 | tf_op jit(solution)/shard_map/ppermute | solution.py:163
  273.5 32.4 %collective-permute-done.12.mine_ref = bf16[3072,256]{1,0:T(8,128)(2,1)} collective-permute-done((bf16[3072,256]{1,0:T(8,128)(2,1)S(1)}, bf16[3072,256]{1,0:T(8,128)(2,1)}, u32[]{:S(2)}, u32[]{:S(2)}) %collective-permute-start.12) | collective-permute-done | bytes 1572896 | tf_op jit(solution)/shard_map/ppermute | solution.py:163
  316.6 13.8 %gather_heads.3.base_ref = f32[1536,2048]{1,0:T(8,128)} custom-call(s32[2]{0:T(128)S(1)} %pad_add_fusion.2.at_ref, bf16[3072,2048]{1,0:T(8,128)(2,1)} %get-tuple-element.361.base_ref, bf16[8,192,384]{2,1,0:T(8,128)(2,1)S(1)} %fusion.27.pick_ref, bf16[3072,256]{1,0:T(8,128)(2,1)S(1)} %get-tuple-element.436.mine_ref, bf16[3072,256]{1,0:T(8,128)(2,1)S(1)} %copy-done.14, ...), custom_call_target="tpu_custom_call" | custom-call | flops 8000000 | bytes 65536 | tf_op jit(solution)/shard_map/gather_heads/pallas_call | solution.py:426
  330.4 10.3 collective-permute-done.14.mine_ref
  348.0 12.6 %gather_heads.4.base_ref = f32[1536,2048]{1,0:T(8,128)} custom-call(s32[2]{0:T(128)S(1)} %pad_add_fusion.at_ref, f32[1536,2048]{1,0:T(8,128)} %gather_heads.3.base_ref, bf16[8,192,384]{2,1,0:T(8,128)(2,1)S(1)} %fusion.27.pick_ref, bf16[3072,256]{1,0:T(8,128)(2,1)} %collective-permute-done.12.mine_ref, ...), custom_call_target="tpu_custom_call", output_to_operand_aliasing={{}: (1, {})} | custom-call | flops 8000000 | bytes 65536 | tf_op jit(solution)/shard_map/gather_heads/pallas_call | solution.py:426
  360.7 12.4 %gather_heads.5.base_ref = f32[1536,2048]{1,0:T(8,128)} custom-call(s32[2]{0:T(128)S(1)} %pad_add_fusion.3.at_ref, f32[1536,2048]{1,0:T(8,128)} %gather_heads.4.base_ref, bf16[8,192,384]{2,1,0:T(8,128)(2,1)S(1)} %fusion.27.pick_ref, bf16[3072,256]{1,0:T(8,128)(2,1)} %collective-permute-done.14.mine_ref, ...), custom_call_target="tpu_custom_call", output_to_operand_aliasing={{}: (1, {})} | custom-call | flops 8000000 | bytes 65536 | tf_op jit(solution)/shard_map/gather_heads/pallas_call | solution.py:426
  390.9 46.1 %expert_forward.1 = (bf16[1536,2048]{1,0:T(8,128)(2,1)}, f32[1536,128]{1,0:T(8,128)}, f32[1536,1024]{1,0:T(8,128)}, f32[1536,1024]{1,0:T(8,128)}, bf16[1536,1024...) custom-call(s32[10]{0:T(128)} %stack.115.order_ref, ...), custom_call_target="tpu_custom_call" | custom-call | flops 45000000 | bytes 65536 | tf_op jit(solution)/shard_map/expert_forward/pallas_call | solution.py:541
  437.1 17.9 %expert_backward.2 = (bf16[1,384,2176]{2,1,0:T(8,128)(2,1)}, bf16[1,384,2176]{2,1,0:T(8,128)(2,1)}, bf16[1536,2048]{1,0:T(8,128)(2,1)}, bf16[1536,1024]{1,0:T(8,128)(2,1)}, bf16[1536,1024]{1,0:T(8,128)(2,1)}) custom-call(s32[3]{0:T(128)} %pad_add_fusion.4.at_ref, bf16[8,192,384]{2,1,0:T(8,128)(2,1)} %copy-done.1, bf16[8,384,192]{2,1,0:T(8,128)(2,1)} %fusion.26.turned_ref, ...), custom_call_target="tpu_custom_call" | custom-call | flops 12000000 | bytes 65536 | tf_op jit(solution)/shard_map/expert_backward/pallas_call | solution.py:682
  467.4 36.1 %expert_backward.3 = (bf16[3,384,2176]{2,1,0:T(8,128)(2,1)}, bf16[3,384,2176]{2,1,0:T(8,128)(2,1)}, bf16[1536,2048]{1,0:T(8,128)(2,1)}, bf16[1536,1024]{1,0:T(8,128)(2,1)}, bf16[1536,1024]{1,0:T(8,128)(2,1)}) custom-call(s32[5]{0:T(128)} %stack.116.at_ref, ...), custom_call_target="tpu_custom_call", output_to_operand_aliasing={{2}: (16, {}), {3}: (17, {}), {4}: (18, {})} | custom-call | flops 36000000 | bytes 65536 | tf_op jit(solution)/shard_map/expert_backward/pallas_call | solution.py:682
  521.1 11.6 %convolution_convert_fusion = bf16[2048,1024]{1,0:T(8,128)(2,1)} fusion(bf16[1536,2048]{1,0:T(8,128)(2,1)} %get-tuple-element.423, bf16[1536,1024]{1,0:T(8,128)(2,1)S(1)} %copy-done.29), kind=kOutput, calls=%fused_computation.7 | convolution fusion | flops 6444548096 | bytes 13631488 | tf_op jit(solution)/shard_map/dot_general | solution.py:1051
  553.8 27.5 %collective-permute-done.28 = bf16[384,2176]{1,0:T(8,128)(2,1)} collective-permute-done((bf16[384,2176]{1,0:T(8,128)(2,1)}, bf16[384,2176]{1,0:T(8,128)(2,1)}, u32[]{:S(2)}, u32[]{:S(2)}) %collective-permute-start.28) | collective-permute-done | bytes 1671200 | tf_op jit(solution)/shard_map/ppermute | solution.py:163
  614.4 22.9 %collective-permute-done.30.arrived_ref = bf16[384,2176]{1,0:T(8,128)(2,1)} collective-permute-done((bf16[384,2176]{1,0:T(8,128)(2,1)}, bf16[384,2176]{1,0:T(8,128)(2,1)}, u32[]{:S(2)}, u32[]{:S(2)}) %collective-permute-start.30) | collective-permute-done | bytes 1671200 | tf_op jit(solution)/shard_map/ppermute | solution.py:163
  644.5 14.4 %owner_backward.1 = (bf16[384,128]{1,0:T(8,128)(2,1)S(1)}, f32[8,2048]{1,0:T(8,128)S(1)}, f32[384,2048]{1,0:T(8,128)}, bf16[384,2048]{1,0:T(8,128)(2,1)S(1)}, bf16[8,384,256]{2,1,0:T(8,128)(2,1)S(1)}) custom-call(bf16[384,2176]{1,0:T(8,128)(2,1)} %collective-permute-done.30.arrived_ref, bf16[384,2176]{1,0:T(8,128)(2,1)} %slice_bitcast_fusion.1.mine_ref, ...), custom_call_target="tpu_custom_call" | custom-call | flops 14000000 | bytes 65536 | tf_op jit(solution)/shard_map/owner_backward/pallas_call | solution.py:806
  667.3 14.8 %collective-permute-done.33 = bf16[2,384,256]{2,1,0:T(8,128)(2,1)S(1)} collective-permute-done((bf16[2,384,256]{2,1,0:T(8,128)(2,1)S(1)}, bf16[2,384,256]{2,1,0:T(8,128)(2,1)S(1)}, u32[]{:S(2)}, u32[]{:S(2)}) %collective-permute-start.33) | collective-permute-done | bytes 393248 | tf_op jit(solution)/shard_map/ppermute | solution.py:163
  682.1 23.9 %collective-permute-done.34 = bf16[2,384,256]{2,1,0:T(8,128)(2,1)S(1)} collective-permute-done((bf16[2,384,256]{2,1,0:T(8,128)(2,1)S(1)}, bf16[2,384,256]{2,1,0:T(8,128)(2,1)S(1)}, u32[]{:S(2)}, u32[]{:S(2)}) %collective-permute-start.34) | collective-permute-done | bytes 393248 | tf_op jit(solution)/shard_map/ppermute | solution.py:163
  714.9 52.5 %attention_backward.1 = (f32[3072,256]{1,0:T(8,128)}, f32[3072,256]{1,0:T(8,128)}, bf16[3072,256]{1,0:T(8,128)(2,1)S(1)}, f32[2,8,1,384]{3,2,1,0:T(1,128)S(1)}, f32[2,8,1,384]{3,2,1,0:T(1,128)S(1)}) custom-call(s32[8]{0:T(128)S(1)} %add_select_fusion.high_ref, s32[8,1,384]{2,1,0:T(1,128)S(1)} %bitcast.210, bf16[3072,256]{1,0:T(8,128)(2,1)S(1)} %copy-done.9, ...), custom_call_target="tpu_custom_call" | custom-call | flops 46000000 | bytes 65536 | tf_op jit(solution)/shard_map/attention_backward/pallas_call | solution.py:363
  775.5 14.2 %exchange_small.6.m_ref = f32[8,2,384]{2,1,0:T(2,128)} custom-call(f32[8,2,384]{2,1,0:T(2,128)} %pad_maximum_fusion.7.refs_0_), custom_call_target="tpu_custom_call" | custom-call | tf_op jit(solution)/shard_map/exchange_small/pallas_call | solution.py:140
  807.5 36.8 %all-reduce.6.cloned.1.call-done = (bf16[1024,2048]{1,0:T(8,128)(2,1)}, bf16[2048,1024]{1,0:T(8,128)(2,1)}, bf16[2048,1024]{1,0:T(8,128)(2,1)}) async-done(((bf16[1024,2048]{1,0:T(8,128)(2,1)}, bf16[2048,1024]{1,0:T(8,128)(2,1)}, bf16[2048,1024]{1,0:T(8,128)(2,1)}), (bf16[1024,2048]{1,0:T(8,128)(2,1)}, bf16[2048,1024]{1,0:T(8,128)(2,1)}, bf16[2048,1024]{1,0:T(8,128)(2,1)})) %all-reduce.6.cloned.1.call-update) | async-done | bytes 12582928 | tf_op jit(solution)/shard_map/psum | solution.py:1288
  849.6 14.6 %project_back.3 = (bf16[3072,768]{1,0:T(8,128)(2,1)}, bf16[3,384,2048]{2,1,0:T(8,128)(2,1)}, bf16[3,384,2048]{2,1,0:T(8,128)(2,1)}, f32[8,256]{1,0:T(8,128)S(1)}) custom-call(s32[4]{0:T(128)S(1)} %pad_add_fusion.5.at_ref, f32[3072,512]{1,0:T(8,128)} %get-tuple-element.343.p_ref, f32[8,2,384]{2,1,0:T(2,128)S(1)} %copy-done.19, ...), custom_call_target="tpu_custom_call", output_to_operand_aliasing={{0}: (11, {})} | custom-call | flops 24000000 | bytes 65536 | tf_op jit(solution)/shard_map/project_back/pallas_call | solution.py:988
  864.2 14.7 %convolution_convert_fusion.5 = bf16[2048,768]{0,1:T(8,128)(2,1)S(1)} fusion(bf16[3072,2048]{1,0:T(8,128)(2,1)} %get-tuple-element.497, bf16[3072,768]{1,0:T(8,128)(2,1)} %get-tuple-element.498), kind=kOutput, calls=%fused_computation.15 | convolution fusion | flops 9665249280 | bytes 20447232 | tf_op jit(solution)/shard_map/dot_general | solution.py:1051
  884.4 31.6 %collective-permute-done.44 = bf16[384,2048]{1,0:T(8,128)(2,1)} collective-permute-done((bf16[384,2048]{1,0:T(8,128)(2,1)}, bf16[384,2048]{1,0:T(8,128)(2,1)}, u32[]{:S(2)}, u32[]{:S(2)}) %collective-permute-start.44) | collective-permute-done | bytes 1572896 | tf_op jit(solution)/shard_map/ppermute | solution.py:163
  941.9 32.8 %exchange_small.7 = f32[32,8,256]{2,1,0:T(8,128)} custom-call(f32[8,256]{1,0:T(8,128)} %add.480.refs_0_), custom_call_target="tpu_custom_call" | custom-call | tf_op jit(solution)/shard_map/exchange_small/pallas_call | solution.py:140
  1004.3 29.6 %collective-permute-done.54 = bf16[64,2048]{1,0:T(8,128)(2,1)} collective-permute-done((bf16[64,2048]{1,0:T(8,128)(2,1)}, bf16[64,2048]{1,0:T(8,128)(2,1)}, u32[]{:S(2)}, u32[]{:S(2)}) %collective-permute-start.54) | collective-permute-done | bytes 262176 | tf_op jit(solution)/shard_map/ppermute | solution.py:163
  1033.8 17.3 %collective-permute-done.55 = bf16[64,2048]{1,0:T(8,128)(2,1)} collective-permute-done((bf16[64,2048]{1,0:T(8,128)(2,1)}, bf16[64,2048]{1,0:T(8,128)(2,1)}, u32[]{:S(2)}, u32[]{:S(2)}) %collective-permute-start.55) | collective-permute-done | bytes 262176 | tf_op jit(solution)/shard_map/ppermute | solution.py:163
  1062.5 14.8 %collective-permute-done.51 = bf16[2,64,896]{2,1,0:T(8,128)(2,1)S(1)} collective-permute-done((bf16[2,64,896]{2,1,0:T(8,128)(2,1)S(1)}, bf16[2,64,896]{2,1,0:T(8,128)(2,1)S(1)}, u32[]{:S(2)}, u32[]{:S(2)}) %collective-permute-start.51) | collective-permute-done | bytes 229408 | tf_op jit(solution)/shard_map/ppermute | solution.py:163
  (441 shorter events, 368.0 us)
Async XLA Ops:
  7.2 109.6 %all-gather.3.cloned.1.call-start = ((), (), s32[]{:S(2)}) async-start(), calls=%async_computation.2 | async-start | bytes 3932160 | tf_op jit(solution)/shard_map/all_gather | solution.py:1122
  7.2 91.8 %collective-permute-start = (bf16[384,2048]{1,0:T(8,128)(2,1)}, bf16[384,2048]{1,0:T(8,128)(2,1)}, u32[]{:S(2)}, u32[]{:S(2)}) collective-permute-start(bf16[384,2048]{1,0:T(8,128)(2,1)} %mine_ref), channel_id=1, source_target_pairs={{0,2},{1,3},{2,4},{3,5},{4,6},{5,7},{6,0},{7,1},{8,10},{9,11},{10,... | collective-permute-start | bytes 4718600 | tf_op jit(solution)/shard_map/ppermute | solution.py:163
  7.3 91.7 %collective-permute-start.1 = (bf16[384,2048]{1,0:T(8,128)(2,1)}, bf16[384,2048]{1,0:T(8,128)(2,1)S(1)}, u32[]{:S(2)}, u32[]{:S(2)}) collective-permute-start(bf16[384,2048]{1,0:T(8,128)(2,1)} %mine_ref), channel_id=1, source_target_pairs={{0,1},{1,0},{2,3},{3,2},{4,5},{5,4},{6,7},{7,6},{8,9},{9,8},{10,11... | collective-permute-start | bytes 4718600 | tf_op jit(solution)/shard_map/ppermute | solution.py:158
  12.3 43.1 %collective-permute-start.3 = (bf16[2,64,768]{2,1,0:T(8,128)(2,1)S(1)}, bf16[2,64,768]{2,1,0:T(8,128)(2,1)}, u32[]{:S(2)}, u32[]{:S(2)}) collective-permute-start(bf16[2,64,768]{2,1,0:T(8,128)(2,1)S(1)} %get-tuple-element.618), channel_id=1, source_target_pairs={{0,4},{1,5},{2,6},{3,7},{4,0},{5,1},{6,2},{7,3},{8,12},{9,13},{10,... | collective-permute-start | bytes 589832 | tf_op jit(solution)/shard_map/ppermute | solution.py:163
  12.3 44.0 %collective-permute-start.2 = (bf16[2,64,768]{2,1,0:T(8,128)(2,1)S(1)}, bf16[2,64,768]{2,1,0:T(8,128)(2,1)}, u32[]{:S(2)}, u32[]{:S(2)}) collective-permute-start(bf16[2,64,768]{2,1,0:T(8,128)(2,1)S(1)} %get-tuple-element.616), channel_id=1, source_target_pairs={{0,2},{1,3},{2,4},{3,5},{4,6},{5,7},{6,0},{7,1},{8,10},{9,11},{10,... | collective-permute-start | bytes 589832 | tf_op jit(solution)/shard_map/ppermute | solution.py:163
  68.7 243.1 %all-gather.5.cloned.1.call-start = ((), (), s32[]{:S(2)}) async-start(), calls=%async_computation.3 | async-start | bytes 8650752 | tf_op jit(solution)/shard_map/all_gather | solution.py:1189
  175.9 668.4 %all-reduce.6.cloned.1.call-start = ((), (), s32[]{:S(2)}) async-start(), calls=%async_computation.6 | async-start | bytes 25165824 | tf_op jit(solution)/shard_map/psum | solution.py:1288
  202.4 69.2 %collective-permute-start.11 = (bf16[384,2048]{1,0:T(8,128)(2,1)}, bf16[384,2048]{1,0:T(8,128)(2,1)}, u32[]{:S(2)}, u32[]{:S(2)}) collective-permute-start(bf16[384,2048]{1,0:T(8,128)(2,1)} %cot_ref.1), channel_id=1, source_target_pairs={{0,2},{1,3},{2,4},{3,5},{4,6},{5,7},{6,0},{7,1},{8,10},{9,11},{10,... | collective-permute-start | bytes 4718600 | tf_op jit(solution)/shard_map/ppermute | solution.py:163
  382.9 54.1 %collective-permute-start.21 = (bf16[384,2048]{1,0:T(8,128)(2,1)}, bf16[384,2048]{1,0:T(8,128)(2,1)}, u32[]{:S(2)}, u32[]{:S(2)}) collective-permute-start(bf16[384,2048]{1,0:T(8,128)(2,1)} %collective-permute-done.11.refs_0_), channel_id=1, source_target_pairs={{0,1},{1,0},{2,3},{3,2},{4,5},{5,4},{6,7},{7,6},{8,9},{9,8},{10,11... | collective-permute-start | bytes 4718600 | tf_op jit(solution)/shard_map/ppermute | solution.py:158
  383.0 72.0 %collective-permute-start.18 = (bf16[384,2048]{1,0:T(8,128)(2,1)}, bf16[384,2048]{1,0:T(8,128)(2,1)}, u32[]{:S(2)}, u32[]{:S(2)}) collective-permute-start(bf16[384,2048]{1,0:T(8,128)(2,1)} %collective-permute-done.11.refs_0_), channel_id=1, source_target_pairs={{0,2},{1,3},{2,4},{3,5},{4,6},{5,7},{6,0},{7,1},{8,10},{9,11},{10,... | collective-permute-start | bytes 4718600 | tf_op jit(solution)/shard_map/ppermute | solution.py:163
  387.0 68.3 %collective-permute-start.19 = (bf16[384,2048]{1,0:T(8,128)(2,1)}, bf16[384,2048]{1,0:T(8,128)(2,1)}, u32[]{:S(2)}, u32[]{:S(2)}) collective-permute-start(bf16[384,2048]{1,0:T(8,128)(2,1)} %cot_ref.1), channel_id=1, source_target_pairs={{0,6},{1,7},{2,0},{3,1},{4,2},{5,3},{6,4},{7,5},{8,14},{9,15},{10,... | collective-permute-start | bytes 4718600 | tf_op jit(solution)/shard_map/ppermute | solution.py:163
  387.2 68.1 %collective-permute-start.20 = (bf16[384,2048]{1,0:T(8,128)(2,1)}, bf16[384,2048]{1,0:T(8,128)(2,1)}, u32[]{:S(2)}, u32[]{:S(2)}) collective-permute-start(bf16[384,2048]{1,0:T(8,128)(2,1)} %cot_ref.1), channel_id=1, source_target_pairs={{0,1},{1,0},{2,3},{3,2},{4,5},{5,4},{6,7},{7,6},{8,9},{9,8},{10,11... | collective-permute-start | bytes 4718600 | tf_op jit(solution)/shard_map/ppermute | solution.py:158
  512.0 69.3 %collective-permute-start.29 = (bf16[384,2176]{1,0:T(8,128)(2,1)}, bf16[384,2176]{1,0:T(8,128)(2,1)}, u32[]{:S(2)}, u32[]{:S(2)}) collective-permute-start(bf16[384,2176]{1,0:T(8,128)(2,1)} %get-tuple-element.594), channel_id=1, source_target_pairs={{0,1},{1,0},{2,3},{3,2},{4,5},{5,4},{6,7},{7,6},{8,9},{9,8},{10,11... | collective-permute-start | bytes 5013512 | tf_op jit(solution)/shard_map/ppermute | solution.py:158
  512.4 132.0 %collective-permute-start.32 = (bf16[384,2176]{1,0:T(8,128)(2,1)}, bf16[384,2176]{1,0:T(8,128)(2,1)}, u32[]{:S(2)}, u32[]{:S(2)}) collective-permute-start(bf16[384,2176]{1,0:T(8,128)(2,1)} %get-tuple-element.593), channel_id=1, source_target_pairs={{0,1},{1,0},{2,3},{3,2},{4,5},{5,4},{6,7},{7,6},{8,9},{9,8},{10,11... | collective-permute-start | bytes 5013512 | tf_op jit(solution)/shard_map/ppermute | solution.py:158
  512.5 196.0 %collective-permute-start.37 = (bf16[384,2048]{1,0:T(8,128)(2,1)}, bf16[384,2048]{1,0:T(8,128)(2,1)}, u32[]{:S(2)}, u32[]{:S(2)}) collective-permute-start(bf16[384,2048]{1,0:T(8,128)(2,1)} %get-tuple-element.591), channel_id=1, source_target_pairs={{0,1},{1,0},{2,3},{3,2},{4,5},{5,4},{6,7},{7,6},{8,9},{9,8},{10,11... | collective-permute-start | bytes 4718600 | tf_op jit(solution)/shard_map/ppermute | solution.py:158
  602.1 389.4 %reduce-scatter.5.cloned.1.call-start = ((), (), s32[]{:S(2)}) async-start(), calls=%async_computation.5 | async-start | bytes 5242880 | tf_op jit(solution)/shard_map/reduce_scatter | solution.py:1385
  637.4 68.6 %collective-permute-start.36 = (bf16[384,2048]{1,0:T(8,128)(2,1)}, bf16[384,2048]{1,0:T(8,128)(2,1)}, u32[]{:S(2)}, u32[]{:S(2)}) collective-permute-start(bf16[384,2048]{1,0:T(8,128)(2,1)} %fusion.25), channel_id=1, source_target_pairs={{0,2},{1,3},{2,4},{3,5},{4,6},{5,7},{6,0},{7,1},{8,10},{9,11},{10,... | collective-permute-start | bytes 4718600 | tf_op jit(solution)/shard_map/ppermute | solution.py:163
  659.1 46.9 %collective-permute-start.34 = (bf16[2,384,256]{2,1,0:T(8,128)(2,1)S(1)}, bf16[2,384,256]{2,1,0:T(8,128)(2,1)S(1)}, u32[]{:S(2)}, u32[]{:S(2)}) collective-permute-start(bf16[2,384,256]{2,1,0:T(8,128)(2,1)S(1)} %get-tuple-element.454), channel_id=1, source_target_pairs={{0,4},{1,5},{2,6},{3,7},{4,0},{5,1},{6,2},{7,3},{8,12},{9,13},{10,... | collective-permute-start | bytes 1179656 | tf_op jit(solution)/shard_map/ppermute | solution.py:163
  659.2 46.8 %collective-permute-start.35 = (bf16[2,384,256]{2,1,0:T(8,128)(2,1)S(1)}, bf16[2,384,256]{2,1,0:T(8,128)(2,1)S(1)}, u32[]{:S(2)}, u32[]{:S(2)}) collective-permute-start(bf16[2,384,256]{2,1,0:T(8,128)(2,1)S(1)} %get-tuple-element.455), channel_id=1, source_target_pairs={{0,6},{1,7},{2,0},{3,1},{4,2},{5,3},{6,4},{7,5},{8,14},{9,15},{10,... | collective-permute-start | bytes 1179656 | tf_op jit(solution)/shard_map/ppermute | solution.py:163
  714.1 54.5 %collective-permute-start.42 = (bf16[1024,2048]{1,0:T(8,128)(2,1)}, bf16[1024,2048]{1,0:T(8,128)(2,1)}, u32[]{:S(2)}, u32[]{:S(2)}) collective-permute-start(bf16[1024,2048]{1,0:T(8,128)(2,1)} %convolution_convert_fusion.3), channel_id=1, source_target_pairs={{0,1},{1,0},{2,3},{3,2},{4,5},{5,4},{6,7},{7,6},{8,9},{9,8},{10,11... | collective-permute-start | bytes 12582920 | tf_op jit(solution)/shard_map/ppermute | solution.py:158
  714.2 60.6 %collective-permute-start.40 = (bf16[384,2048]{1,0:T(8,128)(2,1)}, bf16[384,2048]{1,0:T(8,128)(2,1)}, u32[]{:S(2)}, u32[]{:S(2)}) collective-permute-start(bf16[384,2048]{1,0:T(8,128)(2,1)} %get-tuple-element.590), channel_id=1, source_target_pairs={{0,1},{1,0},{2,3},{3,2},{4,5},{5,4},{6,7},{7,6},{8,9},{9,8},{10,11... | collective-permute-start | bytes 4718600 | tf_op jit(solution)/shard_map/ppermute | solution.py:158
  714.7 60.1 %collective-permute-start.41 = (bf16[384,2048]{1,0:T(8,128)(2,1)}, bf16[384,2048]{1,0:T(8,128)(2,1)}, u32[]{:S(2)}, u32[]{:S(2)}) collective-permute-start(bf16[384,2048]{1,0:T(8,128)(2,1)} %get-tuple-element.589), channel_id=1, source_target_pairs={{0,1},{1,0},{2,3},{3,2},{4,5},{5,4},{6,7},{7,6},{8,9},{9,8},{10,11... | collective-permute-start | bytes 4718600 | tf_op jit(solution)/shard_map/ppermute | solution.py:158
  714.7 60.0 %collective-permute-start.39 = (bf16[384,2048]{1,0:T(8,128)(2,1)}, bf16[384,2048]{1,0:T(8,128)(2,1)}, u32[]{:S(2)}, u32[]{:S(2)}) collective-permute-start(bf16[384,2048]{1,0:T(8,128)(2,1)} %fusion.24), channel_id=1, source_target_pairs={{0,2},{1,3},{2,4},{3,5},{4,6},{5,7},{6,0},{7,1},{8,10},{9,11},{10,... | collective-permute-start | bytes 4718600 | tf_op jit(solution)/shard_map/ppermute | solution.py:163
  844.3 154.0 %reduce-scatter.3.cloned.1.call-start = ((), (), s32[]{:S(2)}) async-start(), calls=%async_computation.4 | async-start | bytes 4587520 | tf_op jit(solution)/shard_map/reduce_scatter | solution.py:1403
  847.0 68.9 %collective-permute-start.44 = (bf16[384,2048]{1,0:T(8,128)(2,1)}, bf16[384,2048]{1,0:T(8,128)(2,1)}, u32[]{:S(2)}, u32[]{:S(2)}) collective-permute-start(bf16[384,2048]{1,0:T(8,128)(2,1)} %fusion.20), channel_id=1, source_target_pairs={{0,2},{1,3},{2,4},{3,5},{4,6},{5,7},{6,0},{7,1},{8,10},{9,11},{10,... | collective-permute-start | bytes 4718600 | tf_op jit(solution)/shard_map/ppermute | solution.py:163
  923.2 62.7 %collective-permute-start.48 = (bf16[384,2048]{1,0:T(8,128)(2,1)}, bf16[384,2048]{1,0:T(8,128)(2,1)}, u32[]{:S(2)}, u32[]{:S(2)}) collective-permute-start(bf16[384,2048]{1,0:T(8,128)(2,1)} %get-tuple-element.597), channel_id=1, source_target_pairs={{0,1},{1,0},{2,3},{3,2},{4,5},{5,4},{6,7},{7,6},{8,9},{9,8},{10,11... | collective-permute-start | bytes 4718600 | tf_op jit(solution)/shard_map/ppermute | solution.py:158
  923.2 62.7 %collective-permute-start.49 = (bf16[384,2048]{1,0:T(8,128)(2,1)}, bf16[384,2048]{1,0:T(8,128)(2,1)S(1)}, u32[]{:S(2)}, u32[]{:S(2)}) collective-permute-start(bf16[384,2048]{1,0:T(8,128)(2,1)} %get-tuple-element.596), channel_id=1, source_target_pairs={{0,1},{1,0},{2,3},{3,2},{4,5},{5,4},{6,7},{7,6},{8,9},{9,8},{10,11... | collective-permute-start | bytes 4718600 | tf_op jit(solution)/shard_map/ppermute | solution.py:158
  930.1 55.8 %collective-permute-start.47 = (bf16[384,2048]{1,0:T(8,128)(2,1)}, bf16[384,2048]{1,0:T(8,128)(2,1)}, u32[]{:S(2)}, u32[]{:S(2)}) collective-permute-start(bf16[384,2048]{1,0:T(8,128)(2,1)} %fusion.19), channel_id=1, source_target_pairs={{0,2},{1,3},{2,4},{3,5},{4,6},{5,7},{6,0},{7,1},{8,10},{9,11},{10,... | collective-permute-start | bytes 4718600 | tf_op jit(solution)/shard_map/ppermute | solution.py:163
  991.4 86.0 %collective-permute-start.53 = (bf16[384,2048]{1,0:T(8,128)(2,1)}, bf16[384,2048]{1,0:T(8,128)(2,1)}, u32[]{:S(2)}, u32[]{:S(2)}) collective-permute-start(bf16[384,2048]{1,0:T(8,128)(2,1)} %fusion.15), channel_id=1, source_target_pairs={{0,2},{1,3},{2,4},{3,5},{4,6},{5,7},{6,0},{7,1},{8,10},{9,11},{10,... | collective-permute-start | bytes 4718600 | tf_op jit(solution)/shard_map/ppermute | solution.py:163
  997.0 54.1 %collective-permute-start.55 = (bf16[64,2048]{1,0:T(8,128)(2,1)}, bf16[64,2048]{1,0:T(8,128)(2,1)}, u32[]{:S(2)}, u32[]{:S(2)}) collective-permute-start(bf16[64,2048]{1,0:T(8,128)(2,1)} %get-tuple-element.607), channel_id=1, source_target_pairs={{0,4},{1,5},{2,6},{3,7},{4,0},{5,1},{6,2},{7,3},{8,12},{9,13},{10,... | collective-permute-start | bytes 786440 | tf_op jit(solution)/shard_map/ppermute | solution.py:163
  997.0 54.1 %collective-permute-start.56 = (bf16[64,2048]{1,0:T(8,128)(2,1)S(1)}, bf16[64,2048]{1,0:T(8,128)(2,1)}, u32[]{:S(2)}, u32[]{:S(2)}) collective-permute-start(bf16[64,2048]{1,0:T(8,128)(2,1)S(1)} %get-tuple-element.606), channel_id=1, source_target_pairs={{0,6},{1,7},{2,0},{3,1},{4,2},{5,3},{6,4},{7,5},{8,14},{9,15},{10,... | collective-permute-start | bytes 786440 | tf_op jit(solution)/shard_map/ppermute | solution.py:163
  1001.8 60.7 %collective-permute-start.50 = (bf16[2,64,896]{2,1,0:T(8,128)(2,1)S(1)}, bf16[2,64,896]{2,1,0:T(8,128)(2,1)S(1)}, u32[]{:S(2)}, u32[]{:S(2)}) collective-permute-start(bf16[2,64,896]{2,1,0:T(8,128)(2,1)S(1)} %get-tuple-element.615), channel_id=1, source_target_pairs={{0,2},{1,3},{2,4},{3,5},{4,6},{5,7},{6,0},{7,1},{8,10},{9,11},{10,... | collective-permute-start | bytes 688136 | tf_op jit(solution)/shard_map/ppermute | solution.py:163
  (93 other events, 1410.6 us)
Sparse Core Ops, SparseCore 0:
  68.8 47.9 all-gather.2
  176.1 98.9 all-gather.4
  602.2 242.0 all-reduce.5
  847.1 52.6 reduce-scatter.4
  916.1 49.1 reduce-scatter.2

commit v3 on v2

--- a/solution.py
+++ b/solution.py
@@ -210,78 +210,99 @@
     return exchange_cores(*exchange_chips(blocks))
 
 
-def add3(arrived, mine, swapped):
-    return (arrived.astype(F32) + mine.astype(F32) + swapped.astype(F32)).astype(BF)
-
-
-def add2(mine, swapped):
-    return (mine.astype(F32) + swapped.astype(F32)).astype(BF)
+def add_rows(*parts):
+    parts = [part if isinstance(part, tuple) else (part[None], 0) for part in parts]
+    _, rows, width = parts[0][0].shape
+    tile = rows // 2
+
+    def kernel(*refs):
+        total = refs[0][0].astype(F32)
+        for ref in refs[1:-1]:
+            total = total + ref[0].astype(F32)
+        refs[-1][...] = total.astype(BF)
+
+    def spec(which):
+        return pl.BlockSpec((1, tile, width), lambda i: (which, i, 0))
+
+    return pl.pallas_call(
+        kernel,
+        out_shape=jax.ShapeDtypeStruct((rows, width), BF),
+        grid=(2,),
+        in_specs=[spec(which) for _, which in parts],
+        out_specs=pl.BlockSpec((tile, width), lambda i: (i, 0)),
+        cost_estimate=cost(3),
+        name="add_rows",
+    )(*[array for array, _ in parts])
 
 
 def attention_forward(queries, keys, values, starts, lowest):
-    rows = queries.shape[0]
-    heads = queries.shape[1] // HEAD_DIM
+    rows, columns = queries.shape
+    heads = columns // HEAD_DIM
     blocks, _, block = starts.shape
     scale = HEAD_DIM ** (-0.5)
 
     def kernel(low_ref, start_ref, q_ref, k_ref, v_ref, o_ref, lse_ref):
-        i = pl.program_id(1)
-        q = q_ref[...]
+        i = pl.program_id(0)
         start = start_ref[0]
         q_index = i * block + lax.broadcasted_iota(jnp.int32, (1, block), 1)
         k_local = lax.broadcasted_iota(jnp.int32, (block, block), 0)
 
         def step(j, carry):
-            top, total, acc = carry
-            at = pl.multiple_of(j * block, block)
-            k = k_ref[pl.ds(at, block), :]
-            v = v_ref[pl.ds(at, block), :]
-            s = (
-                lax.dot_general(k, q, (((1,), (1,)), ((), ())), preferred_element_type=F32)
-                * scale
-            )
+            at = pl.ds(pl.multiple_of(j * block, block), block)
             k_index = k_local + j * block
-            s = jnp.where((k_index <= q_index) & (k_index >= start), s, NEG)
-            new_top = jnp.maximum(top, jnp.max(s, axis=0, keepdims=True))
-            p = jnp.exp(s - new_top)
-            shrink = jnp.exp(top - new_top)
-            total = total * shrink + jnp.sum(p, axis=0, keepdims=True)
-            acc = acc * shrink + lax.dot_general(
-                v, p.astype(BF), (((0,), (0,)), ((), ())), preferred_element_type=F32
-            )
-            return (new_top, total, acc)
-
-        top, total, acc = lax.fori_loop(
-            low_ref[i],
-            i + 1,
-            step,
-            (
-                jnp.full((1, block), NEG, F32),
-                jnp.zeros((1, block), F32),
-                jnp.zeros((HEAD_DIM, block), F32),
-            ),
+            allowed = (k_index <= q_index) & (k_index >= start)
+            after = []
+            for h in range(heads):
+                top, total, acc = carry[h]
+                lanes = slice(h * HEAD_DIM, (h + 1) * HEAD_DIM)
+                s = lax.dot_general(
+                    k_ref[at, lanes],
+                    q_ref[:, lanes],
+                    (((1,), (1,)), ((), ())),
+                    preferred_element_type=F32,
+                )
+                s = jnp.where(allowed, s * scale, NEG)
+                new_top = jnp.maximum(top, jnp.max(s, axis=0, keepdims=True))
+                p = jnp.exp(s - new_top)
+                shrink = jnp.exp(top - new_top)
+                total = total * shrink + jnp.sum(p, axis=0, keepdims=True)
+                acc = acc * shrink + lax.dot_general(
+                    v_ref[at, lanes],
+                    p.astype(BF),
+                    (((0,), (0,)), ((), ())),
+                    preferred_element_type=F32,
+                )
+                after.append((new_top, total, acc))
+            return tuple(after)
+
+        begin = (
+            jnp.full((1, block), NEG, F32),
+            jnp.zeros((1, block), F32),
+            jnp.zeros((HEAD_DIM, block), F32),
         )
-        o_ref[...] = (acc / total).T.astype(BF)
-        lse_ref[0, 0] = top + jnp.log(total)
+        done = lax.fori_loop(low_ref[i], i + 1, step, (begin,) * heads)
+        for h, (top, total, acc) in enumerate(done):
+            o_ref[:, h * HEAD_DIM : (h + 1) * HEAD_DIM] = (acc / total).T.astype(BF)
+            lse_ref[h, 0] = top + jnp.log(total)
 
     return pl.pallas_call(
         kernel,
         out_shape=(
-            jax.ShapeDtypeStruct((rows, heads * HEAD_DIM), BF),
+            jax.ShapeDtypeStruct((rows, columns), BF),
             jax.ShapeDtypeStruct((heads, blocks, 1, block), F32),
         ),
         grid_spec=pltpu.PrefetchScalarGridSpec(
             num_scalar_prefetch=1,
-            grid=(heads, blocks),
+            grid=(blocks,),
             in_specs=[
-                pl.BlockSpec((1, 1, block), lambda h, i, low: (i, 0, 0)),
-                pl.BlockSpec((block, HEAD_DIM), lambda h, i, low: (i, h)),
-                pl.BlockSpec((rows, HEAD_DIM), lambda h, i, low: (0, h)),
-                pl.BlockSpec((rows, HEAD_DIM), lambda h, i, low: (0, h)),
+                pl.BlockSpec((1, 1, block), lambda i, low: (i, 0, 0)),
+                pl.BlockSpec((block, columns), lambda i, low: (i, 0)),
+                pl.BlockSpec((rows, columns), lambda i, low: (0, 0)),
+                pl.BlockSpec((rows, columns), lambda i, low: (0, 0)),
             ],
             out_specs=[
-                pl.BlockSpec((block, HEAD_DIM), lambda h, i, low: (i, h)),
-                pl.BlockSpec((1, 1, 1, block), lambda h, i, low: (h, i, 0, 0)),
+                pl.BlockSpec((block, columns), lambda i, low: (i, 0)),
+                pl.BlockSpec((heads, 1, 1, block), lambda i, low: (0, i, 0, 0)),
             ],
         ),
         compiler_params=pltpu.CompilerParams(vmem_limit_bytes=48 << 20),
@@ -290,9 +311,9 @@
     )(lowest, starts, queries, keys, values)
 
 
-def attention_backward(queries, keys, values, douts, lse, delta, starts, highest):
-    rows = queries.shape[0]
-    heads = queries.shape[1] // HEAD_DIM
+def attention_backward(queries, keys, values, outs, douts, lse, starts, highest):
+    rows, columns = queries.shape
+    heads = columns // HEAD_DIM
     blocks, _, block = starts.shape
     scale = HEAD_DIM ** (-0.5)
 
@@ -300,99 +321,96 @@
         high_ref,
         start_ref,
         q_ref,
+        o_ref,
         do_ref,
         k_ref,
         v_ref,
         lse_ref,
-        delta_ref,
         dq_ref,
         dk_ref,
         dv_ref,
         q_sum_ref,
         k_sum_ref,
+        delta_ref,
     ):
-        j = pl.program_id(1)
+        j = pl.program_id(0)
 
         @pl.when(j == 0)
         def _():
             dq_ref[...] = jnp.zeros_like(dq_ref)
-
-        k = k_ref[...]
-        v = v_ref[...]
+            for h in range(heads):
+                lanes = slice(h * HEAD_DIM, (h + 1) * HEAD_DIM)
+                for i in range(blocks):
+                    at = slice(i * block, (i + 1) * block)
+                    delta_ref[h, i] = row_sums(
+                        o_ref[at, lanes].astype(F32) * do_ref[at, lanes].astype(F32)
+                    )
+
         k_index = j * block + lax.broadcasted_iota(jnp.int32, (block, block), 0)
         q_local = lax.broadcasted_iota(jnp.int32, (1, block), 1)
+        contract = (((1,), (1,)), ((), ()))
 
         def step(i, carry):
-            dk, dv = carry
-            at = pl.multiple_of(i * block, block)
-            q = q_ref[pl.ds(at, block), :]
-            do = do_ref[pl.ds(at, block), :]
-            s = (
-                lax.dot_general(k, q, (((1,), (1,)), ((), ())), preferred_element_type=F32)
-                * scale
-            )
+            at = pl.ds(pl.multiple_of(i * block, block), block)
             allowed = (k_index <= q_local + i * block) & (k_index >= start_ref[i])
-            p = jnp.exp(jnp.where(allowed, s, NEG) - lse_ref[0, i])
-            dv = dv + jnp.dot(p.astype(BF), do, preferred_element_type=F32)
-            dp = lax.dot_general(v, do, (((1,), (1,)), ((), ())), preferred_element_type=F32)
-            ds = (p * (dp - delta_ref[0, i])).astype(BF)
-            dk = dk + jnp.dot(ds, q, preferred_element_type=F32)
-            dq_ref[pl.ds(at, block), :] += (
-                lax.dot_general(ds, k, (((0,), (0,)), ((), ())), preferred_element_type=F32)
-                * scale
-            )
-            return (dk, dv)
+            after = []
+            for h in range(heads):
+                dk, dv = carry[h]
+                lanes = slice(h * HEAD_DIM, (h + 1) * HEAD_DIM)
+                q, do = q_ref[at, lanes], do_ref[at, lanes]
+                k, v = k_ref[:, lanes], v_ref[:, lanes]
+                s = lax.dot_general(k, q, contract, preferred_element_type=F32) * scale
+                p = jnp.exp(jnp.where(allowed, s, NEG) - lse_ref[h, i])
+                dv = dv + jnp.dot(p.astype(BF), do, preferred_element_type=F32)
+                dp = lax.dot_general(v, do, contract, preferred_element_type=F32)
+                ds = (p * (dp - delta_ref[h, i])).astype(BF)
+                dk = dk + jnp.dot(ds, q, preferred_element_type=F32)
+                dq_ref[at, lanes] += (
+                    lax.dot_general(ds, k, (((0,), (0,)), ((), ())), preferred_element_type=F32)
+                    * scale
+                )
+                after.append((dk, dv))
+            return tuple(after)
 
         zero = jnp.zeros((block, HEAD_DIM), F32)
-        dk, dv = lax.fori_loop(j, high_ref[j] + 1, step, (zero, zero))
-        dk = dk * scale
-        dk_ref[...] = dk
-        dv_ref[...] = dv.astype(BF)
-        k_sum_ref[0, 0] = row_sums(k.astype(F32) * dk)
-
-        @pl.when(j == pl.num_programs(1) - 1)
-        def _():
-            for i in range(blocks):
-                at = slice(i * block, (i + 1) * block)
-                q_sum_ref[0, i] = row_sums(q_ref[at, :].astype(F32) * dq_ref[at, :])
-
-    whole = pl.BlockSpec((rows, HEAD_DIM), lambda h, j, high: (0, h))
-    part = pl.BlockSpec((block, HEAD_DIM), lambda h, j, high: (j, h))
-    line = pl.BlockSpec((1, blocks, 1, block), lambda h, j, high: (h, 0, 0, 0))
-    shape = jax.ShapeDtypeStruct((rows, heads * HEAD_DIM), F32)
+        done = lax.fori_loop(j, high_ref[j] + 1, step, ((zero, zero),) * heads)
+        for h, (dk, dv) in enumerate(done):
+            lanes = slice(h * HEAD_DIM, (h + 1) * HEAD_DIM)
+            dk = dk * scale
+            dk_ref[:, lanes] = dk
+            dv_ref[:, lanes] = dv.astype(BF)
+            k_sum_ref[h, 0] = row_sums(k_ref[:, lanes].astype(F32) * dk)
+            at = pl.ds(pl.multiple_of(j * block, block), block)
+            q_sum_ref[h, 0] = row_sums(q_ref[at, lanes].astype(F32) * dq_ref[at, lanes])
+
+    whole = pl.BlockSpec((rows, columns), lambda j, high: (0, 0))
+    part = pl.BlockSpec((block, columns), lambda j, high: (j, 0))
+    line = pl.BlockSpec((heads, blocks, 1, block), lambda j, high: (0, 0, 0, 0))
+    bit = pl.BlockSpec((heads, 1, 1, block), lambda j, high: (0, j, 0, 0))
+    shape = jax.ShapeDtypeStruct((rows, columns), F32)
+    sums = jax.ShapeDtypeStruct((heads, blocks, 1, block), F32)
     return pl.pallas_call(
         kernel,
-        out_shape=(
-            shape,
-            shape,
-            jax.ShapeDtypeStruct(shape.shape, BF),
-            jax.ShapeDtypeStruct((heads, blocks, 1, block), F32),
-            jax.ShapeDtypeStruct((heads, blocks, 1, block), F32),
-        ),
+        out_shape=(shape, shape, jax.ShapeDtypeStruct((rows, columns), BF), sums, sums),
         grid_spec=pltpu.PrefetchScalarGridSpec(
             num_scalar_prefetch=1,
-            grid=(heads, blocks),
+            grid=(blocks,),
             in_specs=[
-                pl.BlockSpec((blocks, 1, block), lambda h, j, high: (0, 0, 0)),
+                pl.BlockSpec((blocks, 1, block), lambda j, high: (0, 0, 0)),
+                whole,
                 whole,
                 whole,
                 part,
                 part,
                 line,
-                line,
             ],
-            out_specs=[
-                whole,
-                part,
-                part,
-                line,
-                pl.BlockSpec((1, 1, 1, block), lambda h, j, high: (h, j, 0, 0)),
-            ],
+            out_specs=[whole, part, part, bit, bit],
+            scratch_shapes=[pltpu.VMEM((heads, blocks, 1, block), F32)],
         ),
         compiler_params=pltpu.CompilerParams(vmem_limit_bytes=48 << 20),
         cost_estimate=cost(46),
         name="attention_backward",
-    )(highest, starts, queries, douts, keys, values, lse, delta)
+    )(highest, starts, queries, outs, douts, keys, values, lse)
 
 
 def gather_heads(tokens, pick, mine, other, source, core, out_weight, whole):
@@ -769,7 +787,7 @@
 
         total = (
             arrived_ref[...].astype(F32)
-            + mine_ref[...].astype(F32)
+            + mine_ref[0].astype(F32)
             + swapped_ref[...].astype(F32)
         )
         share = share_ref[...]
@@ -815,7 +833,7 @@
         grid=(rows // tile,),
         in_specs=[
             rows_of(wide),
-            rows_of(wide),
+            pl.BlockSpec((1, tile, wide), lambda i: (mine.shape[0] - 1, i, 0)),
             rows_of(wide),
             rows_of(128),
             fixed(128, width),
@@ -842,8 +860,8 @@
 
 def project_in(mine, other, chip, core, weight, whole):
     rows, width = mine.shape
-    columns = weight.shape[1] // 3
     ranks = lax.axis_size("expert")
+    columns = width // ranks
 
     def kernel(at_ref, mine_ref, other_ref, w_ref, *refs):
         x_out, n_out, p_out, v_out, s_out = refs[-5:]
@@ -1043,6 +1061,123 @@
     return inverse * (weighted - scaled * mean), jnp.sum(grad * scaled, axis=0)
 
 
+def weight_grad(a, b, tile=512):
+    rows, m = a.shape
+    n = b.shape[1]
+
+    def kernel(a_ref, b_ref, o_ref):
+        o_ref[...] = lax.dot_general(
+            a_ref[...], b_ref[...], (((0,), (0,)), ((), ())), preferred_element_type=F32
+        ).astype(BF)
+
+    return pl.pallas_call(
+        kernel,
+        out_shape=jax.ShapeDtypeStruct((m, n), BF),
+        grid=(m // tile,),
+        in_specs=[
+            pl.BlockSpec((rows, tile), lambda i: (0, i)),
+            pl.BlockSpec((rows, n), lambda i: (0, 0)),
+        ],
+        out_specs=pl.BlockSpec((tile, n), lambda i: (i, 0)),
+        compiler_params=pltpu.CompilerParams(vmem_limit_bytes=48 << 20),
+        cost_estimate=cost(10),
+        name="weight_grad",
+    )(a, b)
+
+
+def in_weight_grad(normed, dpre, mixed, dlogits, rows8, experts):
+    rows, m = normed.shape
+    own = mixed.shape[0]
+    n = dpre.shape[1]
+    tile = 512
+
+    def kernel(a_ref, b_ref, m_ref, l_ref, r_ref, o_ref):
+        contract = (((0,), (0,)), ((), ()))
+        o_ref[:, :n] = lax.dot_general(
+            a_ref[...], b_ref[...], contract, preferred_element_type=F32
+        ).astype(BF)
+        side = lax.dot_general(m_ref[...], l_ref[...], contract, preferred_element_type=F32)
+        turned = r_ref[...].T
+        lane = lax.broadcasted_iota(jnp.int32, side.shape, 1)
+        for i in range(3):
+            side = jnp.where(lane == experts + i, turned[:, i : i + 1], side)
+        o_ref[:, n:] = side.astype(BF)
+
+    return pl.pallas_call(
+        kernel,
+        out_shape=jax.ShapeDtypeStruct((m, n + 128), BF),
+        grid=(m // tile,),
+        in_specs=[
+            pl.BlockSpec((rows, tile), lambda i: (0, i)),
+            pl.BlockSpec((rows, n), lambda i: (0, 0)),
+            pl.BlockSpec((own, tile), lambda i: (0, i)),
+            pl.BlockSpec((own, 128), lambda i: (0, 0)),
+            pl.BlockSpec((8, tile), lambda i: (0, i)),
+        ],
+        out_specs=pl.BlockSpec((tile, n + 128), lambda i: (i, 0)),
+        compiler_params=pltpu.CompilerParams(vmem_limit_bytes=48 << 20),
+        cost_estimate=cost(14),
+        name="in_weight_grad",
+    )(normed, dpre, mixed, dlogits, rows8)
+
+
+def own_forward(places, pieces, tokens, out_weight, mix_gain, router, experts):
+    rows, width = tokens.shape
+    count = len(pieces)
+    columns = width // count
+
+    def kernel(at_ref, *refs):
+        token_ref, w_ref, gain_ref, router_ref = refs[count : count + 4]
+        att_ref, middle_ref, mixed_ref, share_ref, inverse_ref = refs[count + 4 :]
+        for i in range(count):
+            att_ref[:, pl.ds(pl.multiple_of(at_ref[i] * columns, columns), columns)] = refs[i][...]
+        middle = token_ref[...].astype(F32) + jnp.dot(
+            att_ref[...], w_ref[...], preferred_element_type=F32
+        )
+        middle_ref[...] = middle
+        inverse = lax.rsqrt(jnp.mean(middle * middle, axis=1, keepdims=True) + EPS)
+        inverse_ref[...] = jnp.broadcast_to(inverse, inverse_ref.shape)
+        mixed = (middle * inverse * gain_ref[...]).astype(BF)
+        mixed_ref[...] = mixed
+        logits = lax.dot_general(
+            mixed, router_ref[...], (((1,), (1,)), ((), ())), preferred_element_type=F32
+        )
+        lane = lax.broadcasted_iota(jnp.int32, logits.shape, 1)
+        logits = jnp.where(lane < experts, logits, NEG)
+        shifted = jnp.exp(logits - jnp.max(logits, axis=1, keepdims=True))
+        share_ref[...] = shifted / jnp.sum(shifted, axis=1, keepdims=True)
+
+    def fixed(n, m):
+        return pl.BlockSpec((n, m), lambda i, at: (0, 0))
+
+    return pl.pallas_call(
+        kernel,
+        out_shape=(
+            jax.ShapeDtypeStruct((rows, width), BF),
+            jax.ShapeDtypeStruct((rows, width), F32),
+            jax.ShapeDtypeStruct((rows, width), BF),
+            jax.ShapeDtypeStruct((rows, 128), F32),
+            jax.ShapeDtypeStruct((rows, 128), F32),
+        ),
+        grid_spec=pltpu.PrefetchScalarGridSpec(
+            num_scalar_prefetch=1,
+            grid=(1,),
+            in_specs=[pl.BlockSpec((rows, columns), lambda i, at: (at[count], 0))] * count
+            + [fixed(rows, width), fixed(width, width), fixed(1, width), fixed(128, width)],
+            out_specs=[
+                fixed(rows, width),
+                fixed(rows, width),
+                fixed(rows, width),
+                fixed(rows, 128),
+                fixed(rows, 128),
+            ],
+        ),
+        compiler_params=pltpu.CompilerParams(vmem_limit_bytes=48 << 20),
+        cost_estimate=cost(10),
+        name="own_forward",
+    )(places, *pieces, tokens, out_weight, mix_gain, router)
+
+
 def dot_nt(a, b):
     return lax.dot_general(a, b, (((1,), (1,)), ((), ())), preferred_element_type=F32)
 
@@ -1107,6 +1242,10 @@
     heads = columns // HEAD_DIM
 
     own_gain = attnorm.astype(F32)[:, None]
+    beside = jnp.concatenate(
+        [querynorm[:, None], keynorm[:, None], mixnorm[:, None], router_weight], axis=1
+    )
+    beside = jnp.pad(beside, ((0, 0), (0, 128 - beside.shape[1])))
     stacked = jnp.concatenate(
         [
             (part.astype(F32) * own_gain)
@@ -1114,43 +1253,16 @@
             .reshape(shard, ranks, columns)
             .transpose(1, 0, 2)
             for part in (query_weight, key_weight, value_weight)
-        ],
+        ]
+        + [jnp.broadcast_to(beside, (ranks, shard, 128))],
         axis=2,
     )
-    tok, tok_other = [tokens, chip_shift(tokens)], [partner_swap(tokens)]
-    stacked = rank_exchange(stacked)
+    kept, given = exchange_chips(stacked)
+    tokens_, kept, given = tie(tokens, kept, given)
+    tok, tok_other = [tokens, chip_shift(tokens_)], [partner_swap(tokens_)]
+    stacked = exchange_cores(kept, given)
     in_weight = lax.all_gather(
-        stacked.reshape(ranks * shard, 3 * columns), "group", axis=0, tiled=True
-    )
-
-    small = jnp.concatenate(
-        [querynorm, keynorm, mixnorm, router_weight.T.reshape(-1)], axis=0
-    )
-    packed = jnp.zeros((2048,), BF).at[: small.shape[0]].set(small).reshape(16, 128)
-    packed_routes = (
-        jnp.zeros((1024,), jnp.int32)
-        .at[: rows * TOP]
-        .set(routes.T.reshape(-1))
-        .reshape(8, 128)
-    )
-    packed, packed_routes, _ = tie(packed, packed_routes, stacked)
-    everyone, all_routes = exchange_small(1, world=packed, group=packed_routes)
-    everyone = everyone.reshape(groups * ranks, 2048)
-    query_gain = everyone[:, :shard].reshape(width).astype(F32)
-    key_gain = everyone[:, shard : 2 * shard].reshape(width).astype(F32)
-    mix_gain = everyone[:, 2 * shard : 3 * shard].reshape(1, width).astype(F32)
-    router = jnp.pad(
-        everyone[:, 3 * shard : (3 + experts) * shard]
-        .reshape(groups * ranks, experts, shard)
-        .transpose(1, 0, 2)
-        .reshape(experts, width),
-        ((0, 128 - experts), (0, 0)),
-    )
-    my_gains = jnp.stack(
-        [
-            lax.dynamic_slice_in_dim(query_gain, me * columns, columns),
-            lax.dynamic_slice_in_dim(key_gain, me * columns, columns),
-        ]
+        stacked.reshape(ranks * shard, 3 * columns + 128), "group", axis=0, tiled=True
     )
 
     index, begin, final = layout_of(lengths, seq_order, all_rows)
@@ -1164,15 +1276,7 @@
     cosine = jnp.concatenate([cosine, cosine], axis=1)
     sine = jnp.concatenate([-sine, sine], axis=1)
 
-    all_routes = all_routes.reshape(ranks, -1)[:, : rows * TOP].reshape(ranks, TOP, rows)
-    named = jnp.any(all_routes == me, axis=1)
-    counted = jnp.cumsum(named.astype(jnp.int32), axis=1) - 1
-    slot_of = jnp.where(named, counted, -1)
-    slots = jnp.arange(capacity, dtype=jnp.int32)
-    pick = (slot_of[:, None, :] == slots[None, :, None]).astype(BF)
-    pick_t = (slot_of[:, :, None] == slots[None, None, :]).astype(BF)
-
-    tables = (my_gains, mix_gain, router, starts, lowest, highest, cosine, sine, pick, pick_t)
+    tables = (starts, lowest, highest, cosine, sine)
     state, ready = None, 0
     for step in range(1, chips):
         tok, tok_other, state, tables = tie(tok, tok_other, state, tables)
@@ -1184,18 +1288,36 @@
                 tok[ready], tok_other[ready], source_chip(ready), core, in_weight, state
             )
             ready += 1
-    my_gains, mix_gain, router, starts, lowest, highest, cosine, sine, pick, pick_t = tables
+    starts, lowest, highest, cosine, sine = tables
     output_weight_, _ = tie(output_weight, tok)
     full_output = lax.all_gather(output_weight_, ("group", "expert"), axis=0, tiled=True)
     all_tokens, normed, products, values, squares = state
-    (squares,) = exchange_small(2, added=squares)
+    packed_routes = (
+        jnp.zeros((1024,), jnp.int32)
+        .at[: rows * TOP]
+        .set(routes.T.reshape(-1))
+        .reshape(8, 128)
+    )
+    all_routes, squares = exchange_small(2, group=packed_routes, added=squares)
+    beside = in_weight[:, 3 * columns :]
+    my_gains = lax.dynamic_slice_in_dim(beside, me * columns, columns, 0)[:, :2].T.astype(F32)
+    mix_gain = beside[:, 2:3].T.astype(F32)
+    router = jnp.pad(beside[:, 3 : 3 + experts].T, ((0, 128 - experts), (0, 0)))
     queries, keys = make_heads(products, squares, my_gains, cosine, sine, width)
+
+    all_routes = all_routes.reshape(ranks, -1)[:, : rows * TOP].reshape(ranks, TOP, rows)
+    named = jnp.any(all_routes == me, axis=1)
+    counted = jnp.cumsum(named.astype(jnp.int32), axis=1) - 1
+    slot_of = jnp.where(named, counted, -1)
+    slots = jnp.arange(capacity, dtype=jnp.int32)
+    pick = (slot_of[:, None, :] == slots[None, :, None]).astype(BF)
+    pick_t = (slot_of[:, :, None] == slots[None, None, :]).astype(BF)
 
     cotangent_, _ = tie(cotangent, squares)
     cot = [cotangent_, chip_shift(cotangent_)]
     attended_mine, lse = attention_forward(queries, keys, values, starts, lowest)
     att = [attended_mine]
-    att, cot = tie(att, cot)
+    att, cot, pick, pick_t, mix_gain, router = tie(att, cot, pick, pick_t, mix_gain, router)
     att_other = [partner_swap(att[0])]
     att.append(chip_shift(att[0]))
     att, att_other = tie(att, att_other)
@@ -1255,7 +1377,7 @@
     )
     cot, cot_other, own_1, away_1, saved = tie(cot, cot_other, own_1, away_1, saved)
     cot_other += [partner_swap(cot[step]) for step in range(2, chips)]
-    dmixed_moving = add2(own_1[0], partner_swap(away_1[0]))
+    dmixed_moving = add_rows((own_1, 0), partner_swap(away_1[0]))
     cot_other, dmixed_moving, own_att_pieces = tie(
         cot_other, dmixed_moving, (att, att_other)
     )
@@ -1273,50 +1395,48 @@
         saved,
     )
     dmixed_moving, own, away, saved, out_away = tie(dmixed_moving, own, away, saved, out_away)
-    swapped = [partner_swap(away[i]) for i in range(chips - 1)]
+    dmixed_moving = add_rows(dmixed_moving, (own, 0), partner_swap(away[0]))
+    dmixed_moving, own, away, saved, out_away = tie(dmixed_moving, own, away, saved, out_away)
+    dmixed_moving = chip_shift(dmixed_moving)
+    swapped = [partner_swap(away[i]) for i in range(1, chips - 1)]
     out_first = partner_swap(out_away[1])
-    dmixed_moving = add3(dmixed_moving, own[0], swapped[0])
-    dmixed_moving, saved = tie(dmixed_moving, saved)
-    dmixed_moving = chip_shift(dmixed_moving)
     dcopy, dgate_pre, dup_pre = saved
     sums = [
-        dot_tn(hidden, dcopy).astype(BF),
-        dot_tn(mixed_e, dgate_pre).astype(BF),
-        dot_tn(mixed_e, dup_pre).astype(BF),
+        weight_grad(hidden, dcopy),
+        weight_grad(mixed_e, dgate_pre),
+        weight_grad(mixed_e, dup_pre),
     ]
-    dmixed_moving, sums = tie(dmixed_moving, sums)
-    down_sum, gate_sum, up_sum = (lax.psum(term, "group") for term in sums)
+    dmixed_moving, own, swapped, sums = tie(dmixed_moving, own, swapped, sums)
+    sums = lax.psum(tuple(sums), "group")
     for step in range(3, chips):
-        dmixed_moving = add3(dmixed_moving, own[step - 2], swapped[step - 2])
-        dmixed_moving, att_pieces = tie(dmixed_moving, own_att_pieces)
+        dmixed_moving = add_rows(dmixed_moving, (own, step - 2), swapped[step - 3])
+        dmixed_moving, pieces = tie(dmixed_moving, own_att_pieces)
         dmixed_moving = chip_shift(dmixed_moving)
 
-    own_attended = jnp.zeros((rows, width), BF)
+    places = []
     for step in range(chips):
-        at = source_chip(step) * 2
-        for pieces, rank in ((att_pieces[0], at + core), (att_pieces[1], at + 1 - core)):
-            piece = lax.dynamic_slice_in_dim(pieces[step], me * rows, rows, 0)
-            own_attended = lax.dynamic_update_slice(own_attended, piece, (0, rank * columns))
-    middle = tokens.astype(F32) + dot_nn(own_attended, full_output)
-    middle_inverse = lax.rsqrt(jnp.mean(middle * middle, axis=-1, keepdims=True) + EPS)
-    mixed = (middle * middle_inverse * mix_gain).astype(BF)
-    logits = dot_nt(mixed, router)
-    logits = jnp.where(jnp.arange(128, dtype=jnp.int32)[None] < experts, logits, NEG)
-    shifted = jnp.exp(logits - jnp.max(logits, axis=1, keepdims=True))
-    share = shifted / jnp.sum(shifted, axis=1, keepdims=True)
-    middle_inverse = jnp.broadcast_to(middle_inverse, (rows, 128))
+        places += [source_chip(step) * 2 + core, source_chip(step) * 2 + 1 - core]
+    own_attended, middle, mixed, share, middle_inverse = own_forward(
+        jnp.stack(places + [me]).astype(jnp.int32),
+        [piece for pair in zip(*pieces) for piece in pair],
+        tokens,
+        full_output,
+        mix_gain,
+        router,
+        experts,
+    )
     halves = own_attended.reshape(rows, groups * chips, 2, shard)
     att_mine = lax.dynamic_index_in_dim(halves, core, 2, keepdims=False).reshape(rows, -1)
     att_away = lax.dynamic_index_in_dim(halves, 1 - core, 2, keepdims=False).reshape(rows, -1)
-    out_moving = add2(out_own[1], out_first)
+    out_moving = add_rows((out_own, 1), out_first)
     dmixed_moving, middle, middle_inverse, mixed, share, att_mine, att_away, out_moving = tie(
         dmixed_moving, middle, middle_inverse, mixed, share, att_mine, att_away, out_moving
     )
     out_moving = chip_shift(out_moving)
     dlogits, mixnorm_term, dmiddle, dprojected, dattended_own = owner_backward(
         dmixed_moving,
-        own[chips - 2],
-        swapped[chips - 2],
+        own,
+        swapped[chips - 3],
         share,
         router,
         middle,
@@ -1334,123 +1454,118 @@
     ]
     parts, dprojected = tie(parts, dprojected)
     parts = parts[:1] + [chip_shift(parts[step], step) for step in range(1, chips)]
-    output_mine = dot_tn(att_mine, dprojected).astype(BF)
-    output_away = dot_tn(att_away, dprojected).astype(BF)
+    output_mine = weight_grad(att_mine, dprojected)
+    output_away = weight_grad(att_away, dprojected)
     parts, output_mine, output_away, out_moving = tie(parts, output_mine, output_away, out_moving)
     kept = [lax.dynamic_index_in_dim(part, core, 0) for part in parts]
     given = [lax.dynamic_index_in_dim(part, 1 - core, 0) for part in parts]
     dattended = exchange_cores(kept, jnp.concatenate(given, axis=0)).reshape(all_rows, columns)
     out_second = partner_swap(out_away[2])
-    delta = jnp.stack(
-        [
-            jnp.sum(
-                dattended[:, h * HEAD_DIM : (h + 1) * HEAD_DIM].astype(F32)
-                * attended_mine[:, h * HEAD_DIM : (h + 1) * HEAD_DIM].astype(F32),
-                axis=1,
-            )
-            for h in range(heads)
-        ]
-    ).reshape(heads, blocks, 1, block)
-    out_moving = add3(out_moving, out_own[2], out_second)
-
-    out_moving, dattended, delta, output_mine, output_away = tie(
-        out_moving, dattended, delta, output_mine, output_away
+    out_moving = add_rows(out_moving, (out_own, 2), out_second)
+
+    out_moving, dattended, output_mine, output_away = tie(
+        out_moving, dattended, output_mine, output_away
     )
     out_moving = chip_shift(out_moving)
     out_swapped = [partner_swap(out_away[step]) for step in (3, 0)]
-    output_pair = add2(output_mine, partner_swap(output_away))
+    output_swapped = partner_swap(output_away)
     dquery, dkey, dvalue, query_part, key_part = attention_backward(
-        queries, keys, values, dattended, lse, delta, starts, highest
-    )
-    out_moving, out_swapped, output_pair, dquery, dkey, dvalue, query_part, key_part = tie(
-        out_moving, out_swapped, output_pair, dquery, dkey, dvalue, query_part, key_part
-    )
+        queries, keys, values, attended_mine, dattended, lse, starts, highest
+    )
+    out_moving, out_swapped, output_swapped, dquery, dkey, dvalue, query_part, key_part = tie(
+        out_moving, out_swapped, output_swapped, dquery, dkey, dvalue, query_part, key_part
+    )
+    out_moving = add_rows(out_moving, (out_own, 3), out_swapped[0])
     partials = jnp.stack(
         [jnp.sum(query_part[:, :, 0], axis=0), jnp.sum(key_part[:, :, 0], axis=0)], axis=1
     )
+    partials, out_moving = tie(partials, out_moving)
     (means,) = exchange_small(3, added=partials)
-    out_moving = add3(out_moving, out_own[3], out_swapped[0])
-    out_moving, means = tie(out_moving, means)
+    out_moving, means, output_mine, output_swapped = tie(
+        out_moving, means, output_mine, output_swapped
+    )
     out_moving = chip_shift(out_moving)
     back = (products, squares, my_gains, cosine, sine, dquery, dkey, dvalue)
     dpre, dn_own_1, dn_away_1, gains_1 = project_back(
         [source_chip(1)], core, *back, means, in_weight, None
     )
-    dnormed_moving = add2(dn_own_1[0], partner_swap(dn_away_1[0]))
-    dnormed_moving, dpre, down_sum, gate_sum, up_sum = tie(
-        dnormed_moving, dpre, down_sum, gate_sum, up_sum
-    )
+    dnormed_moving = add_rows((dn_own_1, 0), partner_swap(dn_away_1[0]))
+    dnormed_moving, dpre = tie(dnormed_moving, dpre)
     dnormed_moving = chip_shift(dnormed_moving)
-    output_pair, _ = tie(output_pair, down_sum)
-    output_pair = lax.psum_scatter(
-        output_pair, "group", scatter_dimension=0, tiled=True
-    ).reshape(chips, shard, width)
     dpre, dn_own, dn_away, gains_2 = project_back(
         [source_chip(step) for step in rest], core, *back, means, in_weight, dpre
     )
-    in_term = jnp.concatenate(
+    gain_terms = gains_1 + gains_2
+
+    def spread(row):
+        return lax.dynamic_update_slice(jnp.zeros((1, width), F32), row, (0, me * columns))
+
+    rows8 = jnp.concatenate(
         [
-            dot_tn(normed, dpre).astype(BF),
-            dot_tn(mixed, dlogits).astype(BF)[:, :experts],
-            mixnorm_term[0].astype(BF)[:, None],
-            jnp.zeros((width, 128 - experts - 1), BF),
+            mixnorm_term[:1],
+            spread(gain_terms[:1]),
+            spread(gain_terms[1:2]),
+            jnp.zeros((5, width), F32),
         ],
-        axis=1,
-    )
-    dnormed_moving, dn_own, dn_away, in_term, out_moving = tie(
-        dnormed_moving, dn_own, dn_away, in_term, out_moving
-    )
+        axis=0,
+    )
+    in_term = in_weight_grad(normed, dpre, mixed, dlogits, rows8, experts)
+    dnormed_moving, dn_own, dn_away, in_term, out_moving, sums, output_mine = tie(
+        dnormed_moving, dn_own, dn_away, in_term, out_moving, sums, output_mine
+    )
+    output_sum = lax.psum_scatter(
+        add_rows(output_mine, output_swapped), "group", scatter_dimension=0, tiled=True
+    )
+    dnormed_moving = add_rows(dnormed_moving, (dn_own, 0), partner_swap(dn_away[0]))
+    dnormed_moving, dn_own, dn_away, sums, out_moving = tie(
+        dnormed_moving, dn_own, dn_away, sums, out_moving
+    )
+    dnormed_moving = chip_shift(dnormed_moving)
+    dn_swapped = [partner_swap(dn_away[i]) for i in range(1, chips - 1)]
     in_sum = lax.psum_scatter(in_term, "group", scatter_dimension=0, tiled=True)
-    dn_swapped = [partner_swap(dn_away[i]) for i in range(chips - 1)]
-    dnormed_moving = add3(dnormed_moving, dn_own[0], dn_swapped[0])
-    gain_terms = gains_1 + gains_2
-    dnormed_moving, gain_terms, out_moving, down_sum, gate_sum, up_sum = tie(
-        dnormed_moving, gain_terms, out_moving, down_sum, gate_sum, up_sum
-    )
-    dnormed_moving = chip_shift(dnormed_moving)
+    down_sum, gate_sum = sums[0].astype(F32)[None], sums[1].astype(F32)[None]
     layer_result = (
         middle
         + out_moving.astype(F32)
         + out_own[0].astype(F32)
         + out_swapped[1].astype(F32)
     ).astype(BF)
-    down_sum, gate_sum, up_sum = (
-        term.astype(F32)[None] for term in (down_sum, gate_sum, up_sum)
-    )
-    (gain_shares,) = exchange_small(4, world=gain_terms)
-    dnormed_moving, dn_swapped, down_sum, gate_sum, up_sum, gain_shares, layer_result = tie(
-        dnormed_moving, dn_swapped, down_sum, gate_sum, up_sum, gain_shares, layer_result
-    )
-    dnormed_moving = add3(dnormed_moving, dn_own[1], dn_swapped[1])
-    dnormed_moving, output_pair = tie(dnormed_moving, output_pair)
+    dnormed_moving, dn_swapped, down_sum, gate_sum, layer_result = tie(
+        dnormed_moving, dn_swapped, down_sum, gate_sum, layer_result
+    )
+    dnormed_moving = add_rows(dnormed_moving, (dn_own, 1), dn_swapped[0])
+    dnormed_moving, up_sum = tie(dnormed_moving, sums[2])
     dnormed_moving = chip_shift(dnormed_moving)
-
-    def to_chip(step):
-        part = lax.dynamic_index_in_dim(
-            output_pair, source_chip(chips - step), 0, keepdims=False
+    up_sum = up_sum.astype(F32)[None]
+    output_pairs = output_sum.reshape(chips, shard, width)
+
+    def to_chip(array, step):
+        return lax.dynamic_index_in_dim(
+            array, lax.rem(chip + step, chips), 0, keepdims=False
         )
-        return chip_shift(part, step)
-
-    output_parts = [to_chip(step) for step in range(1, chips)]
-    kept, given = exchange_chips(in_sum.reshape(ranks, shard, 3 * columns + 128))
-    output_sum = sum(
-        [part.astype(F32) for part in output_parts],
-        lax.dynamic_index_in_dim(output_pair, source_chip(0), 0, keepdims=False).astype(F32),
-    )
-    kept, given, dnormed_moving, output_sum = tie(kept, given, dnormed_moving, output_sum)
+
+    output_parts = [to_chip(output_pairs, step) for step in range(chips)]
+    output_parts = output_parts[:1] + [chip_shift(output_parts[i], i) for i in range(1, chips)]
+    output_parts, dnormed_moving, up_sum, in_sum = tie(
+        output_parts, dnormed_moving, up_sum, in_sum
+    )
+    in_pairs = in_sum.reshape(chips, 2, shard, 3 * columns + 128)
+    in_parts = [to_chip(in_pairs, step) for step in range(chips)]
+    (in_parts,) = tie(in_parts)
+    in_parts = in_parts[:1] + [chip_shift(in_parts[i], i) for i in range(1, chips)]
+    output_sum = sum(part.astype(F32) for part in output_parts)
+    (in_parts,) = tie(in_parts)
+    kept = [lax.dynamic_index_in_dim(part, core, 0) for part in in_parts]
+    given = jnp.concatenate(
+        [lax.dynamic_index_in_dim(part, 1 - core, 0) for part in in_parts], axis=0
+    )
     in_sum = exchange_cores(kept, given)
     dnormed = (
         dnormed_moving.astype(F32)
         + dn_own[chips - 2].astype(F32)
-        + dn_swapped[chips - 2].astype(F32)
-    )
-
-    norm_grads = jnp.sum(
-        gain_shares.reshape(groups, ranks, 8, columns)[:, :, :2], axis=0
-    )
-    norm_grads = norm_grads.transpose(1, 0, 2).reshape(2, width)
-    flat = lax.axis_index("group") * ranks + me
-    norm_grads = lax.dynamic_slice_in_dim(norm_grads, flat * shard, shard, 1)
+        + dn_swapped[chips - 3].astype(F32)
+    )
+
     raw = [
         in_sum[:, :, i * columns : (i + 1) * columns]
         .transpose(1, 0, 2)
@@ -1478,8 +1593,8 @@
         output_sum,
         others[:, :experts],
         attnorm_grad,
-        norm_grads[0],
-        norm_grads[1],
+        others[:, experts + 1],
+        others[:, experts + 2],
         others[:, experts],
         gate_sum,
         up_sum,

time: 1110 us -> 980 us (0.88)
  matrix products: 58.9 us -> 0 us
  waiting for transfers between devices: 382 us -> 330 us
  other arithmetic: 103 us -> 55.8 us
  Pallas kernels: 385 us -> 424 us
  starting transfers between devices: 79.4 us -> 67.3 us
    pallas_call x2 -> x19, Pallas kernels: 88.4 us -> 175 us  [the longest x1 45.2 us: attention_backward(): pl.pallas_call(kernel, out_shape=(shape, shape, jax.ShapeDtypeStruct((row...]
    dot_general x9 -> x0, matrix products: 58.9 us -> none  [the longest x7 52.2 us: dot_tn(): lax.dot_general(a, b, (((0,), (0,)), ((), ())), preferred_element_type=F32)]
    pallas_call x4 -> x2, Pallas kernels: 72.8 us -> 25.1 us  [exchange_small(): pl.pallas_call(kernel, out_shape=tuple(outputs), in_specs=[vmem] * len(in...]
    convert_element_type x12 -> x2, other arithmetic: 42 us -> 2.05 us  [the longest x1 2.03 us: body(): mix_gain = beside[:, 2:3].T.astype(F32)]
    psum x1, waiting for transfers between devices: 36.8 us -> 0.01 us  [body(): sums = lax.psum(tuple(sums), 'group')]
    ppermute x30, waiting for transfers between devices: 317 us -> 287 us  [chip_shift(): lax.ppermute(block, 'expert', [(i, (i + 2 * step) % ranks) for i in range...]
    reduce_scatter x1, waiting for transfers between devices: 0.01 us -> 13.9 us  [body(): in_sum = lax.psum_scatter(in_term, 'group', scatter_dimension=0, tiled=True)]
    dynamic_slice x19 -> x4, local copies, waits for them, and re-layouts: 12.7 us -> 0.09 us  [body(): lax.dynamic_index_in_dim(part, 1 - core, 0)]
  transfers between devices with their start and end apart: 63 -> 63, of which waited for: 25 -> 25; matrix products, arithmetic and copies ran while one was open for 19% -> 9% of each run, Pallas kernels for 35% -> 43%
where the time goes in v3:
time: 980 us; the launch traced here: 973 us
  Pallas kernels  424 us (43%)
  waiting for transfers between devices  330 us (34%)
  local copies, waits for them, and re-layouts  79.4 us (8%)
  starting transfers between devices  67.3 us (7%)
  other arithmetic  55.8 us (6%)
  between operations  15.4 us (2%)
    ppermute x30, waiting for transfers between devices, chip_shift(): lax.ppermute(block, 'expert', [(i, (i + 2 * step) % ranks) for i in range...  287 us
    pallas_call x2, Pallas kernels, expert_backward(): pl.pallas_call(kernel, out_shape=(jax.ShapeDtypeStruct((count, rows, wide...  54.1 us
    ppermute x30, starting transfers between devices, chip_shift(): lax.ppermute(block, 'expert', [(i, (i + 2 * step) % ranks) for i in range...  46.9 us
    pallas_call x1, Pallas kernels, expert_forward(): pl.pallas_call(kernel, out_shape=(jax.ShapeDtypeStruct((all_slots, width)...  45.8 us
    pallas_call x1, Pallas kernels, attention_backward(): pl.pallas_call(kernel, out_shape=(shape, shape, jax.ShapeDtypeStruct((row...  45.2 us
    pallas_call x5, Pallas kernels, weight_grad(): pl.pallas_call(kernel, out_shape=jax.ShapeDtypeStruct((m, n), BF), grid=(...  39.2 us
    pallas_call x3, Pallas kernels, gather_heads(): pl.pallas_call(kernel, out_shape=jax.ShapeDtypeStruct((ranks * capacity,...  39 us
    pallas_call x4, Pallas kernels, project_in(): pl.pallas_call(kernel, out_shape=shapes, grid_spec=pltpu.PrefetchScalarGr...  38.5 us
  transfers between devices with their start and end apart: 63, of which 25 were waited for; matrix products, arithmetic and copies ran while one was open for 9% of the time, Pallas kernels for 43%

profile of v3, /device:TPU:25, one launch (start us, length us, event | category | flops | bytes accessed | tf_op | source)
XLA Modules:
  0.0 972.7 jit_solution(279648272732342332)
XLA Ops:
  13.5 14.8 %collective-permute-done.1 = bf16[2,64,896]{2,1,0:T(8,128)(2,1)S(1)} collective-permute-done((bf16[2,64,896]{2,1,0:T(8,128)(2,1)S(1)}, bf16[2,64,896]{2,1,0:T(8,128)(2,1)S(1)}, u32[]{:S(2)}, u32[]{:S(2)}) %collective-permute-start.1) | collective-permute-done | bytes 229408 | tf_op jit(solution)/shard_map/ppermute | solution.py:163
  43.8 29.5 %collective-permute-done.3.mine_ref = bf16[384,2048]{1,0:T(8,128)(2,1)S(1)} collective-permute-done((bf16[384,2048]{1,0:T(8,128)(2,1)S(1)}, bf16[384,2048]{1,0:T(8,128)(2,1)S(1)}, u32[]{:S(2)}, u32[]{:S(2)}) %collective-permute-start.3) | collective-permute-done | bytes 1572896 | tf_op jit(solution)/shard_map/ppermute | solution.py:163
  75.6 10.0 %all-gather.3.cloned.1.call-done.w_ref = bf16[2048,896]{1,0:T(8,128)(2,1)} async-done(((bf16[512,896]{1,0:T(8,128)(2,1)}), bf16[2048,896]{1,0:T(8,128)(2,1)}) %all-gather.3.cloned.1.call-update) | async-done | bytes 3670032 | tf_op jit(solution)/shard_map/all_gather | solution.py:1264
  125.3 23.3 %collective-permute-done.8.mine_ref = bf16[384,2048]{1,0:T(8,128)(2,1)S(1)} collective-permute-done((bf16[384,2048]{1,0:T(8,128)(2,1)}, bf16[384,2048]{1,0:T(8,128)(2,1)S(1)}, u32[]{:S(2)}, u32[]{:S(2)}) %collective-permute-start.8) | collective-permute-done | bytes 1572896 | tf_op jit(solution)/shard_map/ppermute | solution.py:163
  163.3 12.8 %exchange_small.2 = (s32[8,8,128]{2,1,0:T(8,128)}, f32[8,2,384]{2,1,0:T(2,128)}) custom-call(s32[8,128]{1,0:T(8,128)} %pad_bitcast_fusion.refs_0_, f32[8,2,384]{2,1,0:T(2,128)} %copy-done.30), custom_call_target="tpu_custom_call" | custom-call | tf_op jit(solution)/shard_map/exchange_small/pallas_call | solution.py:140
  195.3 26.9 %attention_forward.1 = (bf16[3072,256]{1,0:T(8,128)(2,1)S(1)}, f32[2,8,1,384]{3,2,1,0:T(1,128)S(1)}) custom-call(s32[8]{0:T(128)S(1)} %add_select_fusion.1.low_ref, s32[8,1,384]{2,1,0:T(1,128)S(1)} %bitcast.165, bf16[3072,256]{1,0:T(8,128)(2,1)S(1)} %copy-done.16, bf16[3072,256]{1,0:T(8,128)(2,1)S(1)} %copy-done.18, bf16[3072,256]{1,0:T(8,128)(2,1)} %copy-done.3), custom_call_target="tpu_custom_call" | custom-call | flops 35000000 | bytes 65536 | tf_op jit(solution)/shard_map/attention_forward/pallas_call | solution.py:288
  224.4 22.2 %collective-permute-done.11.refs_0_ = bf16[384,2048]{1,0:T(8,128)(2,1)} collective-permute-done((bf16[384,2048]{1,0:T(8,128)(2,1)}, bf16[384,2048]{1,0:T(8,128)(2,1)}, u32[]{:S(2)}, u32[]{:S(2)}) %collective-permute-start.11) | collective-permute-done | bytes 1572896 | tf_op jit(solution)/shard_map/ppermute | solution.py:163
  247.1 34.9 %collective-permute-done.12.mine_ref.refs_2_ = bf16[3072,256]{1,0:T(8,128)(2,1)} collective-permute-done((bf16[3072,256]{1,0:T(8,128)(2,1)S(1)}, bf16[3072,256]{1,0:T(8,128)(2,1)}, u32[]{:S(2)}, u32[]{:S(2)}) %collective-permute-start.12) | collective-permute-done | bytes 1572896 | tf_op jit(solution)/shard_map/ppermute | solution.py:163
  291.5 14.0 %gather_heads.3.base_ref = f32[1536,2048]{1,0:T(8,128)} custom-call(s32[2]{0:T(128)S(1)} %pad_add_fusion.2.at_ref, bf16[3072,2048]{1,0:T(8,128)(2,1)} %get-tuple-element.356.base_ref, bf16[8,192,384]{2,1,0:T(8,128)(2,1)S(1)} %fusion.12.pick_ref, bf16[3072,256]{1,0:T(8,128)(2,1)S(1)} %get-tuple-element.436.mine_ref.refs_0_.o_ref, ...), custom_call_target="tpu_custom_call" | custom-call | flops 8000000 | bytes 65536 | tf_op jit(solution)/shard_map/gather_heads/pallas_call | solution.py:444
  305.6 12.6 %collective-permute-done.14.mine_ref.refs_4_ = bf16[3072,256]{1,0:T(8,128)(2,1)} collective-permute-done((bf16[3072,256]{1,0:T(8,128)(2,1)}, bf16[3072,256]{1,0:T(8,128)(2,1)}, u32[]{:S(2)}, u32[]{:S(2)}) %collective-permute-start.14) | collective-permute-done | bytes 1572896 | tf_op jit(solution)/shard_map/ppermute | solution.py:163
  324.2 12.6 %gather_heads.4.base_ref = f32[1536,2048]{1,0:T(8,128)} custom-call(s32[2]{0:T(128)S(1)} %pad_add_fusion.at_ref, f32[1536,2048]{1,0:T(8,128)} %gather_heads.3.base_ref, bf16[8,192,384]{2,1,0:T(8,128)(2,1)S(1)} %fusion.12.pick_ref, bf16[3072,256]{1,0:T(8,128)(2,1)} %collective-permute-done.12.mine_ref.refs_2_, ...), custom_call_target="tpu_custom_call", output_to_operand_aliasing={{}: (1, {})} | custom-call | flops 8000000 | bytes 65536 | tf_op jit(solution)/shard_map/gather_heads/pallas_call | solution.py:444
  336.9 12.4 %gather_heads.5.base_ref = f32[1536,2048]{1,0:T(8,128)} custom-call(s32[2]{0:T(128)S(1)} %pad_add_fusion.3.at_ref, f32[1536,2048]{1,0:T(8,128)} %gather_heads.4.base_ref, bf16[8,192,384]{2,1,0:T(8,128)(2,1)S(1)} %fusion.12.pick_ref, bf16[3072,256]{1,0:T(8,128)(2,1)} %collective-permute-done.14.mine_ref.refs_4_, ...), custom_call_target="tpu_custom_call", output_to_operand_aliasing={{}: (1, {})} | custom-call | flops 8000000 | bytes 65536 | tf_op jit(solution)/shard_map/gather_heads/pallas_call | solution.py:444
  369.5 45.8 %expert_forward.1 = (bf16[1536,2048]{1,0:T(8,128)(2,1)}, f32[1536,128]{1,0:T(8,128)}, f32[1536,1024]{1,0:T(8,128)}, f32[1536,1024]{1,0:T(8,128)}, bf16[1536,1024...) custom-call(s32[10]{0:T(128)} %stack.122.order_ref, ...), custom_call_target="tpu_custom_call" | custom-call | flops 45000000 | bytes 65536 | tf_op jit(solution)/shard_map/expert_forward/pallas_call | solution.py:559
  415.3 17.9 %expert_backward.2 = (bf16[1,384,2176]{2,1,0:T(8,128)(2,1)}, bf16[1,384,2176]{2,1,0:T(8,128)(2,1)}, bf16[1536,2048]{1,0:T(8,128)(2,1)}, bf16[1536,1024]{1,0:T(8,128)(2,1)}, bf16[1536,1024]{1,0:T(8,128)(2,1)}) custom-call(s32[3]{0:T(128)} %pad_add_fusion.4.at_ref, bf16[8,192,384]{2,1,0:T(8,128)(2,1)} %copy-done.2, bf16[8,384,192]{2,1,0:T(8,128)(2,1)} %fusion.11.turned_ref, ...), custom_call_target="tpu_custom_call" | custom-call | flops 12000000 | bytes 65536 | tf_op jit(solution)/shard_map/expert_backward/pallas_call | solution.py:700
  447.0 36.1 %expert_backward.3 = (bf16[3,384,2176]{2,1,0:T(8,128)(2,1)}, bf16[3,384,2176]{2,1,0:T(8,128)(2,1)}, bf16[1536,2048]{1,0:T(8,128)(2,1)}, bf16[1536,1024]{1,0:T(8,128)(2,1)}, bf16[1536,1024]{1,0:T(8,128)(2,1)}) custom-call(s32[5]{0:T(128)} %stack.123.at_ref, ...), custom_call_target="tpu_custom_call", output_to_operand_aliasing={{2}: (16, {}), {3}: (17, {}), {4}: (18, {})} | custom-call | flops 36000000 | bytes 65536 | tf_op jit(solution)/shard_map/expert_backward/pallas_call | solution.py:700
  507.6 10.3 %weight_grad.7 = bf16[2048,1024]{1,0:T(8,128)(2,1)} custom-call(bf16[1536,2048]{1,0:T(8,128)(2,1)} %get-tuple-element.421.a_ref, bf16[1536,1024]{1,0:T(8,128)(2,1)S(1)} %copy-done.11), custom_call_target="tpu_custom_call" | custom-call | flops 10000000 | bytes 65536 | tf_op jit(solution)/shard_map/weight_grad/pallas_call | solution.py:1073
  517.9 9.9 %weight_grad.6 = bf16[2048,1024]{1,0:T(8,128)(2,1)} custom-call(bf16[1536,2048]{1,0:T(8,128)(2,1)} %get-tuple-element.421.a_ref, bf16[1536,1024]{1,0:T(8,128)(2,1)S(1)} %copy-done.10), custom_call_target="tpu_custom_call" | custom-call | flops 10000000 | bytes 65536 | tf_op jit(solution)/shard_map/weight_grad/pallas_call | solution.py:1073
  527.8 11.2 %weight_grad.5 = bf16[1024,2048]{1,0:T(8,128)(2,1)} custom-call(bf16[1536,1024]{1,0:T(8,128)(2,1)S(1)} %copy-done.23, bf16[1536,2048]{1,0:T(8,128)(2,1)} %get-tuple-element.420.b_ref), custom_call_target="tpu_custom_call" | custom-call | flops 10000000 | bytes 65536 | tf_op jit(solution)/shard_map/weight_grad/pallas_call | solution.py:1073
  547.7 11.1 %own_forward.1 = (bf16[384,2048]{1,0:T(8,128)(2,1)S(1)}, f32[384,2048]{1,0:T(8,128)}, bf16[384,2048]{1,0:T(8,128)(2,1)S(1)}, f32[384,128]{1,0:T(8,128)S(1)}, f32[384,128]{1,0:T(8,128)S(1)}) custom-call(s32[9]{0:T(128)S(1)} %stack.132.at_ref, bf16[3072,256]{1,0:T(8,128)(2,1)S(1)} %get-tuple-element.436.mine_ref.refs_0_.o_ref, bf16[3072,256]{1,0:T(8,128)(2,1)} %copy-done.13, ...), custom_call_target="tpu_custom_call" | custom-call | flops 10000000 | bytes 65536 | tf_op jit(solution)/shard_map/own_forward/pallas_call | solution.py:1153
  566.5 15.1 %collective-permute-done.31.arrived_ref = bf16[384,2176]{1,0:T(8,128)(2,1)} collective-permute-done((bf16[384,2176]{1,0:T(8,128)(2,1)}, bf16[384,2176]{1,0:T(8,128)(2,1)}, u32[]{:S(2)}, u32[]{:S(2)}) %collective-permute-start.31) | collective-permute-done | bytes 1671200 | tf_op jit(solution)/shard_map/ppermute | solution.py:163
  583.3 14.9 %owner_backward.1 = (bf16[384,128]{1,0:T(8,128)(2,1)S(1)}, f32[8,2048]{1,0:T(8,128)S(1)}, f32[384,2048]{1,0:T(8,128)}, bf16[384,2048]{1,0:T(8,128)(2,1)S(1)}, bf16[8,384,256]{2,1,0:T(8,128)(2,1)S(1)}) custom-call(bf16[384,2176]{1,0:T(8,128)(2,1)} %collective-permute-done.31.arrived_ref, bf16[3,384,2176]{2,1,0:T(8,128)(2,1)} %get-tuple-element.425.refs_1_.mine_ref, ...), custom_call_target="tpu_custom_call" | custom-call | flops 14000000 | bytes 65536 | tf_op jit(solution)/shard_map/owner_backward/pallas_call | solution.py:824
  615.3 10.5 %collective-permute-done.33 = bf16[2,384,256]{2,1,0:T(8,128)(2,1)} collective-permute-done((bf16[2,384,256]{2,1,0:T(8,128)(2,1)}, bf16[2,384,256]{2,1,0:T(8,128)(2,1)}, u32[]{:S(2)}, u32[]{:S(2)}) %collective-permute-start.33) | collective-permute-done | bytes 393248 | tf_op jit(solution)/shard_map/ppermute | solution.py:163
  625.8 23.8 %collective-permute-done.34 = bf16[2,384,256]{2,1,0:T(8,128)(2,1)} collective-permute-done((bf16[2,384,256]{2,1,0:T(8,128)(2,1)}, bf16[2,384,256]{2,1,0:T(8,128)(2,1)}, u32[]{:S(2)}, u32[]{:S(2)}) %collective-permute-start.34) | collective-permute-done | bytes 393248 | tf_op jit(solution)/shard_map/ppermute | solution.py:163
  667.0 45.2 %attention_backward.1 = (f32[3072,256]{1,0:T(8,128)}, f32[3072,256]{1,0:T(8,128)}, bf16[3072,256]{1,0:T(8,128)(2,1)S(1)}, f32[2,8,1,384]{3,2,1,0:T(1,128)S(1)}, f32[2,8,1,384]{3,2,1,0:T(1,128)S(1)}) custom-call(s32[8]{0:T(128)S(1)} %add_select_fusion.high_ref, s32[8,1,384]{2,1,0:T(1,128)S(1)} %bitcast.166, bf16[3072,256]{1,0:T(8,128)(2,1)S(1)} %copy-done.17, ...), custom_call_target="tpu_custom_call" | custom-call | flops 46000000 | bytes 65536 | tf_op jit(solution)/shard_map/attention_backward/pallas_call | solution.py:392
  718.0 12.3 %exchange_small.3.m_ref = f32[8,2,384]{2,1,0:T(2,128)} custom-call(f32[8,2,384]{2,1,0:T(2,128)} %pad_maximum_fusion.6.refs_0_), custom_call_target="tpu_custom_call" | custom-call | tf_op jit(solution)/shard_map/exchange_small/pallas_call | solution.py:140
  750.8 15.2 %project_back.3 = (bf16[3072,768]{1,0:T(8,128)(2,1)}, bf16[3,384,2048]{2,1,0:T(8,128)(2,1)}, bf16[3,384,2048]{2,1,0:T(8,128)(2,1)}, f32[8,256]{1,0:T(8,128)S(1)}) custom-call(s32[4]{0:T(128)S(1)} %pad_add_fusion.5.at_ref, f32[3072,512]{1,0:T(8,128)} %get-tuple-element.337.p_ref, f32[8,2,384]{2,1,0:T(2,128)S(1)} %copy-done.33, ...), custom_call_target="tpu_custom_call", output_to_operand_aliasing={{0}: (11, {})} | custom-call | flops 24000000 | bytes 65536 | tf_op jit(solution)/shard_map/project_back/pallas_call | solution.py:1006
  766.1 14.9 %in_weight_grad.1 = bf16[2048,896]{1,0:T(8,128)(2,1)S(1)} custom-call(bf16[3072,2048]{1,0:T(8,128)(2,1)} %get-tuple-element.502.a_ref, bf16[3072,768]{1,0:T(8,128)(2,1)} %get-tuple-element.503.b_ref, bf16[384,2048]{1,0:T(8,128)(2,1)S(1)} %copy-done.29, bf16[384,128]{1,0:T(8,128)(2,1)S(1)} %get-tuple-element.505.l_ref, f32[8,2048]{1,0:T(8,128)S(1)} %maximum_maximum_fusion.r_ref), custom_call_target="tpu_custom_call" | custom-call | flops 14000000 | bytes 65536 | tf_op jit(solution)/shard_map/in_weight_grad/pallas_call | solution.py:1106
  782.8 27.8 %collective-permute-done.44 = bf16[384,2048]{1,0:T(8,128)(2,1)} collective-permute-done((bf16[384,2048]{1,0:T(8,128)(2,1)}, bf16[384,2048]{1,0:T(8,128)(2,1)}, u32[]{:S(2)}, u32[]{:S(2)}) %collective-permute-start.44) | collective-permute-done | bytes 1572896 | tf_op jit(solution)/shard_map/ppermute | solution.py:163
  846.1 19.8 %collective-permute-done.47 = bf16[384,2048]{1,0:T(8,128)(2,1)S(1)} collective-permute-done((bf16[384,2048]{1,0:T(8,128)(2,1)S(1)}, bf16[384,2048]{1,0:T(8,128)(2,1)S(1)}, u32[]{:S(2)}, u32[]{:S(2)}) %collective-permute-start.47) | collective-permute-done | bytes 1572896 | tf_op jit(solution)/shard_map/ppermute | solution.py:163
  885.5 21.6 %collective-permute-done.53 = bf16[384,2048]{1,0:T(8,128)(2,1)} collective-permute-done((bf16[384,2048]{1,0:T(8,128)(2,1)}, bf16[384,2048]{1,0:T(8,128)(2,1)}, u32[]{:S(2)}, u32[]{:S(2)}) %collective-permute-start.53) | collective-permute-done | bytes 1572896 | tf_op jit(solution)/shard_map/ppermute | solution.py:163
  907.2 13.9 %reduce-scatter.5.cloned.1.call-done = bf16[512,896]{1,0:T(8,128)(2,1)} async-done(((bf16[2048,896]{1,0:T(8,128)(2,1)}), bf16[512,896]{1,0:T(8,128)(2,1)}) %reduce-scatter.5.cloned.1.call-update) | async-done | bytes 917520 | tf_op jit(solution)/shard_map/reduce_scatter | solution.py:1525
  945.4 10.7 %collective-permute-done.55 = bf16[2,64,896]{2,1,0:T(8,128)(2,1)S(1)} collective-permute-done((bf16[2,64,896]{2,1,0:T(8,128)(2,1)S(1)}, bf16[2,64,896]{2,1,0:T(8,128)(2,1)S(1)}, u32[]{:S(2)}, u32[]{:S(2)}) %collective-permute-start.55) | collective-permute-done | bytes 229408 | tf_op jit(solution)/shard_map/ppermute | solution.py:163
  (410 shorter events, 343.2 us)
Async XLA Ops:
  7.2 78.5 %all-gather.3.cloned.1.call-start = ((), (), s32[]{:S(2)}) async-start(), calls=%async_computation.2 | async-start | bytes 4587520 | tf_op jit(solution)/shard_map/all_gather | solution.py:1264
  32.8 254.0 %all-gather.5.cloned.1.call-start = ((), (), s32[]{:S(2)}) async-start(), calls=%async_computation.3 | async-start | bytes 8650752 | tf_op jit(solution)/shard_map/all_gather | solution.py:1293
  33.8 39.5 %collective-permute-start.3 = (bf16[384,2048]{1,0:T(8,128)(2,1)S(1)}, bf16[384,2048]{1,0:T(8,128)(2,1)S(1)}, u32[]{:S(2)}, u32[]{:S(2)}) collective-permute-start(bf16[384,2048]{1,0:T(8,128)(2,1)S(1)} %copy-done.4), channel_id=1, source_target_pairs={{0,2},{1,3},{2,4},{3,5},{4,6},{5,7},{6,0},{7,1},{8,10},{9,11},{10,... | collective-permute-start | bytes 4718600 | tf_op jit(solution)/shard_map/ppermute | solution.py:163
  34.7 38.6 %collective-permute-start.4 = (bf16[384,2048]{1,0:T(8,128)(2,1)S(1)}, bf16[384,2048]{1,0:T(8,128)(2,1)S(1)}, u32[]{:S(2)}, u32[]{:S(2)}) collective-permute-start(bf16[384,2048]{1,0:T(8,128)(2,1)S(1)} %copy-done.4), channel_id=1, source_target_pairs={{0,1},{1,0},{2,3},{3,2},{4,5},{5,4},{6,7},{7,6},{8,9},{9,8},{10,11... | collective-permute-start | bytes 4718600 | tf_op jit(solution)/shard_map/ppermute | solution.py:158
  148.6 662.0 %all-reduce.6.cloned.1.call-start = ((), (), s32[]{:S(2)}) async-start(), calls=%async_computation.6 | async-start | bytes 25165824 | tf_op jit(solution)/shard_map/psum | solution.py:1410
  176.1 70.4 %collective-permute-start.11 = (bf16[384,2048]{1,0:T(8,128)(2,1)}, bf16[384,2048]{1,0:T(8,128)(2,1)}, u32[]{:S(2)}, u32[]{:S(2)}) collective-permute-start(bf16[384,2048]{1,0:T(8,128)(2,1)} %cot_ref.1), channel_id=1, source_target_pairs={{0,2},{1,3},{2,4},{3,5},{4,6},{5,7},{6,0},{7,1},{8,10},{9,11},{10,... | collective-permute-start | bytes 4718600 | tf_op jit(solution)/shard_map/ppermute | solution.py:163
  320.3 38.1 %collective-permute-start.16 = (bf16[3072,256]{1,0:T(8,128)(2,1)}, bf16[3072,256]{1,0:T(8,128)(2,1)}, u32[]{:S(2)}, u32[]{:S(2)}) collective-permute-start(bf16[3072,256]{1,0:T(8,128)(2,1)} %collective-permute-done.14.mine_ref.refs_4_), channel_id=1, source_target_pairs={{0,2},{1,3},{2,4},{3,5},{4,6},{5,7},{6,0},{7,1},{8,10},{9,11},{10,... | collective-permute-start | bytes 4718600 | tf_op jit(solution)/shard_map/ppermute | solution.py:163
  359.2 56.1 %collective-permute-start.21 = (bf16[384,2048]{1,0:T(8,128)(2,1)}, bf16[384,2048]{1,0:T(8,128)(2,1)}, u32[]{:S(2)}, u32[]{:S(2)}) collective-permute-start(bf16[384,2048]{1,0:T(8,128)(2,1)} %collective-permute-done.11.refs_0_), channel_id=1, source_target_pairs={{0,1},{1,0},{2,3},{3,2},{4,5},{5,4},{6,7},{7,6},{8,9},{9,8},{10,11... | collective-permute-start | bytes 4718600 | tf_op jit(solution)/shard_map/ppermute | solution.py:158
  359.2 74.1 %collective-permute-start.18 = (bf16[384,2048]{1,0:T(8,128)(2,1)}, bf16[384,2048]{1,0:T(8,128)(2,1)}, u32[]{:S(2)}, u32[]{:S(2)}) collective-permute-start(bf16[384,2048]{1,0:T(8,128)(2,1)} %collective-permute-done.11.refs_0_), channel_id=1, source_target_pairs={{0,2},{1,3},{2,4},{3,5},{4,6},{5,7},{6,0},{7,1},{8,10},{9,11},{10,... | collective-permute-start | bytes 4718600 | tf_op jit(solution)/shard_map/ppermute | solution.py:163
  363.2 70.1 %collective-permute-start.19 = (bf16[384,2048]{1,0:T(8,128)(2,1)}, bf16[384,2048]{1,0:T(8,128)(2,1)}, u32[]{:S(2)}, u32[]{:S(2)}) collective-permute-start(bf16[384,2048]{1,0:T(8,128)(2,1)} %cot_ref.1), channel_id=1, source_target_pairs={{0,6},{1,7},{2,0},{3,1},{4,2},{5,3},{6,4},{7,5},{8,14},{9,15},{10,... | collective-permute-start | bytes 4718600 | tf_op jit(solution)/shard_map/ppermute | solution.py:163
  363.6 69.6 %collective-permute-start.20 = (bf16[384,2048]{1,0:T(8,128)(2,1)}, bf16[384,2048]{1,0:T(8,128)(2,1)}, u32[]{:S(2)}, u32[]{:S(2)}) collective-permute-start(bf16[384,2048]{1,0:T(8,128)(2,1)} %cot_ref.1), channel_id=1, source_target_pairs={{0,1},{1,0},{2,3},{3,2},{4,5},{5,4},{6,7},{7,6},{8,9},{9,8},{10,11... | collective-permute-start | bytes 4718600 | tf_op jit(solution)/shard_map/ppermute | solution.py:158
  443.0 40.2 %collective-permute-start.26 = (bf16[384,2176]{1,0:T(8,128)(2,1)}, bf16[384,2176]{1,0:T(8,128)(2,1)S(1)}, u32[]{:S(2)}, u32[]{:S(2)}) collective-permute-start(bf16[384,2176]{1,0:T(8,128)(2,1)} %add_rows.10), channel_id=1, source_target_pairs={{0,2},{1,3},{2,4},{3,5},{4,6},{5,7},{6,0},{7,1},{8,10},{9,11},{10,... | collective-permute-start | bytes 5013512 | tf_op jit(solution)/shard_map/ppermute | solution.py:163
  496.7 42.2 %collective-permute-start.29 = (bf16[384,2176]{1,0:T(8,128)(2,1)}, bf16[384,2176]{1,0:T(8,128)(2,1)}, u32[]{:S(2)}, u32[]{:S(2)}) collective-permute-start(bf16[384,2176]{1,0:T(8,128)(2,1)} %get-tuple-element.611), channel_id=1, source_target_pairs={{0,1},{1,0},{2,3},{3,2},{4,5},{5,4},{6,7},{7,6},{8,9},{9,8},{10,11... | collective-permute-start | bytes 5013512 | tf_op jit(solution)/shard_map/ppermute | solution.py:158
  497.1 41.9 %collective-permute-start.30 = (bf16[384,2176]{1,0:T(8,128)(2,1)}, bf16[384,2176]{1,0:T(8,128)(2,1)S(1)}, u32[]{:S(2)}, u32[]{:S(2)}) collective-permute-start(bf16[384,2176]{1,0:T(8,128)(2,1)} %get-tuple-element.610), channel_id=1, source_target_pairs={{0,1},{1,0},{2,3},{3,2},{4,5},{5,4},{6,7},{7,6},{8,9},{9,8},{10,11... | collective-permute-start | bytes 5013512 | tf_op jit(solution)/shard_map/ppermute | solution.py:158
  497.2 41.7 %collective-permute-start.28 = (bf16[384,2176]{1,0:T(8,128)(2,1)}, bf16[384,2176]{1,0:T(8,128)(2,1)}, u32[]{:S(2)}, u32[]{:S(2)}) collective-permute-start(bf16[384,2176]{1,0:T(8,128)(2,1)} %add_rows.11), channel_id=1, source_target_pairs={{0,2},{1,3},{2,4},{3,5},{4,6},{5,7},{6,0},{7,1},{8,10},{9,11},{10,... | collective-permute-start | bytes 5013512 | tf_op jit(solution)/shard_map/ppermute | solution.py:163
  507.0 37.6 %collective-permute-start.32 = (bf16[384,2048]{1,0:T(8,128)(2,1)}, bf16[384,2048]{1,0:T(8,128)(2,1)}, u32[]{:S(2)}, u32[]{:S(2)}) collective-permute-start(bf16[384,2048]{1,0:T(8,128)(2,1)} %get-tuple-element.609), channel_id=1, source_target_pairs={{0,1},{1,0},{2,3},{3,2},{4,5},{5,4},{6,7},{7,6},{8,9},{9,8},{10,11... | collective-permute-start | bytes 4718600 | tf_op jit(solution)/shard_map/ppermute | solution.py:158
  543.2 38.4 %collective-permute-start.31 = (bf16[384,2176]{1,0:T(8,128)(2,1)}, bf16[384,2176]{1,0:T(8,128)(2,1)}, u32[]{:S(2)}, u32[]{:S(2)}) collective-permute-start(bf16[384,2176]{1,0:T(8,128)(2,1)} %add_rows.12), channel_id=1, source_target_pairs={{0,2},{1,3},{2,4},{3,5},{4,6},{5,7},{6,0},{7,1},{8,10},{9,11},{10,... | collective-permute-start | bytes 5013512 | tf_op jit(solution)/shard_map/ppermute | solution.py:163
  544.4 330.3 %reduce-scatter.3.cloned.1.call-start = ((), (), s32[]{:S(2)}) async-start(), calls=%async_computation.4 | async-start | bytes 5242880 | tf_op jit(solution)/shard_map/reduce_scatter | solution.py:1516
  581.6 68.1 %collective-permute-start.36 = (bf16[384,2048]{1,0:T(8,128)(2,1)}, bf16[384,2048]{1,0:T(8,128)(2,1)}, u32[]{:S(2)}, u32[]{:S(2)}) collective-permute-start(bf16[384,2048]{1,0:T(8,128)(2,1)} %add_rows.13), channel_id=1, source_target_pairs={{0,2},{1,3},{2,4},{3,5},{4,6},{5,7},{6,0},{7,1},{8,10},{9,11},{10,... | collective-permute-start | bytes 4718600 | tf_op jit(solution)/shard_map/ppermute | solution.py:163
  599.9 49.8 %collective-permute-start.34 = (bf16[2,384,256]{2,1,0:T(8,128)(2,1)}, bf16[2,384,256]{2,1,0:T(8,128)(2,1)}, u32[]{:S(2)}, u32[]{:S(2)}) collective-permute-start(bf16[2,384,256]{2,1,0:T(8,128)(2,1)} %get-tuple-element.460), channel_id=1, source_target_pairs={{0,4},{1,5},{2,6},{3,7},{4,0},{5,1},{6,2},{7,3},{8,12},{9,13},{10,... | collective-permute-start | bytes 1179656 | tf_op jit(solution)/shard_map/ppermute | solution.py:163
  600.5 49.2 %collective-permute-start.35 = (bf16[2,384,256]{2,1,0:T(8,128)(2,1)}, bf16[2,384,256]{2,1,0:T(8,128)(2,1)}, u32[]{:S(2)}, u32[]{:S(2)}) collective-permute-start(bf16[2,384,256]{2,1,0:T(8,128)(2,1)} %get-tuple-element.461), channel_id=1, source_target_pairs={{0,6},{1,7},{2,0},{3,1},{4,2},{5,3},{6,4},{7,5},{8,14},{9,15},{10,... | collective-permute-start | bytes 1179656 | tf_op jit(solution)/shard_map/ppermute | solution.py:163
  601.3 54.2 %collective-permute-start.37 = (bf16[384,2048]{1,0:T(8,128)(2,1)}, bf16[384,2048]{1,0:T(8,128)(2,1)}, u32[]{:S(2)}, u32[]{:S(2)}) collective-permute-start(bf16[384,2048]{1,0:T(8,128)(2,1)} %get-tuple-element.608), channel_id=1, source_target_pairs={{0,1},{1,0},{2,3},{3,2},{4,5},{5,4},{6,7},{7,6},{8,9},{9,8},{10,11... | collective-permute-start | bytes 4718600 | tf_op jit(solution)/shard_map/ppermute | solution.py:158
  665.8 47.7 %collective-permute-start.42 = (bf16[1024,2048]{1,0:T(8,128)(2,1)}, bf16[1024,2048]{1,0:T(8,128)(2,1)}, u32[]{:S(2)}, u32[]{:S(2)}) collective-permute-start(bf16[1024,2048]{1,0:T(8,128)(2,1)} %weight_grad.9), channel_id=1, source_target_pairs={{0,1},{1,0},{2,3},{3,2},{4,5},{5,4},{6,7},{7,6},{8,9},{9,8},{10,11... | collective-permute-start | bytes 12582920 | tf_op jit(solution)/shard_map/ppermute | solution.py:158
  665.9 47.6 %collective-permute-start.40 = (bf16[384,2048]{1,0:T(8,128)(2,1)}, bf16[384,2048]{1,0:T(8,128)(2,1)}, u32[]{:S(2)}, u32[]{:S(2)}) collective-permute-start(bf16[384,2048]{1,0:T(8,128)(2,1)} %get-tuple-element.607), channel_id=1, source_target_pairs={{0,1},{1,0},{2,3},{3,2},{4,5},{5,4},{6,7},{7,6},{8,9},{9,8},{10,11... | collective-permute-start | bytes 4718600 | tf_op jit(solution)/shard_map/ppermute | solution.py:158
  666.4 47.1 %collective-permute-start.41 = (bf16[384,2048]{1,0:T(8,128)(2,1)}, bf16[384,2048]{1,0:T(8,128)(2,1)}, u32[]{:S(2)}, u32[]{:S(2)}) collective-permute-start(bf16[384,2048]{1,0:T(8,128)(2,1)} %get-tuple-element.606), channel_id=1, source_target_pairs={{0,1},{1,0},{2,3},{3,2},{4,5},{5,4},{6,7},{7,6},{8,9},{9,8},{10,11... | collective-permute-start | bytes 4718600 | tf_op jit(solution)/shard_map/ppermute | solution.py:158
  666.5 47.0 %collective-permute-start.39 = (bf16[384,2048]{1,0:T(8,128)(2,1)}, bf16[384,2048]{1,0:T(8,128)(2,1)}, u32[]{:S(2)}, u32[]{:S(2)}) collective-permute-start(bf16[384,2048]{1,0:T(8,128)(2,1)} %add_rows.14), channel_id=1, source_target_pairs={{0,2},{1,3},{2,4},{3,5},{4,6},{5,7},{6,0},{7,1},{8,10},{9,11},{10,... | collective-permute-start | bytes 4718600 | tf_op jit(solution)/shard_map/ppermute | solution.py:163
  740.6 42.2 %collective-permute-start.45 = (bf16[384,2048]{1,0:T(8,128)(2,1)}, bf16[384,2048]{1,0:T(8,128)(2,1)}, u32[]{:S(2)}, u32[]{:S(2)}) collective-permute-start(bf16[384,2048]{1,0:T(8,128)(2,1)} %add_rows.15), channel_id=1, source_target_pairs={{0,2},{1,3},{2,4},{3,5},{4,6},{5,7},{6,0},{7,1},{8,10},{9,11},{10,... | collective-permute-start | bytes 4718600 | tf_op jit(solution)/shard_map/ppermute | solution.py:163
  748.0 62.6 %collective-permute-start.44 = (bf16[384,2048]{1,0:T(8,128)(2,1)}, bf16[384,2048]{1,0:T(8,128)(2,1)}, u32[]{:S(2)}, u32[]{:S(2)}) collective-permute-start(bf16[384,2048]{1,0:T(8,128)(2,1)} %add_rows.16), channel_id=1, source_target_pairs={{0,2},{1,3},{2,4},{3,5},{4,6},{5,7},{6,0},{7,1},{8,10},{9,11},{10,... | collective-permute-start | bytes 4718600 | tf_op jit(solution)/shard_map/ppermute | solution.py:163
  815.9 105.1 %reduce-scatter.5.cloned.1.call-start = ((), (), s32[]{:S(2)}) async-start(), calls=%async_computation.5 | async-start | bytes 4587520 | tf_op jit(solution)/shard_map/reduce_scatter | solution.py:1525
  876.9 44.2 %collective-permute-start.50 = (bf16[64,2048]{1,0:T(8,128)(2,1)}, bf16[64,2048]{1,0:T(8,128)(2,1)}, u32[]{:S(2)}, u32[]{:S(2)}) collective-permute-start(bf16[64,2048]{1,0:T(8,128)(2,1)} %get-tuple-element.622), channel_id=1, source_target_pairs={{0,2},{1,3},{2,4},{3,5},{4,6},{5,7},{6,0},{7,1},{8,10},{9,11},{10,... | collective-permute-start | bytes 786440 | tf_op jit(solution)/shard_map/ppermute | solution.py:163
  876.9 51.1 %collective-permute-start.51 = (bf16[64,2048]{1,0:T(8,128)(2,1)}, bf16[64,2048]{1,0:T(8,128)(2,1)}, u32[]{:S(2)}, u32[]{:S(2)}) collective-permute-start(bf16[64,2048]{1,0:T(8,128)(2,1)} %get-tuple-element.621), channel_id=1, source_target_pairs={{0,4},{1,5},{2,6},{3,7},{4,0},{5,1},{6,2},{7,3},{8,12},{9,13},{10,... | collective-permute-start | bytes 786440 | tf_op jit(solution)/shard_map/ppermute | solution.py:163
  876.9 51.1 %collective-permute-start.52 = (bf16[64,2048]{1,0:T(8,128)(2,1)}, bf16[64,2048]{1,0:T(8,128)(2,1)}, u32[]{:S(2)}, u32[]{:S(2)}) collective-permute-start(bf16[64,2048]{1,0:T(8,128)(2,1)} %get-tuple-element.620), channel_id=1, source_target_pairs={{0,6},{1,7},{2,0},{3,1},{4,2},{5,3},{6,4},{7,5},{8,14},{9,15},{10,... | collective-permute-start | bytes 786440 | tf_op jit(solution)/shard_map/ppermute | solution.py:163
  (98 other events, 1061.9 us)
Sparse Core Ops, SparseCore 0:
  32.9 52.7 all-gather.2
  148.7 99.1 all-gather.4
  544.6 242.3 all-reduce.5
  816.0 53.4 reduce-scatter.2
  872.6 48.3 reduce-scatter.4

commit v4 on v3

--- a/solution.py
+++ b/solution.py
@@ -1237,7 +1237,7 @@
     columns = width // ranks
     shard = query_weight.shape[0]
     experts = router_weight.shape[1]
-    block = rows
+    block = 512 if all_rows % 512 == 0 else rows
     blocks = all_rows // block
     heads = columns // HEAD_DIM
 
@@ -1298,11 +1298,14 @@
         .set(routes.T.reshape(-1))
         .reshape(8, 128)
     )
-    all_routes, squares = exchange_small(2, group=packed_routes, added=squares)
     beside = in_weight[:, 3 * columns :]
     my_gains = lax.dynamic_slice_in_dim(beside, me * columns, columns, 0)[:, :2].T.astype(F32)
     mix_gain = beside[:, 2:3].T.astype(F32)
     router = jnp.pad(beside[:, 3 : 3 + experts].T, ((0, 128 - experts), (0, 0)))
+    squares, packed_routes, my_gains, mix_gain, router = tie(
+        squares, packed_routes, my_gains, mix_gain, router
+    )
+    all_routes, squares = exchange_small(2, group=packed_routes, added=squares)
     queries, keys = make_heads(products, squares, my_gains, cosine, sine, width)
 
     all_routes = all_routes.reshape(ranks, -1)[:, : rows * TOP].reshape(ranks, TOP, rows)
@@ -1477,7 +1480,7 @@
     )
     out_moving = add_rows(out_moving, (out_own, 3), out_swapped[0])
     partials = jnp.stack(
-        [jnp.sum(query_part[:, :, 0], axis=0), jnp.sum(key_part[:, :, 0], axis=0)], axis=1
+        [jnp.sum(part, axis=0).reshape(ranks, rows) for part in (query_part, key_part)], axis=1
     )
     partials, out_moving = tie(partials, out_moving)
     (means,) = exchange_small(3, added=partials)

time: 980 us -> 975 us (level)
    unnamed x138 -> x136, local copies, waits for them, and re-layouts: 33.2 us -> 34 us
  transfers between devices with their start and end apart: 63 -> 63, of which waited for: 25 -> 24; matrix products, arithmetic and copies ran while one was open for 9% -> 9% of each run, Pallas kernels for 43% -> 42%
where the time goes in v4:
time: 975 us; the launch traced here: 968 us
  Pallas kernels  420 us (43%)
  waiting for transfers between devices  328 us (34%)
  local copies, waits for them, and re-layouts  80.8 us (8%)
  starting transfers between devices  68.3 us (7%)
  other arithmetic  55.3 us (6%)
  between operations  15.1 us (2%)
    ppermute x30, waiting for transfers between devices, chip_shift(): lax.ppermute(block, 'expert', [(i, (i + 2 * step) % ranks) for i in range...  287 us
    pallas_call x2, Pallas kernels, expert_backward(): pl.pallas_call(kernel, out_shape=(jax.ShapeDtypeStruct((count, rows, wide...  54.3 us
    ppermute x30, starting transfers between devices, chip_shift(): lax.ppermute(block, 'expert', [(i, (i + 2 * step) % ranks) for i in range...  47.4 us
    pallas_call x1, Pallas kernels, expert_forward(): pl.pallas_call(kernel, out_shape=(jax.ShapeDtypeStruct((all_slots, width)...  45.9 us
    pallas_call x1, Pallas kernels, attention_backward(): pl.pallas_call(kernel, out_shape=(shape, shape, jax.ShapeDtypeStruct((row...  41.4 us
    pallas_call x5, Pallas kernels, weight_grad(): pl.pallas_call(kernel, out_shape=jax.ShapeDtypeStruct((m, n), BF), grid=(...  39 us
    pallas_call x3, Pallas kernels, gather_heads(): pl.pallas_call(kernel, out_shape=jax.ShapeDtypeStruct((ranks * capacity,...  39 us
    pallas_call x4, Pallas kernels, project_in(): pl.pallas_call(kernel, out_shape=shapes, grid_spec=pltpu.PrefetchScalarGr...  38.5 us
  transfers between devices with their start and end apart: 63, of which 24 were waited for; matrix products, arithmetic and copies ran while one was open for 9% of the time, Pallas kernels for 42%

profile of v4, /device:TPU:25, one launch (start us, length us, event | category | flops | bytes accessed | tf_op | source)
XLA Modules:
  0.0 967.9 jit_solution(17035383078746904085)
XLA Ops:
  13.5 14.8 %collective-permute-done.1 = bf16[2,64,896]{2,1,0:T(8,128)(2,1)S(1)} collective-permute-done((bf16[2,64,896]{2,1,0:T(8,128)(2,1)S(1)}, bf16[2,64,896]{2,1,0:T(8,128)(2,1)S(1)}, u32[]{:S(2)}, u32[]{:S(2)}) %collective-permute-start.1) | collective-permute-done | bytes 229408 | tf_op jit(solution)/shard_map/ppermute | solution.py:163
  43.6 29.5 %collective-permute-done.3.mine_ref = bf16[384,2048]{1,0:T(8,128)(2,1)S(1)} collective-permute-done((bf16[384,2048]{1,0:T(8,128)(2,1)S(1)}, bf16[384,2048]{1,0:T(8,128)(2,1)S(1)}, u32[]{:S(2)}, u32[]{:S(2)}) %collective-permute-start.3) | collective-permute-done | bytes 1572896 | tf_op jit(solution)/shard_map/ppermute | solution.py:163
  75.7 9.9 %all-gather.3.cloned.1.call-done.w_ref = bf16[2048,896]{1,0:T(8,128)(2,1)} async-done(((bf16[512,896]{1,0:T(8,128)(2,1)}), bf16[2048,896]{1,0:T(8,128)(2,1)}) %all-gather.3.cloned.1.call-update) | async-done | bytes 3670032 | tf_op jit(solution)/shard_map/all_gather | solution.py:1264
  125.4 23.3 %collective-permute-done.8.mine_ref = bf16[384,2048]{1,0:T(8,128)(2,1)S(1)} collective-permute-done((bf16[384,2048]{1,0:T(8,128)(2,1)}, bf16[384,2048]{1,0:T(8,128)(2,1)S(1)}, u32[]{:S(2)}, u32[]{:S(2)}) %collective-permute-start.8) | collective-permute-done | bytes 1572896 | tf_op jit(solution)/shard_map/ppermute | solution.py:163
  165.1 11.7 %exchange_small.2 = (s32[8,8,128]{2,1,0:T(8,128)}, f32[8,2,384]{2,1,0:T(2,128)}) custom-call(s32[8,128]{1,0:T(8,128)} %pad_bitcast_fusion.refs_0_, f32[8,2,384]{2,1,0:T(2,128)} %copy-done.30), custom_call_target="tpu_custom_call" | custom-call | tf_op jit(solution)/shard_map/exchange_small/pallas_call | solution.py:140
  192.9 27.4 %attention_forward.1 = (bf16[3072,256]{1,0:T(8,128)(2,1)S(1)}, f32[2,6,1,512]{3,2,1,0:T(1,128)S(1)}) custom-call(s32[6]{0:T(128)S(1)} %and_select_fusion.1.low_ref, s32[6,1,512]{2,1,0:T(1,128)S(1)} %bitcast.165, bf16[3072,256]{1,0:T(8,128)(2,1)S(1)} %copy-done.16, bf16[3072,256]{1,0:T(8,128)(2,1)S(1)} %copy-done.18, bf16[3072,256]{1,0:T(8,128)(2,1)} %copy-done.3), custom_call_target="tpu_custom_call" | custom-call | flops 35000000 | bytes 65536 | tf_op jit(solution)/shard_map/attention_forward/pallas_call | solution.py:288
  222.4 23.7 %collective-permute-done.11.refs_0_ = bf16[384,2048]{1,0:T(8,128)(2,1)} collective-permute-done((bf16[384,2048]{1,0:T(8,128)(2,1)}, bf16[384,2048]{1,0:T(8,128)(2,1)}, u32[]{:S(2)}, u32[]{:S(2)}) %collective-permute-start.11) | collective-permute-done | bytes 1572896 | tf_op jit(solution)/shard_map/ppermute | solution.py:163
  246.8 34.6 %collective-permute-done.12.mine_ref.refs_2_ = bf16[3072,256]{1,0:T(8,128)(2,1)} collective-permute-done((bf16[3072,256]{1,0:T(8,128)(2,1)S(1)}, bf16[3072,256]{1,0:T(8,128)(2,1)}, u32[]{:S(2)}, u32[]{:S(2)}) %collective-permute-start.12) | collective-permute-done | bytes 1572896 | tf_op jit(solution)/shard_map/ppermute | solution.py:163
  291.1 14.0 %gather_heads.3.base_ref = f32[1536,2048]{1,0:T(8,128)} custom-call(s32[2]{0:T(128)S(1)} %pad_add_fusion.2.at_ref, bf16[3072,2048]{1,0:T(8,128)(2,1)} %get-tuple-element.366.base_ref, bf16[8,192,384]{2,1,0:T(8,128)(2,1)S(1)} %fusion.12.pick_ref, bf16[3072,256]{1,0:T(8,128)(2,1)S(1)} %get-tuple-element.446.mine_ref.refs_0_.o_ref, ...), custom_call_target="tpu_custom_call" | custom-call | flops 8000000 | bytes 65536 | tf_op jit(solution)/shard_map/gather_heads/pallas_call | solution.py:444
  305.1 12.4 %collective-permute-done.14.mine_ref.refs_4_ = bf16[3072,256]{1,0:T(8,128)(2,1)} collective-permute-done((bf16[3072,256]{1,0:T(8,128)(2,1)}, bf16[3072,256]{1,0:T(8,128)(2,1)}, u32[]{:S(2)}, u32[]{:S(2)}) %collective-permute-start.14) | collective-permute-done | bytes 1572896 | tf_op jit(solution)/shard_map/ppermute | solution.py:163
  323.7 12.6 %gather_heads.4.base_ref = f32[1536,2048]{1,0:T(8,128)} custom-call(s32[2]{0:T(128)S(1)} %pad_add_fusion.at_ref, f32[1536,2048]{1,0:T(8,128)} %gather_heads.3.base_ref, bf16[8,192,384]{2,1,0:T(8,128)(2,1)S(1)} %fusion.12.pick_ref, bf16[3072,256]{1,0:T(8,128)(2,1)} %collective-permute-done.12.mine_ref.refs_2_, ...), custom_call_target="tpu_custom_call", output_to_operand_aliasing={{}: (1, {})} | custom-call | flops 8000000 | bytes 65536 | tf_op jit(solution)/shard_map/gather_heads/pallas_call | solution.py:444
  336.3 12.4 %gather_heads.5.base_ref = f32[1536,2048]{1,0:T(8,128)} custom-call(s32[2]{0:T(128)S(1)} %pad_add_fusion.3.at_ref, f32[1536,2048]{1,0:T(8,128)} %gather_heads.4.base_ref, bf16[8,192,384]{2,1,0:T(8,128)(2,1)S(1)} %fusion.12.pick_ref, bf16[3072,256]{1,0:T(8,128)(2,1)} %collective-permute-done.14.mine_ref.refs_4_, ...), custom_call_target="tpu_custom_call", output_to_operand_aliasing={{}: (1, {})} | custom-call | flops 8000000 | bytes 65536 | tf_op jit(solution)/shard_map/gather_heads/pallas_call | solution.py:444
  368.6 45.9 %expert_forward.1 = (bf16[1536,2048]{1,0:T(8,128)(2,1)}, f32[1536,128]{1,0:T(8,128)}, f32[1536,1024]{1,0:T(8,128)}, f32[1536,1024]{1,0:T(8,128)}, bf16[1536,1024...) custom-call(s32[10]{0:T(128)} %stack.116.order_ref, ...), custom_call_target="tpu_custom_call" | custom-call | flops 45000000 | bytes 65536 | tf_op jit(solution)/shard_map/expert_forward/pallas_call | solution.py:559
  414.5 18.0 %expert_backward.2 = (bf16[1,384,2176]{2,1,0:T(8,128)(2,1)}, bf16[1,384,2176]{2,1,0:T(8,128)(2,1)}, bf16[1536,2048]{1,0:T(8,128)(2,1)}, bf16[1536,1024]{1,0:T(8,128)(2,1)}, bf16[1536,1024]{1,0:T(8,128)(2,1)}) custom-call(s32[3]{0:T(128)} %pad_add_fusion.4.at_ref, bf16[8,192,384]{2,1,0:T(8,128)(2,1)} %copy-done.2, bf16[8,384,192]{2,1,0:T(8,128)(2,1)} %fusion.11.turned_ref, ...), custom_call_target="tpu_custom_call" | custom-call | flops 12000000 | bytes 65536 | tf_op jit(solution)/shard_map/expert_backward/pallas_call | solution.py:700
  446.2 36.3 %expert_backward.3 = (bf16[3,384,2176]{2,1,0:T(8,128)(2,1)}, bf16[3,384,2176]{2,1,0:T(8,128)(2,1)}, bf16[1536,2048]{1,0:T(8,128)(2,1)}, bf16[1536,1024]{1,0:T(8,128)(2,1)}, bf16[1536,1024]{1,0:T(8,128)(2,1)}) custom-call(s32[5]{0:T(128)} %stack.117.at_ref, ...), custom_call_target="tpu_custom_call", output_to_operand_aliasing={{2}: (16, {}), {3}: (17, {}), {4}: (18, {})} | custom-call | flops 36000000 | bytes 65536 | tf_op jit(solution)/shard_map/expert_backward/pallas_call | solution.py:700
  506.8 10.0 %weight_grad.7 = bf16[2048,1024]{1,0:T(8,128)(2,1)} custom-call(bf16[1536,2048]{1,0:T(8,128)(2,1)} %get-tuple-element.431.a_ref, bf16[1536,1024]{1,0:T(8,128)(2,1)S(1)} %copy-done.11), custom_call_target="tpu_custom_call" | custom-call | flops 10000000 | bytes 65536 | tf_op jit(solution)/shard_map/weight_grad/pallas_call | solution.py:1073
  516.8 9.9 %weight_grad.6 = bf16[2048,1024]{1,0:T(8,128)(2,1)} custom-call(bf16[1536,2048]{1,0:T(8,128)(2,1)} %get-tuple-element.431.a_ref, bf16[1536,1024]{1,0:T(8,128)(2,1)S(1)} %copy-done.10), custom_call_target="tpu_custom_call" | custom-call | flops 10000000 | bytes 65536 | tf_op jit(solution)/shard_map/weight_grad/pallas_call | solution.py:1073
  526.7 11.1 %weight_grad.5 = bf16[1024,2048]{1,0:T(8,128)(2,1)} custom-call(bf16[1536,1024]{1,0:T(8,128)(2,1)S(1)} %copy-done.23, bf16[1536,2048]{1,0:T(8,128)(2,1)} %get-tuple-element.430.b_ref), custom_call_target="tpu_custom_call" | custom-call | flops 10000000 | bytes 65536 | tf_op jit(solution)/shard_map/weight_grad/pallas_call | solution.py:1073
  546.8 10.7 %own_forward.1 = (bf16[384,2048]{1,0:T(8,128)(2,1)S(1)}, f32[384,2048]{1,0:T(8,128)}, bf16[384,2048]{1,0:T(8,128)(2,1)S(1)}, f32[384,128]{1,0:T(8,128)S(1)}, f32[384,128]{1,0:T(8,128)S(1)}) custom-call(s32[9]{0:T(128)S(1)} %stack.126.at_ref, bf16[3072,256]{1,0:T(8,128)(2,1)S(1)} %get-tuple-element.446.mine_ref.refs_0_.o_ref, bf16[3072,256]{1,0:T(8,128)(2,1)} %copy-done.13, ...), custom_call_target="tpu_custom_call" | custom-call | flops 10000000 | bytes 65536 | tf_op jit(solution)/shard_map/own_forward/pallas_call | solution.py:1153
  565.5 15.0 %collective-permute-done.31.arrived_ref = bf16[384,2176]{1,0:T(8,128)(2,1)} collective-permute-done((bf16[384,2176]{1,0:T(8,128)(2,1)}, bf16[384,2176]{1,0:T(8,128)(2,1)}, u32[]{:S(2)}, u32[]{:S(2)}) %collective-permute-start.31) | collective-permute-done | bytes 1671200 | tf_op jit(solution)/shard_map/ppermute | solution.py:163
  582.5 14.7 %owner_backward.1 = (bf16[384,128]{1,0:T(8,128)(2,1)S(1)}, f32[8,2048]{1,0:T(8,128)S(1)}, f32[384,2048]{1,0:T(8,128)}, bf16[384,2048]{1,0:T(8,128)(2,1)S(1)}, bf16[8,384,256]{2,1,0:T(8,128)(2,1)S(1)}) custom-call(bf16[384,2176]{1,0:T(8,128)(2,1)} %collective-permute-done.31.arrived_ref, bf16[3,384,2176]{2,1,0:T(8,128)(2,1)} %get-tuple-element.435.refs_1_.mine_ref, ...), custom_call_target="tpu_custom_call" | custom-call | flops 14000000 | bytes 65536 | tf_op jit(solution)/shard_map/owner_backward/pallas_call | solution.py:824
  614.6 10.2 %collective-permute-done.33 = bf16[2,384,256]{2,1,0:T(8,128)(2,1)} collective-permute-done((bf16[2,384,256]{2,1,0:T(8,128)(2,1)}, bf16[2,384,256]{2,1,0:T(8,128)(2,1)}, u32[]{:S(2)}, u32[]{:S(2)}) %collective-permute-start.33) | collective-permute-done | bytes 393248 | tf_op jit(solution)/shard_map/ppermute | solution.py:163
  624.8 23.8 %collective-permute-done.34 = bf16[2,384,256]{2,1,0:T(8,128)(2,1)} collective-permute-done((bf16[2,384,256]{2,1,0:T(8,128)(2,1)}, bf16[2,384,256]{2,1,0:T(8,128)(2,1)}, u32[]{:S(2)}, u32[]{:S(2)}) %collective-permute-start.34) | collective-permute-done | bytes 393248 | tf_op jit(solution)/shard_map/ppermute | solution.py:163
  665.9 41.4 %attention_backward.1 = (f32[3072,256]{1,0:T(8,128)}, f32[3072,256]{1,0:T(8,128)}, bf16[3072,256]{1,0:T(8,128)(2,1)S(1)}, f32[2,6,1,512]{3,2,1,0:T(1,128)S(1)}, f32[2,6,1,512]{3,2,1,0:T(1,128)S(1)}) custom-call(s32[6]{0:T(128)S(1)} %and_select_fusion.high_ref, s32[6,1,512]{2,1,0:T(1,128)S(1)} %bitcast.166, bf16[3072,256]{1,0:T(8,128)(2,1)S(1)} %copy-done.17, ...), custom_call_target="tpu_custom_call" | custom-call | flops 46000000 | bytes 65536 | tf_op jit(solution)/shard_map/attention_backward/pallas_call | solution.py:392
  712.9 12.8 %exchange_small.3.m_ref = f32[8,2,384]{2,1,0:T(2,128)} custom-call(f32[8,2,384]{2,1,0:T(2,128)} %pad_maximum_fusion.6.refs_0_), custom_call_target="tpu_custom_call" | custom-call | tf_op jit(solution)/shard_map/exchange_small/pallas_call | solution.py:140
  746.2 15.6 %project_back.3 = (bf16[3072,768]{1,0:T(8,128)(2,1)}, bf16[3,384,2048]{2,1,0:T(8,128)(2,1)}, bf16[3,384,2048]{2,1,0:T(8,128)(2,1)}, f32[8,256]{1,0:T(8,128)S(1)}) custom-call(s32[4]{0:T(128)S(1)} %pad_add_fusion.5.at_ref, f32[3072,512]{1,0:T(8,128)} %get-tuple-element.342.p_ref, f32[8,2,384]{2,1,0:T(2,128)S(1)} %copy-done.33, ...), custom_call_target="tpu_custom_call", output_to_operand_aliasing={{0}: (11, {})} | custom-call | flops 24000000 | bytes 65536 | tf_op jit(solution)/shard_map/project_back/pallas_call | solution.py:1006
  762.0 14.7 %in_weight_grad.1 = bf16[2048,896]{1,0:T(8,128)(2,1)S(1)} custom-call(bf16[3072,2048]{1,0:T(8,128)(2,1)} %get-tuple-element.512.a_ref, bf16[3072,768]{1,0:T(8,128)(2,1)} %get-tuple-element.513.b_ref, bf16[384,2048]{1,0:T(8,128)(2,1)S(1)} %copy-done.29, bf16[384,128]{1,0:T(8,128)(2,1)S(1)} %get-tuple-element.515.l_ref, f32[8,2048]{1,0:T(8,128)S(1)} %maximum_maximum_fusion.r_ref), custom_call_target="tpu_custom_call" | custom-call | flops 14000000 | bytes 65536 | tf_op jit(solution)/shard_map/in_weight_grad/pallas_call | solution.py:1106
  778.6 27.5 %collective-permute-done.44 = bf16[384,2048]{1,0:T(8,128)(2,1)} collective-permute-done((bf16[384,2048]{1,0:T(8,128)(2,1)}, bf16[384,2048]{1,0:T(8,128)(2,1)}, u32[]{:S(2)}, u32[]{:S(2)}) %collective-permute-start.44) | collective-permute-done | bytes 1572896 | tf_op jit(solution)/shard_map/ppermute | solution.py:163
  841.5 19.8 %collective-permute-done.47 = bf16[384,2048]{1,0:T(8,128)(2,1)S(1)} collective-permute-done((bf16[384,2048]{1,0:T(8,128)(2,1)S(1)}, bf16[384,2048]{1,0:T(8,128)(2,1)S(1)}, u32[]{:S(2)}, u32[]{:S(2)}) %collective-permute-start.47) | collective-permute-done | bytes 1572896 | tf_op jit(solution)/shard_map/ppermute | solution.py:163
  880.9 21.7 %collective-permute-done.53 = bf16[384,2048]{1,0:T(8,128)(2,1)} collective-permute-done((bf16[384,2048]{1,0:T(8,128)(2,1)}, bf16[384,2048]{1,0:T(8,128)(2,1)}, u32[]{:S(2)}, u32[]{:S(2)}) %collective-permute-start.53) | collective-permute-done | bytes 1572896 | tf_op jit(solution)/shard_map/ppermute | solution.py:163
  902.7 13.9 %reduce-scatter.5.cloned.1.call-done = bf16[512,896]{1,0:T(8,128)(2,1)} async-done(((bf16[2048,896]{1,0:T(8,128)(2,1)}), bf16[512,896]{1,0:T(8,128)(2,1)}) %reduce-scatter.5.cloned.1.call-update) | async-done | bytes 917520 | tf_op jit(solution)/shard_map/reduce_scatter | solution.py:1528
  940.8 10.8 %collective-permute-done.55 = bf16[2,64,896]{2,1,0:T(8,128)(2,1)S(1)} collective-permute-done((bf16[2,64,896]{2,1,0:T(8,128)(2,1)S(1)}, bf16[2,64,896]{2,1,0:T(8,128)(2,1)S(1)}, u32[]{:S(2)}, u32[]{:S(2)}) %collective-permute-start.55) | collective-permute-done | bytes 229408 | tf_op jit(solution)/shard_map/ppermute | solution.py:163
  (407 shorter events, 342.6 us)
Async XLA Ops:
  7.2 78.5 %all-gather.3.cloned.1.call-start = ((), (), s32[]{:S(2)}) async-start(), calls=%async_computation.2 | async-start | bytes 4587520 | tf_op jit(solution)/shard_map/all_gather | solution.py:1264
  32.8 253.5 %all-gather.5.cloned.1.call-start = ((), (), s32[]{:S(2)}) async-start(), calls=%async_computation.3 | async-start | bytes 8650752 | tf_op jit(solution)/shard_map/all_gather | solution.py:1293
  33.6 39.5 %collective-permute-start.3 = (bf16[384,2048]{1,0:T(8,128)(2,1)S(1)}, bf16[384,2048]{1,0:T(8,128)(2,1)S(1)}, u32[]{:S(2)}, u32[]{:S(2)}) collective-permute-start(bf16[384,2048]{1,0:T(8,128)(2,1)S(1)} %copy-done.4), channel_id=1, source_target_pairs={{0,2},{1,3},{2,4},{3,5},{4,6},{5,7},{6,0},{7,1},{8,10},{9,11},{10,... | collective-permute-start | bytes 4718600 | tf_op jit(solution)/shard_map/ppermute | solution.py:163
  34.5 38.6 %collective-permute-start.4 = (bf16[384,2048]{1,0:T(8,128)(2,1)S(1)}, bf16[384,2048]{1,0:T(8,128)(2,1)S(1)}, u32[]{:S(2)}, u32[]{:S(2)}) collective-permute-start(bf16[384,2048]{1,0:T(8,128)(2,1)S(1)} %copy-done.4), channel_id=1, source_target_pairs={{0,1},{1,0},{2,3},{3,2},{4,5},{5,4},{6,7},{7,6},{8,9},{9,8},{10,11... | collective-permute-start | bytes 4718600 | tf_op jit(solution)/shard_map/ppermute | solution.py:158
  148.7 657.3 %all-reduce.6.cloned.1.call-start = ((), (), s32[]{:S(2)}) async-start(), calls=%async_computation.6 | async-start | bytes 25165824 | tf_op jit(solution)/shard_map/psum | solution.py:1413
  176.8 69.2 %collective-permute-start.11 = (bf16[384,2048]{1,0:T(8,128)(2,1)}, bf16[384,2048]{1,0:T(8,128)(2,1)}, u32[]{:S(2)}, u32[]{:S(2)}) collective-permute-start(bf16[384,2048]{1,0:T(8,128)(2,1)} %cot_ref.1), channel_id=1, source_target_pairs={{0,2},{1,3},{2,4},{3,5},{4,6},{5,7},{6,0},{7,1},{8,10},{9,11},{10,... | collective-permute-start | bytes 4718600 | tf_op jit(solution)/shard_map/ppermute | solution.py:163
  319.8 38.1 %collective-permute-start.16 = (bf16[3072,256]{1,0:T(8,128)(2,1)}, bf16[3072,256]{1,0:T(8,128)(2,1)}, u32[]{:S(2)}, u32[]{:S(2)}) collective-permute-start(bf16[3072,256]{1,0:T(8,128)(2,1)} %collective-permute-done.14.mine_ref.refs_4_), channel_id=1, source_target_pairs={{0,2},{1,3},{2,4},{3,5},{4,6},{5,7},{6,0},{7,1},{8,10},{9,11},{10,... | collective-permute-start | bytes 4718600 | tf_op jit(solution)/shard_map/ppermute | solution.py:163
  358.6 55.9 %collective-permute-start.21 = (bf16[384,2048]{1,0:T(8,128)(2,1)}, bf16[384,2048]{1,0:T(8,128)(2,1)}, u32[]{:S(2)}, u32[]{:S(2)}) collective-permute-start(bf16[384,2048]{1,0:T(8,128)(2,1)} %collective-permute-done.11.refs_0_), channel_id=1, source_target_pairs={{0,1},{1,0},{2,3},{3,2},{4,5},{5,4},{6,7},{7,6},{8,9},{9,8},{10,11... | collective-permute-start | bytes 4718600 | tf_op jit(solution)/shard_map/ppermute | solution.py:158
  358.6 73.9 %collective-permute-start.18 = (bf16[384,2048]{1,0:T(8,128)(2,1)}, bf16[384,2048]{1,0:T(8,128)(2,1)}, u32[]{:S(2)}, u32[]{:S(2)}) collective-permute-start(bf16[384,2048]{1,0:T(8,128)(2,1)} %collective-permute-done.11.refs_0_), channel_id=1, source_target_pairs={{0,2},{1,3},{2,4},{3,5},{4,6},{5,7},{6,0},{7,1},{8,10},{9,11},{10,... | collective-permute-start | bytes 4718600 | tf_op jit(solution)/shard_map/ppermute | solution.py:163
  362.6 69.9 %collective-permute-start.19 = (bf16[384,2048]{1,0:T(8,128)(2,1)}, bf16[384,2048]{1,0:T(8,128)(2,1)}, u32[]{:S(2)}, u32[]{:S(2)}) collective-permute-start(bf16[384,2048]{1,0:T(8,128)(2,1)} %cot_ref.1), channel_id=1, source_target_pairs={{0,6},{1,7},{2,0},{3,1},{4,2},{5,3},{6,4},{7,5},{8,14},{9,15},{10,... | collective-permute-start | bytes 4718600 | tf_op jit(solution)/shard_map/ppermute | solution.py:163
  362.8 69.8 %collective-permute-start.20 = (bf16[384,2048]{1,0:T(8,128)(2,1)}, bf16[384,2048]{1,0:T(8,128)(2,1)}, u32[]{:S(2)}, u32[]{:S(2)}) collective-permute-start(bf16[384,2048]{1,0:T(8,128)(2,1)} %cot_ref.1), channel_id=1, source_target_pairs={{0,1},{1,0},{2,3},{3,2},{4,5},{5,4},{6,7},{7,6},{8,9},{9,8},{10,11... | collective-permute-start | bytes 4718600 | tf_op jit(solution)/shard_map/ppermute | solution.py:158
  442.2 40.3 %collective-permute-start.26 = (bf16[384,2176]{1,0:T(8,128)(2,1)}, bf16[384,2176]{1,0:T(8,128)(2,1)S(1)}, u32[]{:S(2)}, u32[]{:S(2)}) collective-permute-start(bf16[384,2176]{1,0:T(8,128)(2,1)} %add_rows.10), channel_id=1, source_target_pairs={{0,2},{1,3},{2,4},{3,5},{4,6},{5,7},{6,0},{7,1},{8,10},{9,11},{10,... | collective-permute-start | bytes 5013512 | tf_op jit(solution)/shard_map/ppermute | solution.py:163
  496.1 41.8 %collective-permute-start.29 = (bf16[384,2176]{1,0:T(8,128)(2,1)}, bf16[384,2176]{1,0:T(8,128)(2,1)}, u32[]{:S(2)}, u32[]{:S(2)}) collective-permute-start(bf16[384,2176]{1,0:T(8,128)(2,1)} %get-tuple-element.621), channel_id=1, source_target_pairs={{0,1},{1,0},{2,3},{3,2},{4,5},{5,4},{6,7},{7,6},{8,9},{9,8},{10,11... | collective-permute-start | bytes 5013512 | tf_op jit(solution)/shard_map/ppermute | solution.py:158
  496.5 41.4 %collective-permute-start.30 = (bf16[384,2176]{1,0:T(8,128)(2,1)}, bf16[384,2176]{1,0:T(8,128)(2,1)S(1)}, u32[]{:S(2)}, u32[]{:S(2)}) collective-permute-start(bf16[384,2176]{1,0:T(8,128)(2,1)} %get-tuple-element.620), channel_id=1, source_target_pairs={{0,1},{1,0},{2,3},{3,2},{4,5},{5,4},{6,7},{7,6},{8,9},{9,8},{10,11... | collective-permute-start | bytes 5013512 | tf_op jit(solution)/shard_map/ppermute | solution.py:158
  496.6 41.3 %collective-permute-start.28 = (bf16[384,2176]{1,0:T(8,128)(2,1)}, bf16[384,2176]{1,0:T(8,128)(2,1)}, u32[]{:S(2)}, u32[]{:S(2)}) collective-permute-start(bf16[384,2176]{1,0:T(8,128)(2,1)} %add_rows.11), channel_id=1, source_target_pairs={{0,2},{1,3},{2,4},{3,5},{4,6},{5,7},{6,0},{7,1},{8,10},{9,11},{10,... | collective-permute-start | bytes 5013512 | tf_op jit(solution)/shard_map/ppermute | solution.py:163
  506.2 37.6 %collective-permute-start.32 = (bf16[384,2048]{1,0:T(8,128)(2,1)}, bf16[384,2048]{1,0:T(8,128)(2,1)}, u32[]{:S(2)}, u32[]{:S(2)}) collective-permute-start(bf16[384,2048]{1,0:T(8,128)(2,1)} %get-tuple-element.619), channel_id=1, source_target_pairs={{0,1},{1,0},{2,3},{3,2},{4,5},{5,4},{6,7},{7,6},{8,9},{9,8},{10,11... | collective-permute-start | bytes 4718600 | tf_op jit(solution)/shard_map/ppermute | solution.py:158
  542.1 38.4 %collective-permute-start.31 = (bf16[384,2176]{1,0:T(8,128)(2,1)}, bf16[384,2176]{1,0:T(8,128)(2,1)}, u32[]{:S(2)}, u32[]{:S(2)}) collective-permute-start(bf16[384,2176]{1,0:T(8,128)(2,1)} %add_rows.12), channel_id=1, source_target_pairs={{0,2},{1,3},{2,4},{3,5},{4,6},{5,7},{6,0},{7,1},{8,10},{9,11},{10,... | collective-permute-start | bytes 5013512 | tf_op jit(solution)/shard_map/ppermute | solution.py:163
  543.6 326.6 %reduce-scatter.3.cloned.1.call-start = ((), (), s32[]{:S(2)}) async-start(), calls=%async_computation.4 | async-start | bytes 5242880 | tf_op jit(solution)/shard_map/reduce_scatter | solution.py:1519
  580.5 68.1 %collective-permute-start.36 = (bf16[384,2048]{1,0:T(8,128)(2,1)}, bf16[384,2048]{1,0:T(8,128)(2,1)}, u32[]{:S(2)}, u32[]{:S(2)}) collective-permute-start(bf16[384,2048]{1,0:T(8,128)(2,1)} %add_rows.13), channel_id=1, source_target_pairs={{0,2},{1,3},{2,4},{3,5},{4,6},{5,7},{6,0},{7,1},{8,10},{9,11},{10,... | collective-permute-start | bytes 4718600 | tf_op jit(solution)/shard_map/ppermute | solution.py:163
  598.8 49.8 %collective-permute-start.34 = (bf16[2,384,256]{2,1,0:T(8,128)(2,1)}, bf16[2,384,256]{2,1,0:T(8,128)(2,1)}, u32[]{:S(2)}, u32[]{:S(2)}) collective-permute-start(bf16[2,384,256]{2,1,0:T(8,128)(2,1)} %get-tuple-element.470), channel_id=1, source_target_pairs={{0,4},{1,5},{2,6},{3,7},{4,0},{5,1},{6,2},{7,3},{8,12},{9,13},{10,... | collective-permute-start | bytes 1179656 | tf_op jit(solution)/shard_map/ppermute | solution.py:163
  599.5 49.2 %collective-permute-start.35 = (bf16[2,384,256]{2,1,0:T(8,128)(2,1)}, bf16[2,384,256]{2,1,0:T(8,128)(2,1)}, u32[]{:S(2)}, u32[]{:S(2)}) collective-permute-start(bf16[2,384,256]{2,1,0:T(8,128)(2,1)} %get-tuple-element.471), channel_id=1, source_target_pairs={{0,6},{1,7},{2,0},{3,1},{4,2},{5,3},{6,4},{7,5},{8,14},{9,15},{10,... | collective-permute-start | bytes 1179656 | tf_op jit(solution)/shard_map/ppermute | solution.py:163
  600.3 54.1 %collective-permute-start.37 = (bf16[384,2048]{1,0:T(8,128)(2,1)}, bf16[384,2048]{1,0:T(8,128)(2,1)}, u32[]{:S(2)}, u32[]{:S(2)}) collective-permute-start(bf16[384,2048]{1,0:T(8,128)(2,1)} %get-tuple-element.618), channel_id=1, source_target_pairs={{0,1},{1,0},{2,3},{3,2},{4,5},{5,4},{6,7},{7,6},{8,9},{9,8},{10,11... | collective-permute-start | bytes 4718600 | tf_op jit(solution)/shard_map/ppermute | solution.py:158
  664.7 43.8 %collective-permute-start.42 = (bf16[1024,2048]{1,0:T(8,128)(2,1)}, bf16[1024,2048]{1,0:T(8,128)(2,1)}, u32[]{:S(2)}, u32[]{:S(2)}) collective-permute-start(bf16[1024,2048]{1,0:T(8,128)(2,1)} %weight_grad.9), channel_id=1, source_target_pairs={{0,1},{1,0},{2,3},{3,2},{4,5},{5,4},{6,7},{7,6},{8,9},{9,8},{10,11... | collective-permute-start | bytes 12582920 | tf_op jit(solution)/shard_map/ppermute | solution.py:158
  664.8 43.7 %collective-permute-start.40 = (bf16[384,2048]{1,0:T(8,128)(2,1)}, bf16[384,2048]{1,0:T(8,128)(2,1)}, u32[]{:S(2)}, u32[]{:S(2)}) collective-permute-start(bf16[384,2048]{1,0:T(8,128)(2,1)} %get-tuple-element.617), channel_id=1, source_target_pairs={{0,1},{1,0},{2,3},{3,2},{4,5},{5,4},{6,7},{7,6},{8,9},{9,8},{10,11... | collective-permute-start | bytes 4718600 | tf_op jit(solution)/shard_map/ppermute | solution.py:158
  665.3 43.2 %collective-permute-start.41 = (bf16[384,2048]{1,0:T(8,128)(2,1)}, bf16[384,2048]{1,0:T(8,128)(2,1)}, u32[]{:S(2)}, u32[]{:S(2)}) collective-permute-start(bf16[384,2048]{1,0:T(8,128)(2,1)} %get-tuple-element.616), channel_id=1, source_target_pairs={{0,1},{1,0},{2,3},{3,2},{4,5},{5,4},{6,7},{7,6},{8,9},{9,8},{10,11... | collective-permute-start | bytes 4718600 | tf_op jit(solution)/shard_map/ppermute | solution.py:158
  665.4 43.2 %collective-permute-start.39 = (bf16[384,2048]{1,0:T(8,128)(2,1)}, bf16[384,2048]{1,0:T(8,128)(2,1)}, u32[]{:S(2)}, u32[]{:S(2)}) collective-permute-start(bf16[384,2048]{1,0:T(8,128)(2,1)} %add_rows.14), channel_id=1, source_target_pairs={{0,2},{1,3},{2,4},{3,5},{4,6},{5,7},{6,0},{7,1},{8,10},{9,11},{10,... | collective-permute-start | bytes 4718600 | tf_op jit(solution)/shard_map/ppermute | solution.py:163
  736.1 42.5 %collective-permute-start.45 = (bf16[384,2048]{1,0:T(8,128)(2,1)}, bf16[384,2048]{1,0:T(8,128)(2,1)}, u32[]{:S(2)}, u32[]{:S(2)}) collective-permute-start(bf16[384,2048]{1,0:T(8,128)(2,1)} %add_rows.15), channel_id=1, source_target_pairs={{0,2},{1,3},{2,4},{3,5},{4,6},{5,7},{6,0},{7,1},{8,10},{9,11},{10,... | collective-permute-start | bytes 4718600 | tf_op jit(solution)/shard_map/ppermute | solution.py:163
  743.6 62.5 %collective-permute-start.44 = (bf16[384,2048]{1,0:T(8,128)(2,1)}, bf16[384,2048]{1,0:T(8,128)(2,1)}, u32[]{:S(2)}, u32[]{:S(2)}) collective-permute-start(bf16[384,2048]{1,0:T(8,128)(2,1)} %add_rows.16), channel_id=1, source_target_pairs={{0,2},{1,3},{2,4},{3,5},{4,6},{5,7},{6,0},{7,1},{8,10},{9,11},{10,... | collective-permute-start | bytes 4718600 | tf_op jit(solution)/shard_map/ppermute | solution.py:163
  811.4 105.2 %reduce-scatter.5.cloned.1.call-start = ((), (), s32[]{:S(2)}) async-start(), calls=%async_computation.5 | async-start | bytes 4587520 | tf_op jit(solution)/shard_map/reduce_scatter | solution.py:1528
  872.3 44.3 %collective-permute-start.50 = (bf16[64,2048]{1,0:T(8,128)(2,1)}, bf16[64,2048]{1,0:T(8,128)(2,1)}, u32[]{:S(2)}, u32[]{:S(2)}) collective-permute-start(bf16[64,2048]{1,0:T(8,128)(2,1)} %get-tuple-element.632), channel_id=1, source_target_pairs={{0,2},{1,3},{2,4},{3,5},{4,6},{5,7},{6,0},{7,1},{8,10},{9,11},{10,... | collective-permute-start | bytes 786440 | tf_op jit(solution)/shard_map/ppermute | solution.py:163
  872.3 51.1 %collective-permute-start.51 = (bf16[64,2048]{1,0:T(8,128)(2,1)}, bf16[64,2048]{1,0:T(8,128)(2,1)}, u32[]{:S(2)}, u32[]{:S(2)}) collective-permute-start(bf16[64,2048]{1,0:T(8,128)(2,1)} %get-tuple-element.631), channel_id=1, source_target_pairs={{0,4},{1,5},{2,6},{3,7},{4,0},{5,1},{6,2},{7,3},{8,12},{9,13},{10,... | collective-permute-start | bytes 786440 | tf_op jit(solution)/shard_map/ppermute | solution.py:163
  872.3 51.1 %collective-permute-start.52 = (bf16[64,2048]{1,0:T(8,128)(2,1)}, bf16[64,2048]{1,0:T(8,128)(2,1)}, u32[]{:S(2)}, u32[]{:S(2)}) collective-permute-start(bf16[64,2048]{1,0:T(8,128)(2,1)} %get-tuple-element.630), channel_id=1, source_target_pairs={{0,6},{1,7},{2,0},{3,1},{4,2},{5,3},{6,4},{7,5},{8,14},{9,15},{10,... | collective-permute-start | bytes 786440 | tf_op jit(solution)/shard_map/ppermute | solution.py:163
  (97 other events, 1057.4 us)
Sparse Core Ops, SparseCore 0:
  32.9 52.6 all-gather.2
  148.9 97.4 all-gather.4
  543.7 242.7 all-reduce.5
  811.5 53.5 reduce-scatter.2
  868.2 48.2 reduce-scatter.4

commit v5 on v4

--- a/solution.py
+++ b/solution.py
@@ -12,6 +12,7 @@
 TOP = 2
 EPS = 1e-05
 NEG = -1e30
+LOG2E = 1.4426950408889634
 MESH = pl.DeviceIdType.MESH
 BF = jnp.bfloat16
 F32 = jnp.float32
@@ -261,10 +262,10 @@
                     (((1,), (1,)), ((), ())),
                     preferred_element_type=F32,
                 )
-                s = jnp.where(allowed, s * scale, NEG)
+                s = jnp.where(allowed, s * (scale * LOG2E), NEG)
                 new_top = jnp.maximum(top, jnp.max(s, axis=0, keepdims=True))
-                p = jnp.exp(s - new_top)
-                shrink = jnp.exp(top - new_top)
+                p = jnp.exp2(s - new_top)
+                shrink = jnp.exp2(top - new_top)
                 total = total * shrink + jnp.sum(p, axis=0, keepdims=True)
                 acc = acc * shrink + lax.dot_general(
                     v_ref[at, lanes],
@@ -283,7 +284,7 @@
         done = lax.fori_loop(low_ref[i], i + 1, step, (begin,) * heads)
         for h, (top, total, acc) in enumerate(done):
             o_ref[:, h * HEAD_DIM : (h + 1) * HEAD_DIM] = (acc / total).T.astype(BF)
-            lse_ref[h, 0] = top + jnp.log(total)
+            lse_ref[h, 0] = top + jnp.log(total) * LOG2E
 
     return pl.pallas_call(
         kernel,
@@ -359,15 +360,14 @@
                 lanes = slice(h * HEAD_DIM, (h + 1) * HEAD_DIM)
                 q, do = q_ref[at, lanes], do_ref[at, lanes]
                 k, v = k_ref[:, lanes], v_ref[:, lanes]
-                s = lax.dot_general(k, q, contract, preferred_element_type=F32) * scale
-                p = jnp.exp(jnp.where(allowed, s, NEG) - lse_ref[h, i])
+                s = lax.dot_general(k, q, contract, preferred_element_type=F32) * (scale * LOG2E)
+                p = jnp.exp2(jnp.where(allowed, s, NEG) - lse_ref[h, i])
                 dv = dv + jnp.dot(p.astype(BF), do, preferred_element_type=F32)
                 dp = lax.dot_general(v, do, contract, preferred_element_type=F32)
                 ds = (p * (dp - delta_ref[h, i])).astype(BF)
                 dk = dk + jnp.dot(ds, q, preferred_element_type=F32)
-                dq_ref[at, lanes] += (
-                    lax.dot_general(ds, k, (((0,), (0,)), ((), ())), preferred_element_type=F32)
-                    * scale
+                dq_ref[at, lanes] += lax.dot_general(
+                    ds, k, (((0,), (0,)), ((), ())), preferred_element_type=F32
                 )
                 after.append((dk, dv))
             return tuple(after)
@@ -381,7 +381,9 @@
             dv_ref[:, lanes] = dv.astype(BF)
             k_sum_ref[h, 0] = row_sums(k_ref[:, lanes].astype(F32) * dk)
             at = pl.ds(pl.multiple_of(j * block, block), block)
-            q_sum_ref[h, 0] = row_sums(q_ref[at, lanes].astype(F32) * dq_ref[at, lanes])
+            dq = dq_ref[at, lanes] * scale
+            dq_ref[at, lanes] = dq
+            q_sum_ref[h, 0] = row_sums(q_ref[at, lanes].astype(F32) * dq)
 
     whole = pl.BlockSpec((rows, columns), lambda j, high: (0, 0))
     part = pl.BlockSpec((block, columns), lambda j, high: (j, 0))

time: 975 us -> 975 us (level)
  no operation moved by 1% of the time
where the time goes in v5:
time: 975 us; the launch traced here: 968 us
  Pallas kernels  418 us (43%)
  waiting for transfers between devices  330 us (34%)
  local copies, waits for them, and re-layouts  80.8 us (8%)
  starting transfers between devices  68.2 us (7%)
  other arithmetic  55.3 us (6%)
  between operations  15.1 us (2%)
    ppermute x30, waiting for transfers between devices, chip_shift(): lax.ppermute(block, 'expert', [(i, (i + 2 * step) % ranks) for i in range...  290 us
    pallas_call x2, Pallas kernels, expert_backward(): pl.pallas_call(kernel, out_shape=(jax.ShapeDtypeStruct((count, rows, wide...  54.3 us
    ppermute x30, starting transfers between devices, chip_shift(): lax.ppermute(block, 'expert', [(i, (i + 2 * step) % ranks) for i in range...  47.2 us
    pallas_call x1, Pallas kernels, expert_forward(): pl.pallas_call(kernel, out_shape=(jax.ShapeDtypeStruct((all_slots, width)...  45.9 us
    pallas_call x1, Pallas kernels, attention_backward(): pl.pallas_call(kernel, out_shape=(shape, shape, jax.ShapeDtypeStruct((row...  41.5 us
    pallas_call x5, Pallas kernels, weight_grad(): pl.pallas_call(kernel, out_shape=jax.ShapeDtypeStruct((m, n), BF), grid=(...  39 us
    pallas_call x3, Pallas kernels, gather_heads(): pl.pallas_call(kernel, out_shape=jax.ShapeDtypeStruct((ranks * capacity,...  39 us
    pallas_call x4, Pallas kernels, project_in(): pl.pallas_call(kernel, out_shape=shapes, grid_spec=pltpu.PrefetchScalarGr...  38.5 us
  transfers between devices with their start and end apart: 63, of which 24 were waited for; matrix products, arithmetic and copies ran while one was open for 9% of the time, Pallas kernels for 42%

profile of v5, /device:TPU:25, one launch (start us, length us, event | category | flops | bytes accessed | tf_op | source)
XLA Modules:
  0.0 968.1 jit_solution(13417538001749027602)
XLA Ops:
  13.5 14.8 %collective-permute-done.1 = bf16[2,64,896]{2,1,0:T(8,128)(2,1)S(1)} collective-permute-done((bf16[2,64,896]{2,1,0:T(8,128)(2,1)S(1)}, bf16[2,64,896]{2,1,0:T(8,128)(2,1)S(1)}, u32[]{:S(2)}, u32[]{:S(2)}) %collective-permute-start.1) | collective-permute-done | bytes 229408 | tf_op jit(solution)/shard_map/ppermute | solution.py:164
  43.6 29.5 %collective-permute-done.3.mine_ref = bf16[384,2048]{1,0:T(8,128)(2,1)S(1)} collective-permute-done((bf16[384,2048]{1,0:T(8,128)(2,1)S(1)}, bf16[384,2048]{1,0:T(8,128)(2,1)S(1)}, u32[]{:S(2)}, u32[]{:S(2)}) %collective-permute-start.3) | collective-permute-done | bytes 1572896 | tf_op jit(solution)/shard_map/ppermute | solution.py:164
  75.7 9.9 %all-gather.3.cloned.1.call-done.w_ref = bf16[2048,896]{1,0:T(8,128)(2,1)} async-done(((bf16[512,896]{1,0:T(8,128)(2,1)}), bf16[2048,896]{1,0:T(8,128)(2,1)}) %all-gather.3.cloned.1.call-update) | async-done | bytes 3670032 | tf_op jit(solution)/shard_map/all_gather | solution.py:1266
  125.4 23.3 %collective-permute-done.8.mine_ref = bf16[384,2048]{1,0:T(8,128)(2,1)S(1)} collective-permute-done((bf16[384,2048]{1,0:T(8,128)(2,1)}, bf16[384,2048]{1,0:T(8,128)(2,1)S(1)}, u32[]{:S(2)}, u32[]{:S(2)}) %collective-permute-start.8) | collective-permute-done | bytes 1572896 | tf_op jit(solution)/shard_map/ppermute | solution.py:164
  165.1 11.7 %exchange_small.2 = (s32[8,8,128]{2,1,0:T(8,128)}, f32[8,2,384]{2,1,0:T(2,128)}) custom-call(s32[8,128]{1,0:T(8,128)} %pad_bitcast_fusion.refs_0_, f32[8,2,384]{2,1,0:T(2,128)} %copy-done.30), custom_call_target="tpu_custom_call" | custom-call | tf_op jit(solution)/shard_map/exchange_small/pallas_call | solution.py:141
  192.9 25.3 %attention_forward.1 = (bf16[3072,256]{1,0:T(8,128)(2,1)S(1)}, f32[2,6,1,512]{3,2,1,0:T(1,128)S(1)}) custom-call(s32[6]{0:T(128)S(1)} %and_select_fusion.1.low_ref, s32[6,1,512]{2,1,0:T(1,128)S(1)} %bitcast.165, bf16[3072,256]{1,0:T(8,128)(2,1)S(1)} %copy-done.16, bf16[3072,256]{1,0:T(8,128)(2,1)S(1)} %copy-done.18, bf16[3072,256]{1,0:T(8,128)(2,1)} %copy-done.3), custom_call_target="tpu_custom_call" | custom-call | flops 35000000 | bytes 65536 | tf_op jit(solution)/shard_map/attention_forward/pallas_call | solution.py:289
  220.4 25.7 %collective-permute-done.11.refs_0_ = bf16[384,2048]{1,0:T(8,128)(2,1)} collective-permute-done((bf16[384,2048]{1,0:T(8,128)(2,1)}, bf16[384,2048]{1,0:T(8,128)(2,1)}, u32[]{:S(2)}, u32[]{:S(2)}) %collective-permute-start.11) | collective-permute-done | bytes 1572896 | tf_op jit(solution)/shard_map/ppermute | solution.py:164
  246.8 34.6 %collective-permute-done.12.mine_ref.refs_2_ = bf16[3072,256]{1,0:T(8,128)(2,1)} collective-permute-done((bf16[3072,256]{1,0:T(8,128)(2,1)S(1)}, bf16[3072,256]{1,0:T(8,128)(2,1)}, u32[]{:S(2)}, u32[]{:S(2)}) %collective-permute-start.12) | collective-permute-done | bytes 1572896 | tf_op jit(solution)/shard_map/ppermute | solution.py:164
  291.1 14.0 %gather_heads.3.base_ref = f32[1536,2048]{1,0:T(8,128)} custom-call(s32[2]{0:T(128)S(1)} %pad_add_fusion.2.at_ref, bf16[3072,2048]{1,0:T(8,128)(2,1)} %get-tuple-element.366.base_ref, bf16[8,192,384]{2,1,0:T(8,128)(2,1)S(1)} %fusion.12.pick_ref, bf16[3072,256]{1,0:T(8,128)(2,1)S(1)} %get-tuple-element.446.mine_ref.refs_0_.o_ref, ...), custom_call_target="tpu_custom_call" | custom-call | flops 8000000 | bytes 65536 | tf_op jit(solution)/shard_map/gather_heads/pallas_call | solution.py:446
  305.1 12.4 %collective-permute-done.14.mine_ref.refs_4_ = bf16[3072,256]{1,0:T(8,128)(2,1)} collective-permute-done((bf16[3072,256]{1,0:T(8,128)(2,1)}, bf16[3072,256]{1,0:T(8,128)(2,1)}, u32[]{:S(2)}, u32[]{:S(2)}) %collective-permute-start.14) | collective-permute-done | bytes 1572896 | tf_op jit(solution)/shard_map/ppermute | solution.py:164
  323.7 12.6 %gather_heads.4.base_ref = f32[1536,2048]{1,0:T(8,128)} custom-call(s32[2]{0:T(128)S(1)} %pad_add_fusion.at_ref, f32[1536,2048]{1,0:T(8,128)} %gather_heads.3.base_ref, bf16[8,192,384]{2,1,0:T(8,128)(2,1)S(1)} %fusion.12.pick_ref, bf16[3072,256]{1,0:T(8,128)(2,1)} %collective-permute-done.12.mine_ref.refs_2_, ...), custom_call_target="tpu_custom_call", output_to_operand_aliasing={{}: (1, {})} | custom-call | flops 8000000 | bytes 65536 | tf_op jit(solution)/shard_map/gather_heads/pallas_call | solution.py:446
  336.3 12.4 %gather_heads.5.base_ref = f32[1536,2048]{1,0:T(8,128)} custom-call(s32[2]{0:T(128)S(1)} %pad_add_fusion.3.at_ref, f32[1536,2048]{1,0:T(8,128)} %gather_heads.4.base_ref, bf16[8,192,384]{2,1,0:T(8,128)(2,1)S(1)} %fusion.12.pick_ref, bf16[3072,256]{1,0:T(8,128)(2,1)} %collective-permute-done.14.mine_ref.refs_4_, ...), custom_call_target="tpu_custom_call", output_to_operand_aliasing={{}: (1, {})} | custom-call | flops 8000000 | bytes 65536 | tf_op jit(solution)/shard_map/gather_heads/pallas_call | solution.py:446
  368.6 45.9 %expert_forward.1 = (bf16[1536,2048]{1,0:T(8,128)(2,1)}, f32[1536,128]{1,0:T(8,128)}, f32[1536,1024]{1,0:T(8,128)}, f32[1536,1024]{1,0:T(8,128)}, bf16[1536,1024...) custom-call(s32[10]{0:T(128)} %stack.116.order_ref, ...), custom_call_target="tpu_custom_call" | custom-call | flops 45000000 | bytes 65536 | tf_op jit(solution)/shard_map/expert_forward/pallas_call | solution.py:561
  414.5 18.0 %expert_backward.2 = (bf16[1,384,2176]{2,1,0:T(8,128)(2,1)}, bf16[1,384,2176]{2,1,0:T(8,128)(2,1)}, bf16[1536,2048]{1,0:T(8,128)(2,1)}, bf16[1536,1024]{1,0:T(8,128)(2,1)}, bf16[1536,1024]{1,0:T(8,128)(2,1)}) custom-call(s32[3]{0:T(128)} %pad_add_fusion.4.at_ref, bf16[8,192,384]{2,1,0:T(8,128)(2,1)} %copy-done.2, bf16[8,384,192]{2,1,0:T(8,128)(2,1)} %fusion.11.turned_ref, ...), custom_call_target="tpu_custom_call" | custom-call | flops 12000000 | bytes 65536 | tf_op jit(solution)/shard_map/expert_backward/pallas_call | solution.py:702
  446.2 36.3 %expert_backward.3 = (bf16[3,384,2176]{2,1,0:T(8,128)(2,1)}, bf16[3,384,2176]{2,1,0:T(8,128)(2,1)}, bf16[1536,2048]{1,0:T(8,128)(2,1)}, bf16[1536,1024]{1,0:T(8,128)(2,1)}, bf16[1536,1024]{1,0:T(8,128)(2,1)}) custom-call(s32[5]{0:T(128)} %stack.117.at_ref, ...), custom_call_target="tpu_custom_call", output_to_operand_aliasing={{2}: (16, {}), {3}: (17, {}), {4}: (18, {})} | custom-call | flops 36000000 | bytes 65536 | tf_op jit(solution)/shard_map/expert_backward/pallas_call | solution.py:702
  506.8 10.0 %weight_grad.7 = bf16[2048,1024]{1,0:T(8,128)(2,1)} custom-call(bf16[1536,2048]{1,0:T(8,128)(2,1)} %get-tuple-element.431.a_ref, bf16[1536,1024]{1,0:T(8,128)(2,1)S(1)} %copy-done.11), custom_call_target="tpu_custom_call" | custom-call | flops 10000000 | bytes 65536 | tf_op jit(solution)/shard_map/weight_grad/pallas_call | solution.py:1075
  516.8 9.9 %weight_grad.6 = bf16[2048,1024]{1,0:T(8,128)(2,1)} custom-call(bf16[1536,2048]{1,0:T(8,128)(2,1)} %get-tuple-element.431.a_ref, bf16[1536,1024]{1,0:T(8,128)(2,1)S(1)} %copy-done.10), custom_call_target="tpu_custom_call" | custom-call | flops 10000000 | bytes 65536 | tf_op jit(solution)/shard_map/weight_grad/pallas_call | solution.py:1075
  526.7 11.1 %weight_grad.5 = bf16[1024,2048]{1,0:T(8,128)(2,1)} custom-call(bf16[1536,1024]{1,0:T(8,128)(2,1)S(1)} %copy-done.23, bf16[1536,2048]{1,0:T(8,128)(2,1)} %get-tuple-element.430.b_ref), custom_call_target="tpu_custom_call" | custom-call | flops 10000000 | bytes 65536 | tf_op jit(solution)/shard_map/weight_grad/pallas_call | solution.py:1075
  546.8 10.7 %own_forward.1 = (bf16[384,2048]{1,0:T(8,128)(2,1)S(1)}, f32[384,2048]{1,0:T(8,128)}, bf16[384,2048]{1,0:T(8,128)(2,1)S(1)}, f32[384,128]{1,0:T(8,128)S(1)}, f32[384,128]{1,0:T(8,128)S(1)}) custom-call(s32[9]{0:T(128)S(1)} %stack.126.at_ref, bf16[3072,256]{1,0:T(8,128)(2,1)S(1)} %get-tuple-element.446.mine_ref.refs_0_.o_ref, bf16[3072,256]{1,0:T(8,128)(2,1)} %copy-done.13, ...), custom_call_target="tpu_custom_call" | custom-call | flops 10000000 | bytes 65536 | tf_op jit(solution)/shard_map/own_forward/pallas_call | solution.py:1155
  565.5 15.0 %collective-permute-done.31.arrived_ref = bf16[384,2176]{1,0:T(8,128)(2,1)} collective-permute-done((bf16[384,2176]{1,0:T(8,128)(2,1)}, bf16[384,2176]{1,0:T(8,128)(2,1)}, u32[]{:S(2)}, u32[]{:S(2)}) %collective-permute-start.31) | collective-permute-done | bytes 1671200 | tf_op jit(solution)/shard_map/ppermute | solution.py:164
  582.5 14.7 %owner_backward.1 = (bf16[384,128]{1,0:T(8,128)(2,1)S(1)}, f32[8,2048]{1,0:T(8,128)S(1)}, f32[384,2048]{1,0:T(8,128)}, bf16[384,2048]{1,0:T(8,128)(2,1)S(1)}, bf16[8,384,256]{2,1,0:T(8,128)(2,1)S(1)}) custom-call(bf16[384,2176]{1,0:T(8,128)(2,1)} %collective-permute-done.31.arrived_ref, bf16[3,384,2176]{2,1,0:T(8,128)(2,1)} %get-tuple-element.435.refs_1_.mine_ref, ...), custom_call_target="tpu_custom_call" | custom-call | flops 14000000 | bytes 65536 | tf_op jit(solution)/shard_map/owner_backward/pallas_call | solution.py:826
  614.6 10.2 %collective-permute-done.33 = bf16[2,384,256]{2,1,0:T(8,128)(2,1)} collective-permute-done((bf16[2,384,256]{2,1,0:T(8,128)(2,1)}, bf16[2,384,256]{2,1,0:T(8,128)(2,1)}, u32[]{:S(2)}, u32[]{:S(2)}) %collective-permute-start.33) | collective-permute-done | bytes 393248 | tf_op jit(solution)/shard_map/ppermute | solution.py:164
  624.8 23.8 %collective-permute-done.34 = bf16[2,384,256]{2,1,0:T(8,128)(2,1)} collective-permute-done((bf16[2,384,256]{2,1,0:T(8,128)(2,1)}, bf16[2,384,256]{2,1,0:T(8,128)(2,1)}, u32[]{:S(2)}, u32[]{:S(2)}) %collective-permute-start.34) | collective-permute-done | bytes 393248 | tf_op jit(solution)/shard_map/ppermute | solution.py:164
  665.9 41.5 %attention_backward.1 = (f32[3072,256]{1,0:T(8,128)}, f32[3072,256]{1,0:T(8,128)}, bf16[3072,256]{1,0:T(8,128)(2,1)S(1)}, f32[2,6,1,512]{3,2,1,0:T(1,128)S(1)}, f32[2,6,1,512]{3,2,1,0:T(1,128)S(1)}) custom-call(s32[6]{0:T(128)S(1)} %and_select_fusion.high_ref, s32[6,1,512]{2,1,0:T(1,128)S(1)} %bitcast.166, bf16[3072,256]{1,0:T(8,128)(2,1)S(1)} %copy-done.17, ...), custom_call_target="tpu_custom_call" | custom-call | flops 46000000 | bytes 65536 | tf_op jit(solution)/shard_map/attention_backward/pallas_call | solution.py:394
  713.1 12.9 %exchange_small.3.m_ref = f32[8,2,384]{2,1,0:T(2,128)} custom-call(f32[8,2,384]{2,1,0:T(2,128)} %pad_maximum_fusion.6.refs_0_), custom_call_target="tpu_custom_call" | custom-call | tf_op jit(solution)/shard_map/exchange_small/pallas_call | solution.py:141
  746.5 15.6 %project_back.3 = (bf16[3072,768]{1,0:T(8,128)(2,1)}, bf16[3,384,2048]{2,1,0:T(8,128)(2,1)}, bf16[3,384,2048]{2,1,0:T(8,128)(2,1)}, f32[8,256]{1,0:T(8,128)S(1)}) custom-call(s32[4]{0:T(128)S(1)} %pad_add_fusion.5.at_ref, f32[3072,512]{1,0:T(8,128)} %get-tuple-element.342.p_ref, f32[8,2,384]{2,1,0:T(2,128)S(1)} %copy-done.33, ...), custom_call_target="tpu_custom_call", output_to_operand_aliasing={{0}: (11, {})} | custom-call | flops 24000000 | bytes 65536 | tf_op jit(solution)/shard_map/project_back/pallas_call | solution.py:1008
  762.2 14.7 %in_weight_grad.1 = bf16[2048,896]{1,0:T(8,128)(2,1)S(1)} custom-call(bf16[3072,2048]{1,0:T(8,128)(2,1)} %get-tuple-element.512.a_ref, bf16[3072,768]{1,0:T(8,128)(2,1)} %get-tuple-element.513.b_ref, bf16[384,2048]{1,0:T(8,128)(2,1)S(1)} %copy-done.29, bf16[384,128]{1,0:T(8,128)(2,1)S(1)} %get-tuple-element.515.l_ref, f32[8,2048]{1,0:T(8,128)S(1)} %maximum_maximum_fusion.r_ref), custom_call_target="tpu_custom_call" | custom-call | flops 14000000 | bytes 65536 | tf_op jit(solution)/shard_map/in_weight_grad/pallas_call | solution.py:1108
  778.8 27.6 %collective-permute-done.44 = bf16[384,2048]{1,0:T(8,128)(2,1)} collective-permute-done((bf16[384,2048]{1,0:T(8,128)(2,1)}, bf16[384,2048]{1,0:T(8,128)(2,1)}, u32[]{:S(2)}, u32[]{:S(2)}) %collective-permute-start.44) | collective-permute-done | bytes 1572896 | tf_op jit(solution)/shard_map/ppermute | solution.py:164
  841.7 19.8 %collective-permute-done.47 = bf16[384,2048]{1,0:T(8,128)(2,1)S(1)} collective-permute-done((bf16[384,2048]{1,0:T(8,128)(2,1)S(1)}, bf16[384,2048]{1,0:T(8,128)(2,1)S(1)}, u32[]{:S(2)}, u32[]{:S(2)}) %collective-permute-start.47) | collective-permute-done | bytes 1572896 | tf_op jit(solution)/shard_map/ppermute | solution.py:164
  881.1 21.7 %collective-permute-done.53 = bf16[384,2048]{1,0:T(8,128)(2,1)} collective-permute-done((bf16[384,2048]{1,0:T(8,128)(2,1)}, bf16[384,2048]{1,0:T(8,128)(2,1)}, u32[]{:S(2)}, u32[]{:S(2)}) %collective-permute-start.53) | collective-permute-done | bytes 1572896 | tf_op jit(solution)/shard_map/ppermute | solution.py:164
  902.8 13.9 %reduce-scatter.5.cloned.1.call-done = bf16[512,896]{1,0:T(8,128)(2,1)} async-done(((bf16[2048,896]{1,0:T(8,128)(2,1)}), bf16[512,896]{1,0:T(8,128)(2,1)}) %reduce-scatter.5.cloned.1.call-update) | async-done | bytes 917520 | tf_op jit(solution)/shard_map/reduce_scatter | solution.py:1530
  941.0 10.8 %collective-permute-done.55 = bf16[2,64,896]{2,1,0:T(8,128)(2,1)S(1)} collective-permute-done((bf16[2,64,896]{2,1,0:T(8,128)(2,1)S(1)}, bf16[2,64,896]{2,1,0:T(8,128)(2,1)S(1)}, u32[]{:S(2)}, u32[]{:S(2)}) %collective-permute-start.55) | collective-permute-done | bytes 229408 | tf_op jit(solution)/shard_map/ppermute | solution.py:164
  (407 shorter events, 342.4 us)
Async XLA Ops:
  7.2 78.5 %all-gather.3.cloned.1.call-start = ((), (), s32[]{:S(2)}) async-start(), calls=%async_computation.2 | async-start | bytes 4587520 | tf_op jit(solution)/shard_map/all_gather | solution.py:1266
  32.8 253.5 %all-gather.5.cloned.1.call-start = ((), (), s32[]{:S(2)}) async-start(), calls=%async_computation.3 | async-start | bytes 8650752 | tf_op jit(solution)/shard_map/all_gather | solution.py:1295
  33.6 39.5 %collective-permute-start.3 = (bf16[384,2048]{1,0:T(8,128)(2,1)S(1)}, bf16[384,2048]{1,0:T(8,128)(2,1)S(1)}, u32[]{:S(2)}, u32[]{:S(2)}) collective-permute-start(bf16[384,2048]{1,0:T(8,128)(2,1)S(1)} %copy-done.4), channel_id=1, source_target_pairs={{0,2},{1,3},{2,4},{3,5},{4,6},{5,7},{6,0},{7,1},{8,10},{9,11},{10,... | collective-permute-start | bytes 4718600 | tf_op jit(solution)/shard_map/ppermute | solution.py:164
  34.5 38.6 %collective-permute-start.4 = (bf16[384,2048]{1,0:T(8,128)(2,1)S(1)}, bf16[384,2048]{1,0:T(8,128)(2,1)S(1)}, u32[]{:S(2)}, u32[]{:S(2)}) collective-permute-start(bf16[384,2048]{1,0:T(8,128)(2,1)S(1)} %copy-done.4), channel_id=1, source_target_pairs={{0,1},{1,0},{2,3},{3,2},{4,5},{5,4},{6,7},{7,6},{8,9},{9,8},{10,11... | collective-permute-start | bytes 4718600 | tf_op jit(solution)/shard_map/ppermute | solution.py:159
  148.7 657.7 %all-reduce.6.cloned.1.call-start = ((), (), s32[]{:S(2)}) async-start(), calls=%async_computation.6 | async-start | bytes 25165824 | tf_op jit(solution)/shard_map/psum | solution.py:1415
  176.8 69.2 %collective-permute-start.11 = (bf16[384,2048]{1,0:T(8,128)(2,1)}, bf16[384,2048]{1,0:T(8,128)(2,1)}, u32[]{:S(2)}, u32[]{:S(2)}) collective-permute-start(bf16[384,2048]{1,0:T(8,128)(2,1)} %cot_ref.1), channel_id=1, source_target_pairs={{0,2},{1,3},{2,4},{3,5},{4,6},{5,7},{6,0},{7,1},{8,10},{9,11},{10,... | collective-permute-start | bytes 4718600 | tf_op jit(solution)/shard_map/ppermute | solution.py:164
  319.8 38.1 %collective-permute-start.16 = (bf16[3072,256]{1,0:T(8,128)(2,1)}, bf16[3072,256]{1,0:T(8,128)(2,1)}, u32[]{:S(2)}, u32[]{:S(2)}) collective-permute-start(bf16[3072,256]{1,0:T(8,128)(2,1)} %collective-permute-done.14.mine_ref.refs_4_), channel_id=1, source_target_pairs={{0,2},{1,3},{2,4},{3,5},{4,6},{5,7},{6,0},{7,1},{8,10},{9,11},{10,... | collective-permute-start | bytes 4718600 | tf_op jit(solution)/shard_map/ppermute | solution.py:164
  358.6 55.9 %collective-permute-start.21 = (bf16[384,2048]{1,0:T(8,128)(2,1)}, bf16[384,2048]{1,0:T(8,128)(2,1)}, u32[]{:S(2)}, u32[]{:S(2)}) collective-permute-start(bf16[384,2048]{1,0:T(8,128)(2,1)} %collective-permute-done.11.refs_0_), channel_id=1, source_target_pairs={{0,1},{1,0},{2,3},{3,2},{4,5},{5,4},{6,7},{7,6},{8,9},{9,8},{10,11... | collective-permute-start | bytes 4718600 | tf_op jit(solution)/shard_map/ppermute | solution.py:159
  358.6 73.9 %collective-permute-start.18 = (bf16[384,2048]{1,0:T(8,128)(2,1)}, bf16[384,2048]{1,0:T(8,128)(2,1)}, u32[]{:S(2)}, u32[]{:S(2)}) collective-permute-start(bf16[384,2048]{1,0:T(8,128)(2,1)} %collective-permute-done.11.refs_0_), channel_id=1, source_target_pairs={{0,2},{1,3},{2,4},{3,5},{4,6},{5,7},{6,0},{7,1},{8,10},{9,11},{10,... | collective-permute-start | bytes 4718600 | tf_op jit(solution)/shard_map/ppermute | solution.py:164
  362.6 69.9 %collective-permute-start.19 = (bf16[384,2048]{1,0:T(8,128)(2,1)}, bf16[384,2048]{1,0:T(8,128)(2,1)}, u32[]{:S(2)}, u32[]{:S(2)}) collective-permute-start(bf16[384,2048]{1,0:T(8,128)(2,1)} %cot_ref.1), channel_id=1, source_target_pairs={{0,6},{1,7},{2,0},{3,1},{4,2},{5,3},{6,4},{7,5},{8,14},{9,15},{10,... | collective-permute-start | bytes 4718600 | tf_op jit(solution)/shard_map/ppermute | solution.py:164
  362.8 69.8 %collective-permute-start.20 = (bf16[384,2048]{1,0:T(8,128)(2,1)}, bf16[384,2048]{1,0:T(8,128)(2,1)}, u32[]{:S(2)}, u32[]{:S(2)}) collective-permute-start(bf16[384,2048]{1,0:T(8,128)(2,1)} %cot_ref.1), channel_id=1, source_target_pairs={{0,1},{1,0},{2,3},{3,2},{4,5},{5,4},{6,7},{7,6},{8,9},{9,8},{10,11... | collective-permute-start | bytes 4718600 | tf_op jit(solution)/shard_map/ppermute | solution.py:159
  442.2 40.3 %collective-permute-start.26 = (bf16[384,2176]{1,0:T(8,128)(2,1)}, bf16[384,2176]{1,0:T(8,128)(2,1)S(1)}, u32[]{:S(2)}, u32[]{:S(2)}) collective-permute-start(bf16[384,2176]{1,0:T(8,128)(2,1)} %add_rows.10), channel_id=1, source_target_pairs={{0,2},{1,3},{2,4},{3,5},{4,6},{5,7},{6,0},{7,1},{8,10},{9,11},{10,... | collective-permute-start | bytes 5013512 | tf_op jit(solution)/shard_map/ppermute | solution.py:164
  496.1 41.8 %collective-permute-start.29 = (bf16[384,2176]{1,0:T(8,128)(2,1)}, bf16[384,2176]{1,0:T(8,128)(2,1)}, u32[]{:S(2)}, u32[]{:S(2)}) collective-permute-start(bf16[384,2176]{1,0:T(8,128)(2,1)} %get-tuple-element.621), channel_id=1, source_target_pairs={{0,1},{1,0},{2,3},{3,2},{4,5},{5,4},{6,7},{7,6},{8,9},{9,8},{10,11... | collective-permute-start | bytes 5013512 | tf_op jit(solution)/shard_map/ppermute | solution.py:159
  496.5 41.4 %collective-permute-start.30 = (bf16[384,2176]{1,0:T(8,128)(2,1)}, bf16[384,2176]{1,0:T(8,128)(2,1)S(1)}, u32[]{:S(2)}, u32[]{:S(2)}) collective-permute-start(bf16[384,2176]{1,0:T(8,128)(2,1)} %get-tuple-element.620), channel_id=1, source_target_pairs={{0,1},{1,0},{2,3},{3,2},{4,5},{5,4},{6,7},{7,6},{8,9},{9,8},{10,11... | collective-permute-start | bytes 5013512 | tf_op jit(solution)/shard_map/ppermute | solution.py:159
  496.6 41.3 %collective-permute-start.28 = (bf16[384,2176]{1,0:T(8,128)(2,1)}, bf16[384,2176]{1,0:T(8,128)(2,1)}, u32[]{:S(2)}, u32[]{:S(2)}) collective-permute-start(bf16[384,2176]{1,0:T(8,128)(2,1)} %add_rows.11), channel_id=1, source_target_pairs={{0,2},{1,3},{2,4},{3,5},{4,6},{5,7},{6,0},{7,1},{8,10},{9,11},{10,... | collective-permute-start | bytes 5013512 | tf_op jit(solution)/shard_map/ppermute | solution.py:164
  506.2 37.6 %collective-permute-start.32 = (bf16[384,2048]{1,0:T(8,128)(2,1)}, bf16[384,2048]{1,0:T(8,128)(2,1)}, u32[]{:S(2)}, u32[]{:S(2)}) collective-permute-start(bf16[384,2048]{1,0:T(8,128)(2,1)} %get-tuple-element.619), channel_id=1, source_target_pairs={{0,1},{1,0},{2,3},{3,2},{4,5},{5,4},{6,7},{7,6},{8,9},{9,8},{10,11... | collective-permute-start | bytes 4718600 | tf_op jit(solution)/shard_map/ppermute | solution.py:159
  542.1 38.4 %collective-permute-start.31 = (bf16[384,2176]{1,0:T(8,128)(2,1)}, bf16[384,2176]{1,0:T(8,128)(2,1)}, u32[]{:S(2)}, u32[]{:S(2)}) collective-permute-start(bf16[384,2176]{1,0:T(8,128)(2,1)} %add_rows.12), channel_id=1, source_target_pairs={{0,2},{1,3},{2,4},{3,5},{4,6},{5,7},{6,0},{7,1},{8,10},{9,11},{10,... | collective-permute-start | bytes 5013512 | tf_op jit(solution)/shard_map/ppermute | solution.py:164
  543.6 326.8 %reduce-scatter.3.cloned.1.call-start = ((), (), s32[]{:S(2)}) async-start(), calls=%async_computation.4 | async-start | bytes 5242880 | tf_op jit(solution)/shard_map/reduce_scatter | solution.py:1521
  580.5 68.1 %collective-permute-start.36 = (bf16[384,2048]{1,0:T(8,128)(2,1)}, bf16[384,2048]{1,0:T(8,128)(2,1)}, u32[]{:S(2)}, u32[]{:S(2)}) collective-permute-start(bf16[384,2048]{1,0:T(8,128)(2,1)} %add_rows.13), channel_id=1, source_target_pairs={{0,2},{1,3},{2,4},{3,5},{4,6},{5,7},{6,0},{7,1},{8,10},{9,11},{10,... | collective-permute-start | bytes 4718600 | tf_op jit(solution)/shard_map/ppermute | solution.py:164
  598.8 49.8 %collective-permute-start.34 = (bf16[2,384,256]{2,1,0:T(8,128)(2,1)}, bf16[2,384,256]{2,1,0:T(8,128)(2,1)}, u32[]{:S(2)}, u32[]{:S(2)}) collective-permute-start(bf16[2,384,256]{2,1,0:T(8,128)(2,1)} %get-tuple-element.470), channel_id=1, source_target_pairs={{0,4},{1,5},{2,6},{3,7},{4,0},{5,1},{6,2},{7,3},{8,12},{9,13},{10,... | collective-permute-start | bytes 1179656 | tf_op jit(solution)/shard_map/ppermute | solution.py:164
  599.5 49.2 %collective-permute-start.35 = (bf16[2,384,256]{2,1,0:T(8,128)(2,1)}, bf16[2,384,256]{2,1,0:T(8,128)(2,1)}, u32[]{:S(2)}, u32[]{:S(2)}) collective-permute-start(bf16[2,384,256]{2,1,0:T(8,128)(2,1)} %get-tuple-element.471), channel_id=1, source_target_pairs={{0,6},{1,7},{2,0},{3,1},{4,2},{5,3},{6,4},{7,5},{8,14},{9,15},{10,... | collective-permute-start | bytes 1179656 | tf_op jit(solution)/shard_map/ppermute | solution.py:164
  600.3 54.1 %collective-permute-start.37 = (bf16[384,2048]{1,0:T(8,128)(2,1)}, bf16[384,2048]{1,0:T(8,128)(2,1)}, u32[]{:S(2)}, u32[]{:S(2)}) collective-permute-start(bf16[384,2048]{1,0:T(8,128)(2,1)} %get-tuple-element.618), channel_id=1, source_target_pairs={{0,1},{1,0},{2,3},{3,2},{4,5},{5,4},{6,7},{7,6},{8,9},{9,8},{10,11... | collective-permute-start | bytes 4718600 | tf_op jit(solution)/shard_map/ppermute | solution.py:159
  664.7 44.0 %collective-permute-start.42 = (bf16[1024,2048]{1,0:T(8,128)(2,1)}, bf16[1024,2048]{1,0:T(8,128)(2,1)}, u32[]{:S(2)}, u32[]{:S(2)}) collective-permute-start(bf16[1024,2048]{1,0:T(8,128)(2,1)} %weight_grad.9), channel_id=1, source_target_pairs={{0,1},{1,0},{2,3},{3,2},{4,5},{5,4},{6,7},{7,6},{8,9},{9,8},{10,11... | collective-permute-start | bytes 12582920 | tf_op jit(solution)/shard_map/ppermute | solution.py:159
  664.8 43.9 %collective-permute-start.40 = (bf16[384,2048]{1,0:T(8,128)(2,1)}, bf16[384,2048]{1,0:T(8,128)(2,1)}, u32[]{:S(2)}, u32[]{:S(2)}) collective-permute-start(bf16[384,2048]{1,0:T(8,128)(2,1)} %get-tuple-element.617), channel_id=1, source_target_pairs={{0,1},{1,0},{2,3},{3,2},{4,5},{5,4},{6,7},{7,6},{8,9},{9,8},{10,11... | collective-permute-start | bytes 4718600 | tf_op jit(solution)/shard_map/ppermute | solution.py:159
  665.3 43.4 %collective-permute-start.41 = (bf16[384,2048]{1,0:T(8,128)(2,1)}, bf16[384,2048]{1,0:T(8,128)(2,1)}, u32[]{:S(2)}, u32[]{:S(2)}) collective-permute-start(bf16[384,2048]{1,0:T(8,128)(2,1)} %get-tuple-element.616), channel_id=1, source_target_pairs={{0,1},{1,0},{2,3},{3,2},{4,5},{5,4},{6,7},{7,6},{8,9},{9,8},{10,11... | collective-permute-start | bytes 4718600 | tf_op jit(solution)/shard_map/ppermute | solution.py:159
  665.4 43.3 %collective-permute-start.39 = (bf16[384,2048]{1,0:T(8,128)(2,1)}, bf16[384,2048]{1,0:T(8,128)(2,1)}, u32[]{:S(2)}, u32[]{:S(2)}) collective-permute-start(bf16[384,2048]{1,0:T(8,128)(2,1)} %add_rows.14), channel_id=1, source_target_pairs={{0,2},{1,3},{2,4},{3,5},{4,6},{5,7},{6,0},{7,1},{8,10},{9,11},{10,... | collective-permute-start | bytes 4718600 | tf_op jit(solution)/shard_map/ppermute | solution.py:164
  736.3 42.5 %collective-permute-start.45 = (bf16[384,2048]{1,0:T(8,128)(2,1)}, bf16[384,2048]{1,0:T(8,128)(2,1)}, u32[]{:S(2)}, u32[]{:S(2)}) collective-permute-start(bf16[384,2048]{1,0:T(8,128)(2,1)} %add_rows.15), channel_id=1, source_target_pairs={{0,2},{1,3},{2,4},{3,5},{4,6},{5,7},{6,0},{7,1},{8,10},{9,11},{10,... | collective-permute-start | bytes 4718600 | tf_op jit(solution)/shard_map/ppermute | solution.py:164
  743.8 62.6 %collective-permute-start.44 = (bf16[384,2048]{1,0:T(8,128)(2,1)}, bf16[384,2048]{1,0:T(8,128)(2,1)}, u32[]{:S(2)}, u32[]{:S(2)}) collective-permute-start(bf16[384,2048]{1,0:T(8,128)(2,1)} %add_rows.16), channel_id=1, source_target_pairs={{0,2},{1,3},{2,4},{3,5},{4,6},{5,7},{6,0},{7,1},{8,10},{9,11},{10,... | collective-permute-start | bytes 4718600 | tf_op jit(solution)/shard_map/ppermute | solution.py:164
  811.7 105.1 %reduce-scatter.5.cloned.1.call-start = ((), (), s32[]{:S(2)}) async-start(), calls=%async_computation.5 | async-start | bytes 4587520 | tf_op jit(solution)/shard_map/reduce_scatter | solution.py:1530
  872.5 44.3 %collective-permute-start.50 = (bf16[64,2048]{1,0:T(8,128)(2,1)}, bf16[64,2048]{1,0:T(8,128)(2,1)}, u32[]{:S(2)}, u32[]{:S(2)}) collective-permute-start(bf16[64,2048]{1,0:T(8,128)(2,1)} %get-tuple-element.632), channel_id=1, source_target_pairs={{0,2},{1,3},{2,4},{3,5},{4,6},{5,7},{6,0},{7,1},{8,10},{9,11},{10,... | collective-permute-start | bytes 786440 | tf_op jit(solution)/shard_map/ppermute | solution.py:164
  872.5 51.2 %collective-permute-start.51 = (bf16[64,2048]{1,0:T(8,128)(2,1)}, bf16[64,2048]{1,0:T(8,128)(2,1)}, u32[]{:S(2)}, u32[]{:S(2)}) collective-permute-start(bf16[64,2048]{1,0:T(8,128)(2,1)} %get-tuple-element.631), channel_id=1, source_target_pairs={{0,4},{1,5},{2,6},{3,7},{4,0},{5,1},{6,2},{7,3},{8,12},{9,13},{10,... | collective-permute-start | bytes 786440 | tf_op jit(solution)/shard_map/ppermute | solution.py:164
  872.5 51.2 %collective-permute-start.52 = (bf16[64,2048]{1,0:T(8,128)(2,1)}, bf16[64,2048]{1,0:T(8,128)(2,1)}, u32[]{:S(2)}, u32[]{:S(2)}) collective-permute-start(bf16[64,2048]{1,0:T(8,128)(2,1)} %get-tuple-element.630), channel_id=1, source_target_pairs={{0,6},{1,7},{2,0},{3,1},{4,2},{5,3},{6,4},{7,5},{8,14},{9,15},{10,... | collective-permute-start | bytes 786440 | tf_op jit(solution)/shard_map/ppermute | solution.py:164
  (97 other events, 1059.4 us)
Sparse Core Ops, SparseCore 0:
  32.9 52.6 all-gather.2
  148.9 97.4 all-gather.4
  543.7 242.7 all-reduce.5
  811.8 53.4 reduce-scatter.2
  868.4 48.3 reduce-scatter.4
